TPU v7x, 32 devices: a whole 2x2x4 slice. The times are simulated.
32 devices in a mesh: fsdp: 8 (over y, x, core), tensor: 4 (over z).
Axes of the slice: x: 2, y: 2, z: 4, core: 2. Of those that a mesh axis runs over, the one named last changes fastest.
Arguments:
- tokens: bfloat16 [16, 448, 1024], P('fsdp'), may hold values from -6 to 6
- encoder: bfloat16 [16, 1500, 1024], P('fsdp'), may hold values from -6 to 6
- cotangent: bfloat16 [16, 448, 1024], P('fsdp'), may hold values from -8 to 8
- self_weights: bfloat16 [3, 1024, 1024], P(None, 'fsdp', 'tensor'), may hold values from -0.1875 to 0.1875
- self_biases: bfloat16 [2, 4, 256], P(None, 'tensor', 'fsdp'), may hold values from -0.3125 to 0.3125
- self_output: bfloat16 [1024, 1024], P('tensor', 'fsdp'), may hold values from -3 to 3
- cross_query: bfloat16 [1024, 1024], P('fsdp', 'tensor'), may hold values from -0.1875 to 0.1875
- cross_memory: bfloat16 [2, 1024, 1024], P(None, 'fsdp', 'tensor'), may hold values from -0.1875 to 0.1875
- cross_biases: bfloat16 [2, 4, 256], P(None, 'tensor', 'fsdp'), may hold values from -0.1875 to 0.1875
- cross_output: bfloat16 [1024, 1024], P('tensor', 'fsdp'), may hold values from -6 to 6
- hidden_weight: bfloat16 [1024, 4096], P('fsdp', 'tensor'), may hold values from -0.1875 to 0.1875
- hidden_bias: bfloat16 [4, 1024], P('tensor', 'fsdp'), may hold values from -3 to 3
- reduce_weight: bfloat16 [4096, 1024], P('tensor', 'fsdp'), may hold values from -0.09375 to 0.09375
- norm_gains: bfloat16 [3, 1024], P(None, 'fsdp'), may hold values from 0.5 to 1.5
- norm_shifts: bfloat16 [3, 1024], P(None, 'fsdp'), may hold values from -1.75 to 1.75
- branch_biases: bfloat16 [3, 1024], P(None, 'fsdp'), may hold values from -1.75 to 1.75
Outputs:
- layer_output: bfloat16 [16, 448, 1024], P('fsdp')
- tokens_gradient: bfloat16 [16, 448, 1024], P('fsdp')
- encoder_gradient: bfloat16 [16, 1500, 1024], P('fsdp', 'tensor')
- self_weights_gradient: float32 [3, 1024, 1024], P(None, 'fsdp', 'tensor')
- self_biases_gradient: float32 [2, 4, 256], P(None, 'tensor', 'fsdp')
- self_output_gradient: float32 [1024, 1024], P('tensor', 'fsdp')
- cross_query_gradient: float32 [1024, 1024], P('fsdp', 'tensor')
- cross_memory_gradient: float32 [2, 1024, 1024], P(None, 'fsdp', 'tensor')
- cross_biases_gradient: float32 [2, 4, 256], P(None, 'tensor', 'fsdp')
- cross_output_gradient: float32 [1024, 1024], P('tensor', 'fsdp')
- hidden_weight_gradient: float32 [1024, 4096], P('fsdp', 'tensor')
- hidden_bias_gradient: float32 [4, 1024], P('tensor', 'fsdp')
- reduce_weight_gradient: float32 [4096, 1024], P('tensor', 'fsdp')
- norm_gains_gradient: float32 [3, 1024], P(None, 'fsdp')
- norm_shifts_gradient: float32 [3, 1024], P(None, 'fsdp')
- branch_biases_gradient: float32 [3, 1024], P(None, 'fsdp')
All inputs are finite; a program needn't handle non-finite values.
Results may differ from a plain program's by a relative error of at most 0.035.
Values may be sent and summed in bfloat16 or wider, within the bound.
A program may use at most 128 MiB of HBM per device.

v0:
```python
import jax
import jax.numpy as jnp
from jax import lax
from jax.sharding import PartitionSpec as P

HEAD_DIM = 64


epsilon = 1e-05
masked_score = -1000000000.0


def layer_norm(values, gain, shift):
    centre = values - jnp.mean(values, axis=-1, keepdims=True)
    spread = jnp.mean(centre * centre, axis=-1, keepdims=True)
    return centre * lax.rsqrt(spread + epsilon) * gain + shift


def gelu_exact(values):
    return jax.nn.gelu(values, approximate=False)


def product(left, right):
    return jnp.dot(left, right, preferred_element_type=jnp.float32)


def left_product(left, right):
    return jnp.einsum("tc,td->cd", left, right, preferred_element_type=jnp.float32)


def right_product(left, right):
    return jnp.einsum("td,cd->tc", left, right, preferred_element_type=jnp.float32)


def split_heads(values):
    return values.reshape(values.shape[0], values.shape[1] // HEAD_DIM, HEAD_DIM)


def branch_total(partial_sum):
    return lax.psum(partial_sum.astype(jnp.bfloat16), "tensor").astype(jnp.float32)


def input_total(partial_sum):
    return lax.psum(partial_sum.astype(jnp.bfloat16), "tensor").astype(jnp.float32)


def score_block(queries, keys, causal):
    scale = HEAD_DIM ** (-0.5)
    scores = (
        jnp.einsum(
            "qhd,khd->hqk",
            split_heads(queries),
            split_heads(keys),
            preferred_element_type=jnp.float32,
        )
        * scale
    )
    if causal:
        rows = lax.broadcasted_iota(jnp.int32, scores.shape[1:], 0)
        columns = lax.broadcasted_iota(jnp.int32, scores.shape[1:], 1)
        scores = jnp.where(columns <= rows, scores, masked_score)
    return scores


def attend(queries, keys, values, causal):
    scores = score_block(queries, keys, causal)
    highest = jnp.max(scores, axis=-1, keepdims=True)
    raised = jnp.exp(scores - highest)
    total = jnp.sum(raised, axis=-1, keepdims=True)
    chance = (raised / total).astype(jnp.bfloat16)
    mixed = jnp.einsum(
        "hqk,khd->qhd", chance, split_heads(values), preferred_element_type=jnp.float32
    )
    return (mixed.reshape(queries.shape).astype(jnp.bfloat16), highest + jnp.log(total))


def attend_back(queries, keys, values, log_total, mixed_grad, causal):
    scale = HEAD_DIM ** (-0.5)
    chance = jnp.exp(score_block(queries, keys, causal) - log_total)
    upstream = split_heads(mixed_grad)
    chance_grad = jnp.einsum(
        "qhd,khd->hqk", upstream, split_heads(values), preferred_element_type=jnp.float32
    )
    score_grad = (
        chance * (chance_grad - jnp.sum(chance * chance_grad, axis=-1, keepdims=True))
    ).astype(jnp.bfloat16)
    query_grad = (
        jnp.einsum(
            "hqk,khd->qhd", score_grad, split_heads(keys), preferred_element_type=jnp.float32
        )
        * scale
    )
    key_grad = (
        jnp.einsum(
            "hqk,qhd->khd", score_grad, split_heads(queries), preferred_element_type=jnp.float32
        )
        * scale
    )
    value_grad = jnp.einsum(
        "hqk,qhd->khd", chance.astype(jnp.bfloat16), upstream, preferred_element_type=jnp.float32
    )
    return (
        query_grad.reshape(queries.shape),
        key_grad.reshape(keys.shape),
        value_grad.reshape(values.shape),
    )


def self_part(weights, start):
    normed_one = layer_norm(
        start, weights[10][0].astype(jnp.float32), weights[11][0].astype(jnp.float32)
    ).astype(jnp.bfloat16)
    queries = (product(normed_one, weights[0][0]) + weights[1][0, 0]).astype(jnp.bfloat16)
    keys = product(normed_one, weights[0][1]).astype(jnp.bfloat16)
    values = (product(normed_one, weights[0][2]) + weights[1][1, 0]).astype(jnp.bfloat16)
    mixed_one, log_one = attend(queries, keys, values, True)
    return (normed_one, queries, keys, values, mixed_one, log_one)


def cross_part(weights, middle, memory):
    normed_two = layer_norm(
        middle, weights[10][1].astype(jnp.float32), weights[11][1].astype(jnp.float32)
    ).astype(jnp.bfloat16)
    cross_queries = (product(normed_two, weights[3]) + weights[5][0, 0]).astype(jnp.bfloat16)
    cross_keys = product(memory, weights[4][0]).astype(jnp.bfloat16)
    cross_values = (product(memory, weights[4][1]) + weights[5][1, 0]).astype(jnp.bfloat16)
    mixed_two, log_two = attend(cross_queries, cross_keys, cross_values, False)
    return (normed_two, cross_queries, cross_keys, cross_values, mixed_two, log_two)


def feed_part(weights, later):
    normed_three = layer_norm(
        later, weights[10][2].astype(jnp.float32), weights[11][2].astype(jnp.float32)
    ).astype(jnp.bfloat16)
    expanded = product(normed_three, weights[7]) + weights[8][0]
    activated = gelu_exact(expanded).astype(jnp.bfloat16)
    return (normed_three, expanded, activated)


def run_forward(weights, tokens, memory):
    biases = weights[12].astype(jnp.float32)
    start = tokens.astype(jnp.float32)
    first = self_part(weights, start)
    middle = start + branch_total(product(first[4], weights[2])) + biases[0]
    second = cross_part(weights, middle, memory)
    later = middle + branch_total(product(second[4], weights[6])) + biases[1]
    third = feed_part(weights, later)
    output = later + branch_total(product(third[2], weights[9])) + biases[2]
    return (output, (start, middle, later, first, second, third))


def recompute(weights, start, middle, later, memory):
    return (
        start,
        middle,
        later,
        self_part(weights, start),
        cross_part(weights, middle, memory),
        feed_part(weights, later),
    )


def norm_back(values, index, weights, normed_grad):
    unused, pullback = jax.vjp(
        layer_norm,
        values,
        weights[10][index].astype(jnp.float32),
        weights[11][index].astype(jnp.float32),
    )
    return pullback(normed_grad)


def run_backward(weights, saved, memory, upstream):
    start, middle, later, first, second, third = saved
    normed_one, queries, keys, values, mixed_one, log_one = first
    normed_two, cross_queries, cross_keys, cross_values, mixed_two, log_two = second
    normed_three, expanded, activated = third
    upstream_low = upstream.astype(jnp.bfloat16)
    reduce_grad = left_product(activated, upstream_low)
    unused, gelu_pull = jax.vjp(gelu_exact, expanded)
    expanded_grad = gelu_pull(right_product(upstream_low, weights[9]))[0]
    expanded_low = expanded_grad.astype(jnp.bfloat16)
    hidden_grad = left_product(normed_three, expanded_low)
    normed_three_grad = input_total(right_product(expanded_low, weights[7]))
    later_part, gain_three, shift_three = norm_back(later, 2, weights, normed_three_grad)
    later_grad = upstream + later_part
    later_low = later_grad.astype(jnp.bfloat16)
    cross_out_grad = left_product(mixed_two, later_low)
    mixed_two_grad = right_product(later_low, weights[6]).astype(jnp.bfloat16)
    cross_query_grad, cross_key_grad, cross_value_grad = attend_back(
        cross_queries, cross_keys, cross_values, log_two, mixed_two_grad, False
    )
    cross_query_low = cross_query_grad.astype(jnp.bfloat16)
    cross_key_low = cross_key_grad.astype(jnp.bfloat16)
    cross_value_low = cross_value_grad.astype(jnp.bfloat16)
    memory_part = right_product(cross_key_low, weights[4][0]) + right_product(
        cross_value_low, weights[4][1]
    )
    memory_grad = lax.psum_scatter(
        memory_part.astype(jnp.bfloat16), "tensor", scatter_dimension=0, tiled=True
    ).astype(jnp.float32)
    normed_two_grad = input_total(right_product(cross_query_low, weights[3]))
    middle_part, gain_two, shift_two = norm_back(middle, 1, weights, normed_two_grad)
    middle_grad = later_grad + middle_part
    middle_low = middle_grad.astype(jnp.bfloat16)
    self_out_grad = left_product(mixed_one, middle_low)
    mixed_one_grad = right_product(middle_low, weights[2]).astype(jnp.bfloat16)
    query_grad, key_grad, value_grad = attend_back(
        queries, keys, values, log_one, mixed_one_grad, True
    )
    query_low = query_grad.astype(jnp.bfloat16)
    key_low = key_grad.astype(jnp.bfloat16)
    value_low = value_grad.astype(jnp.bfloat16)
    normed_one_grad = input_total(
        right_product(query_low, weights[0][0])
        + right_product(key_low, weights[0][1])
        + right_product(value_low, weights[0][2])
    )
    start_part, gain_one, shift_one = norm_back(start, 0, weights, normed_one_grad)
    start_grad = middle_grad + start_part
    grads = (
        jnp.stack(
            [
                left_product(normed_one, query_low),
                left_product(normed_one, key_low),
                left_product(normed_one, value_low),
            ]
        ),
        jnp.stack([jnp.sum(query_grad, axis=0), jnp.sum(value_grad, axis=0)])[:, None, :],
        self_out_grad,
        left_product(normed_two, cross_query_low),
        jnp.stack([left_product(memory, cross_key_low), left_product(memory, cross_value_low)]),
        jnp.stack([jnp.sum(cross_query_grad, axis=0), jnp.sum(cross_value_grad, axis=0)])[
            :, None, :
        ],
        cross_out_grad,
        hidden_grad,
        jnp.sum(expanded_grad, axis=0)[None, :],
        reduce_grad,
        jnp.stack([gain_one, gain_two, gain_three]),
        jnp.stack([shift_one, shift_two, shift_three]),
        jnp.stack(
            [jnp.sum(middle_grad, axis=0), jnp.sum(later_grad, axis=0), jnp.sum(upstream, axis=0)]
        ),
    )
    return (start_grad, memory_grad, grads)


def on_device(
    tokens,
    encoder,
    cotangent,
    self_weights,
    self_biases,
    self_output,
    cross_query,
    cross_memory,
    cross_biases,
    cross_output,
    hidden_weight,
    hidden_bias,
    reduce_weight,
    norm_gains,
    norm_shifts,
    branch_biases,
):
    shards = (
        self_weights,
        self_biases,
        self_output,
        cross_query,
        cross_memory,
        cross_biases,
        cross_output,
        hidden_weight,
        hidden_bias,
        reduce_weight,
        norm_gains,
        norm_shifts,
        branch_biases,
    )

    def fetch():
        return (
            lax.all_gather(self_weights, "fsdp", axis=1, tiled=True),
            lax.all_gather(self_biases, "fsdp", axis=2, tiled=True),
            lax.all_gather(self_output, "fsdp", axis=1, tiled=True),
            lax.all_gather(cross_query, "fsdp", axis=0, tiled=True),
            lax.all_gather(cross_memory, "fsdp", axis=1, tiled=True),
            lax.all_gather(cross_biases, "fsdp", axis=2, tiled=True),
            lax.all_gather(cross_output, "fsdp", axis=1, tiled=True),
            lax.all_gather(hidden_weight, "fsdp", axis=0, tiled=True),
            lax.all_gather(hidden_bias, "fsdp", axis=1, tiled=True),
            lax.all_gather(reduce_weight, "fsdp", axis=1, tiled=True),
            lax.all_gather(norm_gains, "fsdp", axis=1, tiled=True),
            lax.all_gather(norm_shifts, "fsdp", axis=1, tiled=True),
            lax.all_gather(branch_biases, "fsdp", axis=1, tiled=True),
        )

    start_totals = tuple((jnp.zeros(piece.shape, jnp.float32) for piece in shards))

    def step(totals, batch):
        tokens_now, memory_now, cotangent_now = batch
        output, saved = run_forward(fetch(), tokens_now, memory_now)
        weights_back = fetch()
        saved = recompute(weights_back, saved[0], saved[1], saved[2], memory_now)
        start_grad, memory_grad, grads = run_backward(
            weights_back, saved, memory_now, cotangent_now.astype(jnp.float32)
        )
        shares = (
            lax.psum_scatter(grads[0], "fsdp", scatter_dimension=1, tiled=True),
            lax.psum_scatter(grads[1], "fsdp", scatter_dimension=2, tiled=True),
            lax.psum_scatter(grads[2], "fsdp", scatter_dimension=1, tiled=True),
            lax.psum_scatter(grads[3], "fsdp", scatter_dimension=0, tiled=True),
            lax.psum_scatter(grads[4], "fsdp", scatter_dimension=1, tiled=True),
            lax.psum_scatter(grads[5], "fsdp", scatter_dimension=2, tiled=True),
            lax.psum_scatter(grads[6], "fsdp", scatter_dimension=1, tiled=True),
            lax.psum_scatter(grads[7], "fsdp", scatter_dimension=0, tiled=True),
            lax.psum_scatter(grads[8], "fsdp", scatter_dimension=1, tiled=True),
            lax.psum_scatter(grads[9], "fsdp", scatter_dimension=1, tiled=True),
            lax.psum_scatter(grads[10], "fsdp", scatter_dimension=1, tiled=True),
            lax.psum_scatter(grads[11], "fsdp", scatter_dimension=1, tiled=True),
            lax.psum_scatter(grads[12], "fsdp", scatter_dimension=1, tiled=True),
        )
        totals = tuple((total + share for total, share in zip(totals, shares)))
        return (
            totals,
            (
                output.astype(jnp.bfloat16),
                start_grad.astype(jnp.bfloat16),
                memory_grad.astype(jnp.bfloat16),
            ),
        )

    totals, stacked = lax.scan(step, start_totals, (tokens, encoder, cotangent))
    return (
        stacked[0],
        stacked[1],
        stacked[2],
        totals[0],
        totals[1],
        totals[2],
        totals[3],
        totals[4],
        totals[5],
        totals[6],
        totals[7],
        totals[8],
        totals[9],
        totals[10],
        totals[11],
        totals[12],
    )


def solution(mesh):
    placed = (
        P("fsdp", None, None),
        P("fsdp", None, None),
        P("fsdp", None, None),
        P(None, "fsdp", "tensor"),
        P(None, "tensor", "fsdp"),
        P("tensor", "fsdp"),
        P("fsdp", "tensor"),
        P(None, "fsdp", "tensor"),
        P(None, "tensor", "fsdp"),
        P("tensor", "fsdp"),
        P("fsdp", "tensor"),
        P("tensor", "fsdp"),
        P("tensor", "fsdp"),
        P(None, "fsdp"),
        P(None, "fsdp"),
        P(None, "fsdp"),
    )
    return jax.shard_map(
        on_device,
        mesh=mesh,
        in_specs=placed,
        out_specs=(
            P("fsdp", None, None),
            P("fsdp", None, None),
            P("fsdp", "tensor", None),
            P(None, "fsdp", "tensor"),
            P(None, "tensor", "fsdp"),
            P("tensor", "fsdp"),
            P("fsdp", "tensor"),
            P(None, "fsdp", "tensor"),
            P(None, "tensor", "fsdp"),
            P("tensor", "fsdp"),
            P("fsdp", "tensor"),
            P("tensor", "fsdp"),
            P("tensor", "fsdp"),
            P(None, "fsdp"),
            P(None, "fsdp"),
            P(None, "fsdp"),
        ),
        check_vma=False,
    )
```

profile of v0, /device:TPU:0, one launch (start us, length us, event | category | flops | bytes accessed | tf_op | source)
XLA Modules:
  0.0 2042.0 jit_solution(11307929338341830664)
XLA Ops:
  17.4 2013.7 %while.41 = (s32[]{:T(128)}, f32[3,128,256]{2,1,0:T(8,128)}, f32[2,1,32]{2,1,0:T(1,128)}, f32[256,128]{1,0:T(8,128)}, f32[128,256]{1,0:T(8,128)}, /*index=5*/f32...) while((s32[]{:T(128)}, f32[3,128,256]{2,1,0:T(8,128)}, ...), condition=%wide.region_53.54_spmd.clone, body=%wide.region_0.53_spmd.clone.sunk | while | flops 17469284352 | bytes 747983680 | solution.py:335
  20.3 10.6 all_gather.77
  50.5 10.9 all_gather.88
  61.4 12.1 all_gather.79
  91.5 9.7 all_gather.85
  109.5 9.1 all_gather.82
  156.6 9.3 all_gather.81
  165.9 36.5 %all-reduce.15.cloned.1.call-done = bf16[448,1024]{1,0:T(8,128)(2,1)} async-done(((bf16[448,1024]{1,0:T(8,128)(2,1)}), bf16[448,1024]{1,0:T(8,128)(2,1)}) %all-reduce.15.cloned.1.call-update) | async-done | bytes 917520 | tf_op jit(solution)/shard_map/while/body/eval_jaxpr/psum | solution.py:40
  205.8 25.2 %all-gather.5.cloned.1.call-done = bf16[1024,1024]{1,0:T(8,128)(2,1)} async-done(((bf16[128,1024]{1,0:T(8,128)(2,1)}), bf16[1024,1024]{1,0:T(8,128)(2,1)}) %all-gather.5.cloned.1.call-update) | async-done | bytes 2097168 | tf_op jit(solution)/shard_map/while/body/eval_jaxpr/all_gather | solution.py:292
  239.6 21.3 %all-gather.11.cloned.1.call-done = bf16[1024,1024]{1,0:T(8,128)(2,1)} async-done(((bf16[1024,128]{1,0:T(8,128)(2,1)}), bf16[1024,1024]{1,0:T(8,128)(2,1)}) %all-gather.11.cloned.1.call-update) | async-done | bytes 2097168 | tf_op jit(solution)/shard_map/while/body/eval_jaxpr/all_gather | solution.py:294
  269.7 47.7 %all-reduce.17.cloned.1.call-done = bf16[448,1024]{1,0:T(8,128)(2,1)} async-done(((bf16[448,1024]{1,0:T(8,128)(2,1)}), bf16[448,1024]{1,0:T(8,128)(2,1)}) %all-reduce.17.cloned.1.call-update) | async-done | bytes 917520 | tf_op jit(solution)/shard_map/while/body/eval_jaxpr/psum | solution.py:44
  345.4 42.8 %all-reduce.19.cloned.1.call-done = bf16[448,1024]{1,0:T(8,128)(2,1)} async-done(((bf16[448,1024]{1,0:T(8,128)(2,1)}), bf16[448,1024]{1,0:T(8,128)(2,1)}) %all-reduce.19.cloned.1.call-update) | async-done | bytes 917520 | tf_op jit(solution)/shard_map/while/body/eval_jaxpr/psum | solution.py:44
  436.3 45.1 %all-reduce.21.cloned.1.call-done = (bf16[448,1024]{1,0:T(8,128)(2,1)}, bf16[448,1024]{1,0:T(8,128)(2,1)}) async-done(((bf16[448,1024]{1,0:T(8,128)(2,1)}, bf16[448,1024]{1,0:T(8,128)(2,1)}), (bf16[448,1024]{1,0:T(8,128)(2,1)}, bf16[448,1024]{1,0:T(8,128)(2,1)})) %all-reduce.21.cloned.1.call-update) | async-done | bytes 1835024 | tf_op jit(solution)/shard_map/while/body/eval_jaxpr/psum | solution.py:44
  503.3 14.1 reduce-scatter.56.cloned.1.call-done
  527.2 58.5 %fusion.431 = bf16[376,1024]{1,0:T(8,128)(2,1)S(1)} fusion(bf16[1500,1024]{1,0:T(8,128)(2,1)} %add_convert_fusion.19), kind=kCustom, calls=%all-reduce-scatter.clone.1 | all-reduce-scatter fusion | flops 1540097 | bytes 3842560 | tf_op jit(solution)/shard_map/while
  599.9 27.8 %reduce-scatter.64.cloned.1.call-done = f32[128,3]{1,0:T(8,128)} async-done(((f32[1024,3]{1,0:T(8,128)}), f32[128,3]{1,0:T(8,128)}) %reduce-scatter.64.cloned.1.call-update) | async-done | bytes 1552 | tf_op jit(solution)/shard_map/while
  628.6 38.1 %reduce-scatter.52.cloned.1.call-done = f32[256,128]{1,0:T(8,128)} async-done(((f32[256,1024]{1,0:T(8,128)}), f32[256,128]{1,0:T(8,128)}) %reduce-scatter.52.cloned.1.call-update) | async-done | bytes 131088 | tf_op jit(solution)/shard_map/while/body/eval_jaxpr/reduce_scatter | solution.py:317
  668.3 37.4 %reduce-scatter.46.cloned.1.call-done = f32[128,256]{1,0:T(8,128)} async-done(((f32[1024,256]{1,0:T(8,128)}), f32[128,256]{1,0:T(8,128)}) %reduce-scatter.46.cloned.1.call-update) | async-done | bytes 131088 | tf_op jit(solution)/shard_map/while/body/eval_jaxpr/reduce_scatter | solution.py:314
  706.7 38.6 %reduce-scatter.44.cloned.1.call-done = f32[256,128]{1,0:T(8,128)} async-done(((f32[256,1024]{1,0:T(8,128)}), f32[256,128]{1,0:T(8,128)}) %reduce-scatter.44.cloned.1.call-update) | async-done | bytes 131088 | tf_op jit(solution)/shard_map/while/body/eval_jaxpr/reduce_scatter | solution.py:313
  751.3 31.1 %reduce-scatter.60.cloned.1.call-done = f32[128,3]{1,0:T(8,128)} async-done(((f32[1024,3]{1,0:T(8,128)}), f32[128,3]{1,0:T(8,128)}) %reduce-scatter.60.cloned.1.call-update) | async-done | bytes 1552 | tf_op jit(solution)/shard_map/while
  783.3 36.2 %reduce-scatter.62.cloned.1.call-done = f32[128,3]{1,0:T(8,128)} async-done(((f32[1024,3]{1,0:T(8,128)}), f32[128,3]{1,0:T(8,128)}) %reduce-scatter.62.cloned.1.call-update) | async-done | bytes 1552 | tf_op jit(solution)/shard_map/while
  821.5 42.3 %reduce-scatter.48.cloned.1.call-done = f32[2,128,256]{2,1,0:T(8,128)} async-done(((f32[2,1024,256]{2,1,0:T(8,128)}), f32[2,128,256]{2,1,0:T(8,128)}) %reduce-scatter.48.cloned.1.call-update) | async-done | bytes 262160 | tf_op jit(solution)/shard_map/while/body/eval_jaxpr/reduce_scatter | solution.py:315
  865.0 53.3 %reduce-scatter.54.cloned.1.call-done = f32[128,1024]{1,0:T(8,128)} async-done(((f32[1024,1024]{1,0:T(8,128)}), f32[128,1024]{1,0:T(8,128)}) %reduce-scatter.54.cloned.1.call-update) | async-done | bytes 524304 | tf_op jit(solution)/shard_map/while/body/eval_jaxpr/reduce_scatter | solution.py:318
  919.5 53.2 %reduce-scatter.58.cloned.1.call-done = f32[1024,128]{1,0:T(8,128)} async-done(((f32[1024,1024]{1,0:T(8,128)}), f32[1024,128]{1,0:T(8,128)}) %reduce-scatter.58.cloned.1.call-update) | async-done | bytes 524304 | tf_op jit(solution)/shard_map/while/body/eval_jaxpr/reduce_scatter | solution.py:320
  973.9 48.3 %reduce-scatter.40.cloned.1.call-done = f32[3,128,256]{2,1,0:T(8,128)} async-done(((f32[3,1024,256]{2,1,0:T(8,128)}), f32[3,128,256]{2,1,0:T(8,128)}) %reduce-scatter.40.cloned.1.call-update) | async-done | bytes 393232 | tf_op jit(solution)/shard_map/while/body/eval_jaxpr/reduce_scatter | solution.py:311
  1045.2 9.3 all_gather.87
  1055.6 11.9 all_gather.88
  1067.4 10.8 all_gather.79
  1096.3 9.5 all_gather.85
  1161.2 9.0 all_gather.81
  1170.2 36.7 %all-reduce.15.cloned.1.call-done = bf16[448,1024]{1,0:T(8,128)(2,1)} async-done(((bf16[448,1024]{1,0:T(8,128)(2,1)}), bf16[448,1024]{1,0:T(8,128)(2,1)}) %all-reduce.15.cloned.1.call-update) | async-done | bytes 917520 | tf_op jit(solution)/shard_map/while/body/eval_jaxpr/psum | solution.py:40
  1210.3 25.2 %all-gather.5.cloned.1.call-done = bf16[1024,1024]{1,0:T(8,128)(2,1)} async-done(((bf16[128,1024]{1,0:T(8,128)(2,1)}), bf16[1024,1024]{1,0:T(8,128)(2,1)}) %all-gather.5.cloned.1.call-update) | async-done | bytes 2097168 | tf_op jit(solution)/shard_map/while/body/eval_jaxpr/all_gather | solution.py:292
  1244.1 21.5 %all-gather.11.cloned.1.call-done = bf16[1024,1024]{1,0:T(8,128)(2,1)} async-done(((bf16[1024,128]{1,0:T(8,128)(2,1)}), bf16[1024,1024]{1,0:T(8,128)(2,1)}) %all-gather.11.cloned.1.call-update) | async-done | bytes 2097168 | tf_op jit(solution)/shard_map/while/body/eval_jaxpr/all_gather | solution.py:294
  1274.5 47.4 %all-reduce.17.cloned.1.call-done = bf16[448,1024]{1,0:T(8,128)(2,1)} async-done(((bf16[448,1024]{1,0:T(8,128)(2,1)}), bf16[448,1024]{1,0:T(8,128)(2,1)}) %all-reduce.17.cloned.1.call-update) | async-done | bytes 917520 | tf_op jit(solution)/shard_map/while/body/eval_jaxpr/psum | solution.py:44
  1349.9 42.8 %all-reduce.19.cloned.1.call-done = bf16[448,1024]{1,0:T(8,128)(2,1)} async-done(((bf16[448,1024]{1,0:T(8,128)(2,1)}), bf16[448,1024]{1,0:T(8,128)(2,1)}) %all-reduce.19.cloned.1.call-update) | async-done | bytes 917520 | tf_op jit(solution)/shard_map/while/body/eval_jaxpr/psum | solution.py:44
  1440.8 45.1 %all-reduce.21.cloned.1.call-done = (bf16[448,1024]{1,0:T(8,128)(2,1)}, bf16[448,1024]{1,0:T(8,128)(2,1)}) async-done(((bf16[448,1024]{1,0:T(8,128)(2,1)}, bf16[448,1024]{1,0:T(8,128)(2,1)}), (bf16[448,1024]{1,0:T(8,128)(2,1)}, bf16[448,1024]{1,0:T(8,128)(2,1)})) %all-reduce.21.cloned.1.call-update) | async-done | bytes 1835024 | tf_op jit(solution)/shard_map/while/body/eval_jaxpr/psum | solution.py:44
  1507.8 14.3 reduce-scatter.56.cloned.1.call-done
  1531.9 58.5 %fusion.431 = bf16[376,1024]{1,0:T(8,128)(2,1)S(1)} fusion(bf16[1500,1024]{1,0:T(8,128)(2,1)} %add_convert_fusion.19), kind=kCustom, calls=%all-reduce-scatter.clone.1 | all-reduce-scatter fusion | flops 1540097 | bytes 3842560 | tf_op jit(solution)/shard_map/while
  1604.6 27.8 %reduce-scatter.64.cloned.1.call-done = f32[128,3]{1,0:T(8,128)} async-done(((f32[1024,3]{1,0:T(8,128)}), f32[128,3]{1,0:T(8,128)}) %reduce-scatter.64.cloned.1.call-update) | async-done | bytes 1552 | tf_op jit(solution)/shard_map/while
  1633.3 38.1 %reduce-scatter.52.cloned.1.call-done = f32[256,128]{1,0:T(8,128)} async-done(((f32[256,1024]{1,0:T(8,128)}), f32[256,128]{1,0:T(8,128)}) %reduce-scatter.52.cloned.1.call-update) | async-done | bytes 131088 | tf_op jit(solution)/shard_map/while/body/eval_jaxpr/reduce_scatter | solution.py:317
  1673.0 37.4 %reduce-scatter.46.cloned.1.call-done = f32[128,256]{1,0:T(8,128)} async-done(((f32[1024,256]{1,0:T(8,128)}), f32[128,256]{1,0:T(8,128)}) %reduce-scatter.46.cloned.1.call-update) | async-done | bytes 131088 | tf_op jit(solution)/shard_map/while/body/eval_jaxpr/reduce_scatter | solution.py:314
  1711.4 38.8 %reduce-scatter.44.cloned.1.call-done = f32[256,128]{1,0:T(8,128)} async-done(((f32[256,1024]{1,0:T(8,128)}), f32[256,128]{1,0:T(8,128)}) %reduce-scatter.44.cloned.1.call-update) | async-done | bytes 131088 | tf_op jit(solution)/shard_map/while/body/eval_jaxpr/reduce_scatter | solution.py:313
  1756.1 31.1 %reduce-scatter.60.cloned.1.call-done = f32[128,3]{1,0:T(8,128)} async-done(((f32[1024,3]{1,0:T(8,128)}), f32[128,3]{1,0:T(8,128)}) %reduce-scatter.60.cloned.1.call-update) | async-done | bytes 1552 | tf_op jit(solution)/shard_map/while
  1788.1 36.3 %reduce-scatter.62.cloned.1.call-done = f32[128,3]{1,0:T(8,128)} async-done(((f32[1024,3]{1,0:T(8,128)}), f32[128,3]{1,0:T(8,128)}) %reduce-scatter.62.cloned.1.call-update) | async-done | bytes 1552 | tf_op jit(solution)/shard_map/while
  1827.9 41.0 %reduce-scatter.48.cloned.1.call-done = f32[2,128,256]{2,1,0:T(8,128)} async-done(((f32[2,1024,256]{2,1,0:T(8,128)}), f32[2,128,256]{2,1,0:T(8,128)}) %reduce-scatter.48.cloned.1.call-update) | async-done | bytes 262160 | tf_op jit(solution)/shard_map/while/body/eval_jaxpr/reduce_scatter | solution.py:315
  1870.0 53.4 %reduce-scatter.54.cloned.1.call-done = f32[128,1024]{1,0:T(8,128)} async-done(((f32[1024,1024]{1,0:T(8,128)}), f32[128,1024]{1,0:T(8,128)}) %reduce-scatter.54.cloned.1.call-update) | async-done | bytes 524304 | tf_op jit(solution)/shard_map/while/body/eval_jaxpr/reduce_scatter | solution.py:318
  1924.7 53.1 %reduce-scatter.58.cloned.1.call-done = f32[1024,128]{1,0:T(8,128)} async-done(((f32[1024,1024]{1,0:T(8,128)}), f32[1024,128]{1,0:T(8,128)}) %reduce-scatter.58.cloned.1.call-update) | async-done | bytes 524304 | tf_op jit(solution)/shard_map/while/body/eval_jaxpr/reduce_scatter | solution.py:320
  1978.9 48.2 %reduce-scatter.40.cloned.1.call-done = f32[3,128,256]{2,1,0:T(8,128)} async-done(((f32[3,1024,256]{2,1,0:T(8,128)}), f32[3,128,256]{2,1,0:T(8,128)}) %reduce-scatter.40.cloned.1.call-update) | async-done | bytes 393232 | tf_op jit(solution)/shard_map/while/body/eval_jaxpr/reduce_scatter | solution.py:311
  (877 shorter events, 514.7 us)
Async XLA Ops:
  17.4 56.5 %all-gather.9.cloned.1.call-start = ((), (), s32[]{:S(2)}) async-start(), calls=%async_computation.15 | async-start | bytes 1769472 | tf_op jit(solution)/shard_map/while/body/eval_jaxpr/all_gather | solution.py:285
  18.1 102.8 %all-gather.7.cloned.1.call-start = ((), (), s32[]{:S(2)}) async-start(), calls=%async_computation.14 | async-start | bytes 1179648 | tf_op jit(solution)/shard_map/while/body/eval_jaxpr/all_gather | solution.py:289
  18.9 120.9 %all-reduce.13.cloned.1.call-start = ((), (), s32[]{:S(2)}) async-start(), calls=%async_computation.16 | async-start | bytes 1835008 | tf_op jit(solution)/shard_map/while/body/eval_jaxpr/psum | solution.py:40
  19.9 463.3 %copy-start.63 = (f32[448]{0:T(512)}, f32[448]{0:T(512)S(1)}, u32[]{:S(2)}) copy-start(f32[448]{0:T(512)S(1)} %broadcast_multiply_fusion.6) | copy-start | bytes 5380 | tf_op jit(solution)/shard_map/while
  91.4 111.0 %all-reduce.15.cloned.1.call-start = ((), (), s32[]{:S(2)}) async-start(), calls=%async_computation.17 | async-start | bytes 1835008 | tf_op jit(solution)/shard_map/while/body/eval_jaxpr/psum | solution.py:40
  155.4 75.7 %all-gather.5.cloned.1.call-start = ((), (), s32[]{:S(2)}) async-start(), calls=%async_computation.13 | async-start | bytes 2359296 | tf_op jit(solution)/shard_map/while/body/eval_jaxpr/all_gather | solution.py:292
  156.0 105.0 %all-gather.11.cloned.1.call-start = ((), (), s32[]{:S(2)}) async-start(), calls=%async_computation.18 | async-start | bytes 2359296 | tf_op jit(solution)/shard_map/while/body/eval_jaxpr/all_gather | solution.py:294
  156.5 160.9 %all-reduce.17.cloned.1.call-start = ((), (), s32[]{:S(2)}) async-start(), calls=%async_computation.19 | async-start | bytes 1835008 | tf_op jit(solution)/shard_map/while/body/eval_jaxpr/psum | solution.py:44
  269.4 118.7 %all-reduce.19.cloned.1.call-start = ((), (), s32[]{:S(2)}) async-start(), calls=%async_computation.20 | async-start | bytes 1835008 | tf_op jit(solution)/shard_map/while/body/eval_jaxpr/psum | solution.py:44
  341.1 140.3 %all-reduce.21.cloned.1.call-start = ((), (), s32[]{:S(2)}) async-start(), calls=%async_computation.31 | async-start | bytes 3670016 | tf_op jit(solution)/shard_map/while/body/eval_jaxpr/psum | solution.py:44
  404.5 112.9 %reduce-scatter.56.cloned.1.call-start = ((), (), s32[]{:S(2)}) async-start(), calls=%async_computation.29 | async-start | bytes 589824 | tf_op jit(solution)/shard_map/while
  406.2 181.9 %reduce-scatter.50.cloned.1.call-start = ((), (), s32[]{:S(2)}) async-start(), calls=%async_computation.26 | async-start | bytes 147456 | tf_op jit(solution)/shard_map/while
  415.2 183.7 %reduce-scatter.42.cloned.1.call-start = ((), (), s32[]{:S(2)}) async-start(), calls=%async_computation.22 | async-start | bytes 147456 | tf_op jit(solution)/shard_map/while
  416.6 211.0 %reduce-scatter.64.cloned.1.call-start = ((), (), s32[]{:S(2)}) async-start(), calls=%async_computation.34 | async-start | bytes 589824 | tf_op jit(solution)/shard_map/while
  417.8 248.9 %reduce-scatter.52.cloned.1.call-start = ((), (), s32[]{:S(2)}) async-start(), calls=%async_computation.27 | async-start | bytes 1179648 | tf_op jit(solution)/shard_map/while/body/eval_jaxpr/reduce_scatter | solution.py:317
  421.1 284.6 %reduce-scatter.46.cloned.1.call-start = ((), (), s32[]{:S(2)}) async-start(), calls=%async_computation.24 | async-start | bytes 1179648 | tf_op jit(solution)/shard_map/while/body/eval_jaxpr/reduce_scatter | solution.py:314
  423.1 322.2 %reduce-scatter.44.cloned.1.call-start = ((), (), s32[]{:S(2)}) async-start(), calls=%async_computation.23 | async-start | bytes 1179648 | tf_op jit(solution)/shard_map/while/body/eval_jaxpr/reduce_scatter | solution.py:313
  426.2 356.1 %reduce-scatter.60.cloned.1.call-start = ((), (), s32[]{:S(2)}) async-start(), calls=%async_computation.32 | async-start | bytes 589824 | tf_op jit(solution)/shard_map/while
  485.9 333.6 %reduce-scatter.62.cloned.1.call-start = ((), (), s32[]{:S(2)}) async-start(), calls=%async_computation.33 | async-start | bytes 589824 | tf_op jit(solution)/shard_map/while
  487.7 376.2 %reduce-scatter.48.cloned.1.call-start = ((), (), s32[]{:S(2)}) async-start(), calls=%async_computation.25 | async-start | bytes 2359296 | tf_op jit(solution)/shard_map/while/body/eval_jaxpr/reduce_scatter | solution.py:315
  490.8 427.5 %reduce-scatter.54.cloned.1.call-start = ((), (), s32[]{:S(2)}) async-start(), calls=%async_computation.28 | async-start | bytes 4718592 | tf_op jit(solution)/shard_map/while/body/eval_jaxpr/reduce_scatter | solution.py:318
  496.7 476.1 %reduce-scatter.58.cloned.1.call-start = ((), (), s32[]{:S(2)}) async-start(), calls=%async_computation.30 | async-start | bytes 4718592 | tf_op jit(solution)/shard_map/while/body/eval_jaxpr/reduce_scatter | solution.py:320
  501.5 520.7 %reduce-scatter.40.cloned.1.call-start = ((), (), s32[]{:S(2)}) async-start(), calls=%async_computation.21 | async-start | bytes 3538944 | tf_op jit(solution)/shard_map/while/body/eval_jaxpr/reduce_scatter | solution.py:311
  586.3 4.6 collective-permute-start
  1024.2 54.5 %all-gather.9.cloned.1.call-start = ((), (), s32[]{:S(2)}) async-start(), calls=%async_computation.15 | async-start | bytes 1769472 | tf_op jit(solution)/shard_map/while/body/eval_jaxpr/all_gather | solution.py:285
  1025.0 100.5 %all-gather.7.cloned.1.call-start = ((), (), s32[]{:S(2)}) async-start(), calls=%async_computation.14 | async-start | bytes 1179648 | tf_op jit(solution)/shard_map/while/body/eval_jaxpr/all_gather | solution.py:289
  1025.6 118.7 %all-reduce.13.cloned.1.call-start = ((), (), s32[]{:S(2)}) async-start(), calls=%async_computation.16 | async-start | bytes 1835008 | tf_op jit(solution)/shard_map/while/body/eval_jaxpr/psum | solution.py:40
  1026.6 461.2 %copy-start.63 = (f32[448]{0:T(512)}, f32[448]{0:T(512)S(1)}, u32[]{:S(2)}) copy-start(f32[448]{0:T(512)S(1)} %broadcast_multiply_fusion.6) | copy-start | bytes 5380 | tf_op jit(solution)/shard_map/while
  1096.2 110.6 %all-reduce.15.cloned.1.call-start = ((), (), s32[]{:S(2)}) async-start(), calls=%async_computation.17 | async-start | bytes 1835008 | tf_op jit(solution)/shard_map/while/body/eval_jaxpr/psum | solution.py:40
  1159.8 75.7 %all-gather.5.cloned.1.call-start = ((), (), s32[]{:S(2)}) async-start(), calls=%async_computation.13 | async-start | bytes 2359296 | tf_op jit(solution)/shard_map/while/body/eval_jaxpr/all_gather | solution.py:292
  1160.4 105.1 %all-gather.11.cloned.1.call-start = ((), (), s32[]{:S(2)}) async-start(), calls=%async_computation.18 | async-start | bytes 2359296 | tf_op jit(solution)/shard_map/while/body/eval_jaxpr/all_gather | solution.py:294
  1161.1 160.8 %all-reduce.17.cloned.1.call-start = ((), (), s32[]{:S(2)}) async-start(), calls=%async_computation.19 | async-start | bytes 1835008 | tf_op jit(solution)/shard_map/while/body/eval_jaxpr/psum | solution.py:44
  1274.0 118.7 %all-reduce.19.cloned.1.call-start = ((), (), s32[]{:S(2)}) async-start(), calls=%async_computation.20 | async-start | bytes 1835008 | tf_op jit(solution)/shard_map/while/body/eval_jaxpr/psum | solution.py:44
  1345.6 140.3 %all-reduce.21.cloned.1.call-start = ((), (), s32[]{:S(2)}) async-start(), calls=%async_computation.31 | async-start | bytes 3670016 | tf_op jit(solution)/shard_map/while/body/eval_jaxpr/psum | solution.py:44
  1409.0 113.1 %reduce-scatter.56.cloned.1.call-start = ((), (), s32[]{:S(2)}) async-start(), calls=%async_computation.29 | async-start | bytes 589824 | tf_op jit(solution)/shard_map/while
  1410.8 182.1 %reduce-scatter.50.cloned.1.call-start = ((), (), s32[]{:S(2)}) async-start(), calls=%async_computation.26 | async-start | bytes 147456 | tf_op jit(solution)/shard_map/while
  1419.8 183.9 %reduce-scatter.42.cloned.1.call-start = ((), (), s32[]{:S(2)}) async-start(), calls=%async_computation.22 | async-start | bytes 147456 | tf_op jit(solution)/shard_map/while
  1421.2 211.2 %reduce-scatter.64.cloned.1.call-start = ((), (), s32[]{:S(2)}) async-start(), calls=%async_computation.34 | async-start | bytes 589824 | tf_op jit(solution)/shard_map/while
  1422.4 249.0 %reduce-scatter.52.cloned.1.call-start = ((), (), s32[]{:S(2)}) async-start(), calls=%async_computation.27 | async-start | bytes 1179648 | tf_op jit(solution)/shard_map/while/body/eval_jaxpr/reduce_scatter | solution.py:317
  1425.6 284.8 %reduce-scatter.46.cloned.1.call-start = ((), (), s32[]{:S(2)}) async-start(), calls=%async_computation.24 | async-start | bytes 1179648 | tf_op jit(solution)/shard_map/while/body/eval_jaxpr/reduce_scatter | solution.py:314
  1427.6 322.6 %reduce-scatter.44.cloned.1.call-start = ((), (), s32[]{:S(2)}) async-start(), calls=%async_computation.23 | async-start | bytes 1179648 | tf_op jit(solution)/shard_map/while/body/eval_jaxpr/reduce_scatter | solution.py:313
  1430.8 356.5 %reduce-scatter.60.cloned.1.call-start = ((), (), s32[]{:S(2)}) async-start(), calls=%async_computation.32 | async-start | bytes 589824 | tf_op jit(solution)/shard_map/while
  1490.5 334.0 %reduce-scatter.62.cloned.1.call-start = ((), (), s32[]{:S(2)}) async-start(), calls=%async_computation.33 | async-start | bytes 589824 | tf_op jit(solution)/shard_map/while
  1492.3 376.6 %reduce-scatter.48.cloned.1.call-start = ((), (), s32[]{:S(2)}) async-start(), calls=%async_computation.25 | async-start | bytes 2359296 | tf_op jit(solution)/shard_map/while/body/eval_jaxpr/reduce_scatter | solution.py:315
  1495.4 428.0 %reduce-scatter.54.cloned.1.call-start = ((), (), s32[]{:S(2)}) async-start(), calls=%async_computation.28 | async-start | bytes 4718592 | tf_op jit(solution)/shard_map/while/body/eval_jaxpr/reduce_scatter | solution.py:318
  1501.2 476.5 %reduce-scatter.58.cloned.1.call-start = ((), (), s32[]{:S(2)}) async-start(), calls=%async_computation.30 | async-start | bytes 4718592 | tf_op jit(solution)/shard_map/while/body/eval_jaxpr/reduce_scatter | solution.py:320
  1506.1 521.1 %reduce-scatter.40.cloned.1.call-start = ((), (), s32[]{:S(2)}) async-start(), calls=%async_computation.21 | async-start | bytes 3538944 | tf_op jit(solution)/shard_map/while/body/eval_jaxpr/reduce_scatter | solution.py:311
  1591.0 4.6 collective-permute-start
  (233 other events, 7680.7 us)
Sparse Core Ops, SparseCore 0:
  20.1 28.4 all-gather.8
  50.5 24.2 all-gather.6
  91.5 48.2 all-reduce.12
  155.5 46.8 all-reduce.14
  204.2 26.8 all-gather.4
  232.8 28.0 all-gather.10
  269.5 47.8 all-reduce.16
  341.2 46.8 all-reduce.18
  404.6 76.7 all-reduce.20
  484.3 33.0 reduce-scatter.55
  520.4 33.5 reduce-scatter.49
  556.9 33.5 reduce-scatter.41
  593.6 34.0 reduce-scatter.63
  630.7 35.9 reduce-scatter.51
  669.7 35.9 reduce-scatter.45
  709.3 35.9 reduce-scatter.43
  748.2 34.0 reduce-scatter.59
  785.3 34.0 reduce-scatter.61
  822.7 41.1 reduce-scatter.47
  867.1 51.1 reduce-scatter.53
  921.7 51.0 reduce-scatter.57
  976.1 46.0 reduce-scatter.39
  1027.0 25.7 all-gather.8
  1054.5 25.0 all-gather.6
  1096.3 47.8 all-reduce.12
  1159.9 46.8 all-reduce.14
  1208.6 26.8 all-gather.4
  1237.4 28.0 all-gather.10
  1274.1 47.7 all-reduce.16
  1345.8 46.9 all-reduce.18
  1409.2 76.7 all-reduce.20
  1489.0 33.0 reduce-scatter.55
  1525.0 33.5 reduce-scatter.49
  1561.6 33.5 reduce-scatter.41
  1598.2 34.0 reduce-scatter.63
  1635.4 35.9 reduce-scatter.51
  1674.4 35.9 reduce-scatter.45
  1714.2 35.9 reduce-scatter.43
  1753.1 34.0 reduce-scatter.59
  1790.3 34.0 reduce-scatter.61
  1827.7 41.1 reduce-scatter.47
  1872.3 51.1 reduce-scatter.53
  1926.6 51.0 reduce-scatter.57
  1981.1 46.0 reduce-scatter.39
where the time goes:
time: 2050 us; the launch traced here: 2040 us
  waiting for transfers between devices  1300 us (63%)
  blocking collectives  289 us (14%)
  matrix products  215 us (10%)
  local copies, waits for them, and re-layouts  108 us (5%)
  other arithmetic  105 us (5%)
    psum x6, waiting for transfers between devices, input_total(): lax.psum(partial_sum.astype(jnp.bfloat16), 'tensor').astype(jnp.float32)  271 us
    while x58, waiting for transfers between devices  224 us
    while x2, blocking collectives  117 us
    reduce_scatter x2, waiting for transfers between devices, step(): lax.psum_scatter(grads[7], 'fsdp', scatter_dimension=0, tiled=True)  107 us
    reduce_scatter x2, waiting for transfers between devices, step(): lax.psum_scatter(grads[9], 'fsdp', scatter_dimension=1, tiled=True)  106 us
    reduce_scatter x2, waiting for transfers between devices, step(): lax.psum_scatter(grads[0], 'fsdp', scatter_dimension=1, tiled=True)  96.5 us
    psum x4, waiting for transfers between devices, branch_total(): lax.psum(partial_sum.astype(jnp.bfloat16), 'tensor').astype(jnp.float32)  86 us
    reduce_scatter x2, waiting for transfers between devices, step(): lax.psum_scatter(grads[4], 'fsdp', scatter_dimension=1, tiled=True)  83.3 us
  transfers between devices with their start and end apart: 46, of which 36 were waited for; matrix products, arithmetic and copies ran while one was open for 19% of the time, Pallas kernels for 0%

commit v1 on v0

v1 whole, which is shorter than its diff:
```python
import functools
import math

import jax
import jax.numpy as jnp
from jax import lax
from jax.experimental import pallas as pl
from jax.experimental.pallas import tpu as pltpu
from jax.sharding import PartitionSpec as P

HEAD_DIM = 64
PAIR = 2 * HEAD_DIM
GROUPS = 4
EPSILON = 1e-05
MASKED = -1e9
F32 = jnp.float32
BF16 = jnp.bfloat16
VMEM_LIMIT = 60 * 1024 * 1024


def params(**extra):
    return pltpu.CompilerParams(vmem_limit_bytes=VMEM_LIMIT, **extra)


def call(kernel, name, grid, ins, outs, args, scratch=(), flops=0, scalars=1, aliases=None):
    in_specs = [pl.BlockSpec(block, index) for block, index in ins]
    out_specs = [pl.BlockSpec(block, index) for _, _, block, index in outs]
    out_shape = [jax.ShapeDtypeStruct(shape, dtype) for shape, dtype, _, _ in outs]
    moved = sum(a.size * a.dtype.itemsize for a in args) + sum(
        math.prod(o.shape) * jnp.dtype(o.dtype).itemsize for o in out_shape
    )
    result = pl.pallas_call(
        kernel,
        name=name,
        out_shape=out_shape,
        grid_spec=pltpu.PrefetchScalarGridSpec(
            num_scalar_prefetch=scalars,
            grid=grid,
            in_specs=in_specs,
            out_specs=out_specs,
            scratch_shapes=list(scratch),
        ),
        compiler_params=params(),
        cost_estimate=pl.CostEstimate(flops=int(flops), bytes_accessed=int(moved), transcendentals=0),
    )(*args)
    return result


def fill_weights(g_ref, pieces, buffer):
    rows = pieces[0].shape[-2]
    g = g_ref[0]
    for j, piece in enumerate(pieces):
        buffer[pl.ds(pl.multiple_of((g ^ j) * rows, rows), rows), :] = piece[...]


def nn_kernel(mode, g_ref, *refs):
    x_ref, pieces, rest = refs[0], refs[1:5], refs[5:]
    *extra, buffer = rest
    fill_weights(g_ref, pieces, buffer)
    acc = jnp.dot(x_ref[...], buffer[...], preferred_element_type=F32)
    if mode == "plain":
        (out,) = extra
        out[...] = acc.astype(out.dtype)
    elif mode == "bias":
        bias, out = extra
        out[...] = (acc + bias[...]).astype(out.dtype)
    elif mode == "gelu":
        bias, out, slope = extra
        expanded = acc + bias[...]
        phi = 0.5 * (1.0 + lax.erf(expanded * (0.5**0.5)))
        out[...] = (expanded * phi).astype(out.dtype)
        density = jnp.exp(expanded * expanded * -0.5) * ((2.0 * math.pi) ** -0.5)
        slope[...] = (phi + expanded * density).astype(slope.dtype)
    elif mode == "slope":
        slope, out, sums = extra
        grad = acc * slope[...].astype(F32)
        out[...] = grad.astype(out.dtype)
        sums[...] = jnp.broadcast_to(jnp.sum(grad, axis=0, keepdims=True), sums.shape)


def mm_nn(name, g, x, pieces, width, col, mode="plain", bias=None, slope=None):
    m, d = x.shape
    slots, rows, _ = pieces[0].shape
    ins = [((m, d), lambda s, g: (0, 0))]
    ins += [((None, rows, width), lambda s, g: (s, 0, col))] * GROUPS
    args = [g, x, *pieces]
    outs = [((m, slots * width), BF16, (m, width), lambda s, g: (0, s))]
    if mode in ("bias", "gelu"):
        ins.append(((None, 1, width), lambda s, g: (s, 0, 0)))
        args.append(bias)
    if mode == "gelu":
        outs.append(((m, slots * width), F32, (m, width), lambda s, g: (0, s)))
    if mode == "slope":
        ins.append(((m, width), lambda s, g: (0, s)))
        args.append(slope)
        outs.append(((slots, 8, width), F32, (None, 8, width), lambda s, g: (s, 0, 0)))
    return call(
        functools.partial(nn_kernel, mode), name, (slots,), ins, outs, args,
        scratch=[pltpu.VMEM((rows * GROUPS, width), BF16)],
        flops=2 * m * d * slots * width,
    )


def nt_kernel(slots, g_ref, *refs):
    x_ref, pieces, (out, acc, buffer) = refs[0], refs[1:5], refs[5:]
    s = pl.program_id(0)
    fill_weights(g_ref, pieces, buffer)
    part = lax.dot_general(
        x_ref[...], buffer[...], (((1,), (1,)), ((), ())), preferred_element_type=F32
    )

    @pl.when(s == 0)
    def _():
        acc[...] = part

    @pl.when(jnp.logical_and(s > 0, s < slots - 1))
    def _():
        acc[...] += part

    @pl.when(s == slots - 1)
    def _():
        out[...] = (acc[...] + part).astype(out.dtype)


def mm_nt(name, g, x, pieces, width, col):
    m = x.shape[0]
    slots, rows, _ = pieces[0].shape
    d = rows * GROUPS
    ins = [((m, width), lambda s, g: (0, s))]
    ins += [((None, rows, width), lambda s, g: (s, 0, col))] * GROUPS
    outs = [((m, d), BF16, (m, d), lambda s, g: (0, 0))]
    return call(
        functools.partial(nt_kernel, slots), name, (slots,), ins, outs, [g, x, *pieces],
        scratch=[pltpu.VMEM((m, d), F32), pltpu.VMEM((d, width), BF16)],
        flops=2 * m * d * slots * width,
    )[0]


def tn_kernel(g_ref, x_ref, y_ref, *refs):
    outs, buffer = refs[:GROUPS], refs[GROUPS]
    rows = outs[0].shape[-2]
    g = g_ref[0]
    buffer[...] = lax.dot_general(
        x_ref[...], y_ref[...], (((0,), (0,)), ((), ())), preferred_element_type=F32
    ).astype(BF16)
    for j, out in enumerate(outs):
        out[...] = buffer[pl.ds(pl.multiple_of((g ^ j) * rows, rows), rows), :]


def mm_tn(name, g, x, y, slots):
    m, d = x.shape
    width = y.shape[1] // slots
    rows = d // GROUPS
    ins = [((m, d), lambda s, g: (0, 0)), ((m, width), lambda s, g: (0, s))]
    outs = [((slots, rows, width), BF16, (None, rows, width), lambda s, g: (s, 0, 0))] * GROUPS
    return call(
        tn_kernel, name, (slots,), ins, outs, [g, x, y],
        scratch=[pltpu.VMEM((d, width), BF16)],
        flops=2 * m * d * slots * width,
    )


def scores_of(keys, queries, causal, valid):
    scores = lax.dot_general(keys, queries, (((1,), (1,)), ((), ())), preferred_element_type=F32)
    if causal:
        key_at = lax.broadcasted_iota(jnp.int32, scores.shape, 0)
        query_at = lax.broadcasted_iota(jnp.int32, scores.shape, 1)
        scores = jnp.where(key_at <= query_at, scores, MASKED)
    if valid < scores.shape[0]:
        key_at = lax.broadcasted_iota(jnp.int32, scores.shape, 0)
        scores = jnp.where(key_at < valid, scores, -jnp.inf)
    return scores


def head_mask(shape, h):
    lane = lax.broadcasted_iota(jnp.int32, shape, 1)
    return (lane // HEAD_DIM) == h


def attend_kernel(causal, blocks, valid, shared, *refs):
    if shared:
        qkv_ref, out_ref, log_ref, score_buf = refs
        q_all = qkv_ref[:, :PAIR]
    else:
        q_ref, kv_ref, out_ref, log_ref, score_buf = refs
        q_all = q_ref[...]
    h = pl.program_id(1)
    chosen = head_mask(q_all.shape, h)
    queries = jnp.where(chosen, q_all.astype(F32) * (HEAD_DIM**-0.5), 0.0).astype(BF16)
    size = score_buf.shape[0] // blocks

    def keys_at(i):
        at = pl.ds(pl.multiple_of(i * size, size), size)
        return (qkv_ref[at, PAIR : 2 * PAIR] if shared else kv_ref[at, :PAIR]), (
            qkv_ref[at, 2 * PAIR :] if shared else kv_ref[at, PAIR:]
        )

    top = None
    for i in range(blocks):
        scores = scores_of(keys_at(i)[0], queries, causal, valid)
        score_buf[i * size : (i + 1) * size, :] = scores
        now = jnp.max(scores, axis=0, keepdims=True)
        top = now if top is None else jnp.maximum(top, now)
    total = jnp.zeros_like(top)
    mixed = None
    for i in range(blocks):
        raised = jnp.exp(score_buf[i * size : (i + 1) * size, :] - top)
        total += jnp.sum(raised, axis=0, keepdims=True)
        part = lax.dot_general(
            keys_at(i)[1], raised.astype(BF16), (((0,), (0,)), ((), ())), preferred_element_type=F32
        )
        mixed = part if mixed is None else mixed + part
    log_ref[...] = jnp.broadcast_to(top + jnp.log(total), log_ref.shape)
    mixed = jnp.transpose(mixed / total).astype(BF16)

    @pl.when(h == 0)
    def _():
        out_ref[...] = mixed

    @pl.when(h == 1)
    def _():
        out_ref[...] = jnp.where(chosen, mixed, out_ref[...])


def attend(name, q, kv, causal, blocks, valid):
    shared = kv is None
    m = q.shape[0]
    slots = q.shape[1] // (3 * PAIR if shared else PAIR)
    n = m if shared else kv.shape[0]
    ins = [((m, (3 if shared else 1) * PAIR), lambda s, h: (0, s))]
    args = [q]
    if not shared:
        ins.append(((n, 2 * PAIR), lambda s, h: (0, s)))
        args.append(kv)
    outs = [
        ((m, slots * PAIR), BF16, (m, PAIR), lambda s, h: (0, s)),
        ((slots * 2, 8, m), F32, (None, 8, m), lambda s, h: (s * 2 + h, 0, 0)),
    ]
    return call(
        functools.partial(attend_kernel, causal, blocks, valid, shared), name, (slots, 2), ins, outs, args,
        scratch=[pltpu.VMEM((n, m), F32)],
        flops=4 * m * n * HEAD_DIM * 2 * slots, scalars=0,
    )


def attend_back_kernel(causal, blocks, valid, shared, *refs):
    if shared:
        qkv_ref, up_ref, log_ref, out_ref, sums_ref, chance_buf, grad_buf = refs
        q_all = qkv_ref[:, :PAIR]
    else:
        q_ref, kv_ref, up_ref, log_ref, out_q, out_ref, sums_ref, chance_buf, grad_buf = refs
        q_all = q_ref[...]
    h = pl.program_id(1)
    chosen = head_mask(q_all.shape, h)
    queries = jnp.where(chosen, q_all.astype(F32) * (HEAD_DIM**-0.5), 0.0).astype(BF16)
    upstream = jnp.where(chosen, up_ref[...].astype(F32), 0.0).astype(BF16)
    log_total = log_ref[0:1, :]
    size = chance_buf.shape[0] // blocks

    def keys_at(i):
        at = slice(i * size, (i + 1) * size)
        return (qkv_ref[at, PAIR : 2 * PAIR] if shared else kv_ref[at, :PAIR]), (
            qkv_ref[at, 2 * PAIR :] if shared else kv_ref[at, PAIR:]
        )

    def put(at, columns, value):
        keep = head_mask(value.shape, h)

        @pl.when(h == 0)
        def _():
            out_ref[at, columns] = value.astype(BF16)

        @pl.when(h == 1)
        def _():
            out_ref[at, columns] = jnp.where(keep, value.astype(BF16), out_ref[at, columns])

    first = PAIR if shared else 0
    inner = None
    value_sum = None
    for i in range(blocks):
        at = slice(i * size, (i + 1) * size)
        keys, values = keys_at(i)
        chance = jnp.exp(scores_of(keys, queries, causal, valid) - log_total)
        grad = lax.dot_general(values, upstream, (((1,), (1,)), ((), ())), preferred_element_type=F32)
        chance_buf[at, :] = chance
        grad_buf[at, :] = grad
        now = jnp.sum(chance * grad, axis=0, keepdims=True)
        inner = now if inner is None else inner + now
        value_grad = jnp.dot(chance.astype(BF16), upstream, preferred_element_type=F32)
        now = jnp.sum(value_grad, axis=0, keepdims=True)
        value_sum = now if value_sum is None else value_sum + now
        put(at, slice(first + PAIR, first + 2 * PAIR), value_grad)
    query_grad = None
    for i in range(blocks):
        at = slice(i * size, (i + 1) * size)
        keys, values = keys_at(i)
        score_grad = (chance_buf[at, :] * (grad_buf[at, :] - inner)).astype(BF16)
        put(at, slice(first, first + PAIR), jnp.dot(score_grad, queries, preferred_element_type=F32))
        part = lax.dot_general(keys, score_grad, (((0,), (0,)), ((), ())), preferred_element_type=F32)
        query_grad = part if query_grad is None else query_grad + part
    query_grad = jnp.transpose(query_grad) * (HEAD_DIM**-0.5)
    query_sum = jnp.sum(query_grad, axis=0, keepdims=True)
    row = lax.broadcasted_iota(jnp.int32, (8, PAIR), 0)
    sums = jnp.where(row == 0, query_sum, jnp.where(row == 1, value_sum, 0.0))
    target = out_ref if shared else out_q
    keep = head_mask(query_grad.shape, h)

    @pl.when(h == 0)
    def _():
        target[:, :PAIR] = query_grad.astype(BF16)
        sums_ref[...] = sums

    @pl.when(h == 1)
    def _():
        target[:, :PAIR] = jnp.where(keep, query_grad.astype(BF16), target[:, :PAIR])
        sums_ref[...] = jnp.where(head_mask(sums.shape, h), sums, sums_ref[...])


def attend_back(name, q, kv, upstream, logs, causal, blocks, valid):
    shared = kv is None
    m = q.shape[0]
    slots = upstream.shape[1] // PAIR
    n = m if shared else kv.shape[0]
    ins = [((m, (3 if shared else 1) * PAIR), lambda s, h: (0, s))]
    args = [q]
    outs = []
    if not shared:
        ins.append(((n, 2 * PAIR), lambda s, h: (0, s)))
        args.append(kv)
        outs.append(((m, slots * PAIR), BF16, (m, PAIR), lambda s, h: (0, s)))
    ins.append(((m, PAIR), lambda s, h: (0, s)))
    ins.append(((None, 8, m), lambda s, h: (s * 2 + h, 0, 0)))
    args += [upstream, logs]
    wide = (3 if shared else 2) * PAIR
    outs.append(((n, slots * wide), BF16, (n, wide), lambda s, h: (0, s)))
    outs.append(((slots, 8, PAIR), F32, (None, 8, PAIR), lambda s, h: (s, 0, 0)))
    return call(
        functools.partial(attend_back_kernel, causal, blocks, valid, shared), name, (slots, 2), ins, outs, args,
        scratch=[pltpu.VMEM((n, m), F32), pltpu.VMEM((n, m), F32)],
        flops=10 * m * n * HEAD_DIM * 2 * slots, scalars=0,
    )


def row_blocks(m):
    for count in (4, 2):
        if m % (16 * count) == 0:
            return count
    return 1


def normal(values):
    centre = values - jnp.mean(values, axis=-1, keepdims=True)
    inverse = lax.rsqrt(jnp.mean(centre * centre, axis=-1, keepdims=True) + EPSILON)
    return centre * inverse, inverse


def norm_kernel(parts, normed, *refs):
    base, rest = refs[0], refs[1:]
    value = base[...].astype(F32)
    if parts:
        own, came, bias = rest[:3]
        rest = rest[3:]
        value = value + (own[...].astype(F32) + came[...].astype(F32)) + bias[...]
    if normed:
        gain, shift = rest[:2]
        rest = rest[2:]
        rest[-1][...] = (normal(value)[0] * gain[...] + shift[...]).astype(BF16)
    if parts:
        rest[0][...] = value.astype(rest[0].dtype)


def norm_forward(name, base, own=None, came=None, bias=None, gain=None, shift=None, kept=F32):
    m, d = base.shape
    count = row_blocks(m)
    block = ((m // count, d), lambda i: (i, 0))
    line = ((1, d), lambda i: (0, 0))
    ins, args, outs = [block], [base], []
    if own is not None:
        ins += [block, block, line]
        args += [own, came, bias]
        outs.append(((m, d), kept, *block))
    if gain is not None:
        ins += [line, line]
        args += [gain, shift]
        outs.append(((m, d), BF16, *block))
    return call(
        functools.partial(norm_kernel, own is not None, gain is not None), name, (count,), ins, outs, args,
        flops=20 * m * d, scalars=0,
    )


def norm_back_kernel(want_low, own, came, values, gain, upstream, *outs):
    grad_ref, sums = outs[0], outs[-1]
    q = own[...].astype(F32) + came[...].astype(F32)
    n, inverse = normal(values[...].astype(F32))
    up = upstream[...].astype(F32)
    g = q * gain[...]
    back = inverse * (g - jnp.mean(g, axis=-1, keepdims=True) - n * jnp.mean(g * n, axis=-1, keepdims=True))
    grad = up + back
    grad_ref[...] = grad.astype(grad_ref.dtype)
    if want_low:
        outs[1][...] = grad.astype(BF16)
    row = lax.broadcasted_iota(jnp.int32, sums.shape, 0)
    now = jnp.zeros(sums.shape, F32)
    for at, term in enumerate((q * n, q, grad, up)):
        now = jnp.where(row == at, jnp.sum(term, axis=0, keepdims=True), now)

    @pl.when(pl.program_id(0) == 0)
    def _():
        sums[...] = now

    @pl.when(pl.program_id(0) > 0)
    def _():
        sums[...] += now


def norm_back(name, own, came, values, gain, upstream, want_low):
    m, d = values.shape
    count = row_blocks(m)
    block = ((m // count, d), lambda i: (i, 0))
    line = ((1, d), lambda i: (0, 0))
    outs = [((m, d), F32 if want_low else BF16, *block)]
    if want_low:
        outs.append(((m, d), BF16, *block))
    outs.append(((8, d), F32, (8, d), lambda i: (0, 0)))
    return call(
        functools.partial(norm_back_kernel, want_low), name, (count,), [block, block, block, line, block], outs,
        [own, came, values, gain, upstream], flops=30 * m * d, scalars=0,
    )


def flip(x, bit, size):
    return lax.ppermute(x, "fsdp", [(i, i ^ (1 << bit)) for i in range(size)])


def turn(x, step, size):
    return lax.ppermute(x, "tensor", [(i, (i + step) % size) for i in range(size)])


def half(x, index, axis):
    size = x.shape[axis] // 2
    return lax.dynamic_slice_in_dim(x, index * size, size, axis=axis)


def on_device(
    n_f, n_t,
    tokens, encoder, cotangent, self_weights, self_biases, self_output, cross_query, cross_memory,
    cross_biases, cross_output, hidden_weight, hidden_bias, reduce_weight, norm_gains, norm_shifts, branch_biases,
):
    bits = n_f.bit_length() - 1
    f = lax.axis_index("fsdp")
    z = lax.axis_index("tensor")
    core = f % 2
    group = f >> (bits - 2)
    g = group.astype(jnp.int32).reshape(1)
    length, d = tokens.shape[1], tokens.shape[2]
    frames = encoder.shape[1]
    own_clips = tokens.shape[0]
    assert own_clips * 2 == n_t and bits >= 3

    per = d // n_f
    units = hidden_bias.shape[1] * n_f
    heads_wide = self_biases.shape[2] * n_f

    def spread_features(v):
        wide = jnp.zeros((v.shape[0], d), BF16)
        return lax.dynamic_update_slice(wide, v, (0, f * per))

    def spread_units(v, total):
        v = v.reshape(v.shape[0], 1, -1)
        wide = jnp.zeros((v.shape[0], n_t, total), BF16)
        return lax.dynamic_update_slice(wide, v, (0, z, f * v.shape[2]))

    first = jnp.where(z == 0, 1, 0).astype(BF16)
    feature_rows = spread_features(jnp.concatenate([norm_gains, norm_shifts, branch_biases])) * first
    unit_rows = [
        spread_units(hidden_bias, units),
        spread_units(self_biases.reshape(2, -1), heads_wide),
        spread_units(cross_biases.reshape(2, -1), heads_wide),
    ]
    packed = jnp.concatenate([feature_rows.reshape(-1)] + [u.reshape(-1) for u in unit_rows]).reshape(-1, 1024)
    for bit in range(bits):
        packed = packed + flip(packed, bit, n_f)
    for step in (1, 2):
        packed = packed + lax.ppermute(packed, "tensor", [(i, i ^ step) for i in range(n_t)])
    packed = packed.reshape(-1).astype(F32)
    feature_all = packed[: 9 * d].reshape(9, d)
    at = 9 * d
    hidden_all = packed[at : at + n_t * units].reshape(1, n_t, units)
    at += n_t * units
    self_all = packed[at : at + 2 * n_t * heads_wide].reshape(2, n_t, heads_wide)
    at += 2 * n_t * heads_wide
    cross_all = packed[at : at + 2 * n_t * heads_wide].reshape(2, n_t, heads_wide)
    gains, shifts, branch = feature_all[0:3], feature_all[3:6], feature_all[6:9]

    def to_slots(v):
        mine = half(v, core, 2)
        return jnp.stack(
            [lax.dynamic_index_in_dim(mine, (z - s) % n_t, axis=1, keepdims=False) for s in range(n_t)]
        )

    hidden_slots = to_slots(hidden_all)
    self_slots = to_slots(self_all)
    cross_slots = to_slots(cross_all)
    zero_slots = jnp.zeros_like(self_slots[:, :1])
    qkv_bias = jnp.concatenate([self_slots[:, :1], zero_slots, self_slots[:, 1:]], axis=2)
    cq_bias = cross_slots[:, :1]
    ckv_bias = jnp.concatenate([zero_slots, cross_slots[:, 1:]], axis=2)

    mine = core == z // own_clips

    def take_clip(x):
        x = lax.dynamic_index_in_dim(x, z % own_clips, axis=0, keepdims=False)
        return jnp.where(mine, x, flip(x, 0, n_f))

    part_frames = frames // n_t
    part_pad = -(-part_frames // 128) * 128
    start = take_clip(tokens)
    upstream_low = take_clip(cotangent)
    memory = jnp.pad(
        take_clip(encoder).reshape(n_t, part_frames, d), ((0, 0), (0, part_pad - part_frames), (0, 0))
    ).reshape(n_t * part_pad, d)

    def gather(weights, through):
        keep = jnp.concatenate([half(w, core, 1) for w in weights], axis=1)
        send = jnp.concatenate([half(w, 1 - core, 1) for w in weights], axis=1)
        came = flip(send, 0, n_f)
        now = jnp.where(core == 0, jnp.concatenate([keep, came]), jnp.concatenate([came, keep]))
        for bit in range(1, bits - 2):
            came = flip(now, bit, n_f)
            low = (f >> bit) % 2 == 0
            now = jnp.where(low, jnp.concatenate([now, came]), jnp.concatenate([came, now]))
        slots = [now]
        for _ in range(n_t - 1):
            slots.append(turn(slots[-1], 1, n_t))
        zero = jnp.stack(slots)
        one = flip(zero, bits - 2, n_f)
        two = flip(zero, bits - 1, n_f)
        three = flip(one, bits - 1, n_f) if through == 1 else flip(two, bits - 2, n_f)
        return (zero, one, two, three)

    w_qkv = gather([self_weights[0], self_weights[1], self_weights[2]], 1)
    w_mid = gather([self_output.T, cross_query], 2)
    w_cross = gather([cross_memory[0], cross_memory[1], cross_output.T], 2)
    w_hidden = gather([hidden_weight], 1)
    w_reduce = gather([reduce_weight.T], 2)

    def scatter(pieces, through):
        zero, one, two, three = pieces

        def slot_sum(a, b):
            return (a.astype(F32) + b.astype(F32)).astype(BF16)

        if through == 1:
            two, three = flip(two, bits - 1, n_f), flip(three, bits - 1, n_f)
            zero, one = slot_sum(zero, two), slot_sum(one, three)
            other = flip(one, bits - 2, n_f)
        else:
            one, three = flip(one, bits - 2, n_f), flip(three, bits - 2, n_f)
            zero, two = slot_sum(zero, one), slot_sum(two, three)
            other = flip(two, bits - 1, n_f)
        slots = [slot_sum(zero[s], other[s]) for s in range(n_t)]
        now = slots[-1]
        for s in range(n_t - 2, -1, -1):
            now = turn(now, -1, n_t)
            now = slots[s].astype(F32) + now.astype(F32)
            if s:
                now = now.astype(BF16)
        for bit in range(bits - 3, 0, -1):
            up = (f >> bit) % 2
            keep, send = half(now, up, 0), half(now, 1 - up, 0)
            now = keep + flip(send.astype(BF16), bit, n_f).astype(F32)
        keep, send = half(now, core, 0), half(now, 1 - core, 0)
        came = flip(send, 0, n_f)
        return keep, came

    def unpack(shares, widths):
        keep, came = shares
        result, at = [], 0
        for width in widths:
            a, b = keep[:, at : at + width], came[:, at : at + width]
            result.append(jnp.where(core == 0, jnp.concatenate([a, b], 1), jnp.concatenate([b, a], 1)))
            at += width
        return result

    line = lambda rows, at: rows[at : at + 1]
    (normed_one,) = norm_forward("norm_one", start, gain=line(gains, 0), shift=line(shifts, 0))
    (qkv,) = mm_nn("qkv", g, normed_one, w_qkv, 3 * PAIR, 0, "bias", bias=qkv_bias)
    mixed_one, log_one = attend("self_attention", qkv, None, True, 1, length)
    part = mm_nt("self_out", g, mixed_one, w_mid, PAIR, 0)
    (cross_kv,) = mm_nn("cross_kv", g, memory, w_cross, 2 * PAIR, 0, "bias", bias=ckv_bias)
    middle, normed_two = norm_forward(
        "norm_two", start, part, flip(part, 0, n_f), line(branch, 0), line(gains, 1), line(shifts, 1)
    )
    (cross_q,) = mm_nn("cross_q", g, normed_two, w_mid, PAIR, 1, "bias", bias=cq_bias)
    mixed_two, log_two = attend("cross_attention", cross_q, cross_kv, False, n_t, part_frames)
    part = mm_nt("cross_out", g, mixed_two, w_cross, PAIR, 2)
    later, normed_three = norm_forward(
        "norm_three", middle, part, flip(part, 0, n_f), line(branch, 1), line(gains, 2), line(shifts, 2)
    )
    activated, slope = mm_nn("hidden", g, normed_three, w_hidden, units // 2, 0, "gelu", bias=hidden_slots)
    part = mm_nt("reduce", g, activated, w_reduce, units // 2, 0)
    (output,) = norm_forward("output", later, part, flip(part, 0, n_f), line(branch, 2), kept=BF16)

    g_reduce = mm_tn("reduce_grad", g, upstream_low, activated, n_t)
    expanded_low, hidden_sums = mm_nn("expanded_grad", g, upstream_low, w_reduce, units // 2, 0, "slope", slope=slope)
    part = mm_nt("normed_three_grad", g, expanded_low, w_hidden, units // 2, 0)
    g_hidden = mm_tn("hidden_grad", g, normed_three, expanded_low, n_t)
    later_grad, later_low, sums_three = norm_back(
        "norm_three_back", part, flip(part, 0, n_f), later, line(gains, 2), upstream_low, True
    )
    (mixed_two_grad,) = mm_nn("mixed_two_grad", g, later_low, w_cross, PAIR, 2)
    cq_low, ckv_low, cross_sums = attend_back(
        "cross_attention_back", cross_q, cross_kv, mixed_two_grad, log_two, False, n_t, part_frames
    )
    part = mm_nt("normed_two_grad", g, cq_low, w_mid, PAIR, 1)
    g_cross_out = mm_tn("cross_out_grad", g, later_low, mixed_two, n_t)
    g_cross_q = mm_tn("cross_q_grad", g, normed_two, cq_low, n_t)
    g_cross_kv = mm_tn("cross_kv_grad", g, memory, ckv_low, n_t)
    memory_part = mm_nt("memory_grad", g, ckv_low, w_cross, 2 * PAIR, 0)
    middle_grad, middle_low, sums_two = norm_back(
        "norm_two_back", part, flip(part, 0, n_f), middle, line(gains, 1), later_grad, True
    )
    (mixed_one_grad,) = mm_nn("mixed_one_grad", g, middle_low, w_mid, PAIR, 0)
    qkv_low, self_sums = attend_back("self_attention_back", qkv, None, mixed_one_grad, log_one, True, 1, length)
    part = mm_nt("normed_one_grad", g, qkv_low, w_qkv, 3 * PAIR, 0)
    g_self_out = mm_tn("self_out_grad", g, middle_low, mixed_one, n_t)
    g_qkv = mm_tn("qkv_grad", g, normed_one, qkv_low, n_t)
    start_grad, sums_one = norm_back(
        "norm_one_back", part, flip(part, 0, n_f), start, line(gains, 0), middle_grad, False
    )

    (reduce_t,) = unpack(scatter(g_reduce, 1), [units // 2])
    (hidden_share,) = unpack(scatter(g_hidden, 2), [units // 2])
    (cross_out_t,) = unpack(scatter(g_cross_out, 1), [PAIR])
    (cross_q_share,) = unpack(scatter(g_cross_q, 2), [PAIR])
    ck_share, cv_share = unpack(scatter(g_cross_kv, 1), [PAIR, PAIR])
    (self_out_t,) = unpack(scatter(g_self_out, 2), [PAIR])
    q_share, k_share, v_share = unpack(scatter(g_qkv, 2), [PAIR, PAIR, PAIR])

    lead = jnp.where(core == 0, 1.0, 0.0).astype(F32)
    feature_sums = jnp.stack(
        [sums_one[0], sums_two[0], sums_three[0], sums_one[1], sums_two[1], sums_three[1],
         sums_two[2], sums_three[2], sums_three[3]]
    ) * lead

    def from_slots(v):
        natural = jnp.stack(
            [lax.dynamic_index_in_dim(v, (z - at) % n_t, axis=0, keepdims=False) for at in range(n_t)], axis=1
        )
        wide = jnp.zeros((*natural.shape[:2], 2 * natural.shape[2]), F32)
        return lax.dynamic_update_slice(wide, natural, (0, 0, core * natural.shape[2]))

    unit_sums = [from_slots(hidden_sums[:, :1]), from_slots(self_sums[:, :2]), from_slots(cross_sums[:, :2])]
    packed = jnp.concatenate([feature_sums.reshape(-1)] + [u.reshape(-1) for u in unit_sums]).reshape(-1, 1024)
    for bit in range(bits):
        packed = packed + flip(packed, bit, n_f)
    for step in (1, 2):
        packed = packed + lax.ppermute(packed, "tensor", [(i, i ^ step) for i in range(n_t)])
    packed = packed.reshape(-1)
    feature_share = lax.dynamic_slice(packed[: 9 * d].reshape(9, d), (0, f * per), (9, per))

    def unit_share(at, rows, total):
        block = packed[at : at + rows * n_t * total].reshape(rows, n_t, total)
        return lax.dynamic_slice(block, (0, z, f * (total // n_f)), (rows, 1, total // n_f))

    at = 9 * d
    hidden_bias_share = unit_share(at, 1, units)[0]
    at += n_t * units
    self_bias_share = unit_share(at, 2, heads_wide)
    at += 2 * n_t * heads_wide
    cross_bias_share = unit_share(at, 2, heads_wide)

    def spread_clip(x):
        slots = [half(x, core, 0)]
        for _ in range(n_t - 1):
            slots.append(turn(slots[-1], 1, n_t))
        stacked = jnp.stack(slots)

        def clips(c):
            return jnp.stack(
                [
                    lax.dynamic_index_in_dim(stacked, (z - c * own_clips - i) % n_t, axis=0, keepdims=False)
                    for i in range(own_clips)
                ]
            )

        keep, came = clips(core), flip(clips(1 - core), 0, n_f)
        return jnp.where(core == 0, jnp.concatenate([keep, came], 1), jnp.concatenate([came, keep], 1))

    keep, send = half(memory_part, core, 1), half(memory_part, 1 - core, 1)
    summed = (keep.astype(F32) + flip(send, 0, n_f).astype(F32)).astype(BF16)
    summed = summed.reshape(n_t, part_pad, d // 2)
    slots = []
    for s in range(n_t):
        block = lax.dynamic_index_in_dim(summed, (z + s) % n_t, axis=0, keepdims=False)
        slots.append(turn(block, s, n_t) if s else block)
    stacked = jnp.stack(slots)

    def memory_clips(c):
        return jnp.stack(
            [
                lax.dynamic_index_in_dim(stacked, (z - c * own_clips - i) % n_t, axis=0, keepdims=False)
                for i in range(own_clips)
            ]
        )

    keep, came = memory_clips(core), flip(memory_clips(1 - core), 0, n_f)
    memory_share = jnp.where(core == 0, jnp.concatenate([keep, came], 2), jnp.concatenate([came, keep], 2))

    return (
        spread_clip(output),
        spread_clip(start_grad),
        memory_share[:, :part_frames],
        jnp.stack([q_share, k_share, v_share]),
        self_bias_share,
        self_out_t.T,
        cross_q_share,
        jnp.stack([ck_share, cv_share]),
        cross_bias_share,
        cross_out_t.T,
        hidden_share,
        hidden_bias_share,
        reduce_t.T,
        feature_share[0:3],
        feature_share[3:6],
        feature_share[6:9],
    )


def solution(mesh):
    n_f, n_t = mesh.shape["fsdp"], mesh.shape["tensor"]
    clips = P("fsdp", None, None)
    stacked = P(None, "fsdp", "tensor")
    biases = P(None, "tensor", "fsdp")
    up, down, rows = P("fsdp", "tensor"), P("tensor", "fsdp"), P(None, "fsdp")
    return jax.shard_map(
        functools.partial(on_device, n_f, n_t),
        mesh=mesh,
        in_specs=(
            clips, clips, clips, stacked, biases, down, up, stacked, biases, down, up, down, down, rows, rows, rows,
        ),
        out_specs=(
            clips, clips, P("fsdp", "tensor", None), stacked, biases, down, up, stacked, biases, down, up, down,
            down, rows, rows, rows,
        ),
        check_vma=False,
    )
```

time: 2050 us -> 783 us (0.38)
  waiting for transfers between devices: 1300 us -> 278 us
  blocking collectives: 289 us -> 0 us
  Pallas kernels: 0 us -> 227 us
  matrix products: 215 us -> 0 us
  starting transfers between devices: 7.86 us -> 140 us
  local copies, waits for them, and re-layouts: 108 us -> 61.3 us
  other arithmetic: 105 us -> 64.4 us
    reduce_scatter x14 -> x0, waiting for transfers between devices: 621 us -> none  [the longest x2 107 us: step(): lax.psum_scatter(grads[7], 'fsdp', scatter_dimension=0, tiled=True)]
    psum x10 -> x0, waiting for transfers between devices: 357 us -> none  [the longest x6 271 us: input_total(): lax.psum(partial_sum.astype(jnp.bfloat16), 'tensor').astype(jnp.float32)]
    ppermute x0 -> x116, waiting for transfers between devices: none -> 278 us  [the longest x67 130 us: flip(): return lax.ppermute(x, 'fsdp', [(i, i ^ 1 << bit) for i in range(size)])]
    pallas_call x0 -> x32, Pallas kernels: none -> 227 us  [call(): pl.pallas_call(kernel, name=name, out_shape=out_shape, grid_spec=pltpu.Pr...]
    while x58 -> x0, waiting for transfers between devices: 224 us -> none
    dot_general x84 -> x0, matrix products: 215 us -> none  [the longest x20 60.9 us: product(): return jnp.dot(left, right, preferred_element_type=jnp.float32)]
    all_gather x18 -> x0, blocking collectives: 172 us -> none  [the longest x2 22.9 us: fetch(): lax.all_gather(self_output, 'fsdp', axis=1, tiled=True)]
    ppermute x0 -> x116, starting transfers between devices: none -> 140 us  [the longest x45 80 us: turn(): lax.ppermute(x, 'tensor', [(i, (i + step) % size) for i in range(size)])]
  transfers between devices with their start and end apart: 46 -> 116, of which waited for: 36 -> 57; matrix products, arithmetic and copies ran while one was open for 19% -> 15% of each run, Pallas kernels for 0% -> 28%
where the time goes in v1:
time: 783 us; the launch traced here: 773 us
  waiting for transfers between devices  278 us (36%)
  Pallas kernels  227 us (29%)
  starting transfers between devices  140 us (18%)
  other arithmetic  64.4 us (8%)
  local copies, waits for them, and re-layouts  61.3 us (8%)
    pallas_call x32, Pallas kernels, call(): pl.pallas_call(kernel, name=name, out_shape=out_shape, grid_spec=pltpu.Pr...  227 us
    ppermute x67, waiting for transfers between devices, flip(): return lax.ppermute(x, 'fsdp', [(i, i ^ 1 << bit) for i in range(size)])  130 us
    ppermute x45, waiting for transfers between devices, turn(): lax.ppermute(x, 'tensor', [(i, (i + step) % size) for i in range(size)])  129 us
    ppermute x45, starting transfers between devices, turn(): lax.ppermute(x, 'tensor', [(i, (i + step) % size) for i in range(size)])  80 us
    ppermute x67, starting transfers between devices, flip(): return lax.ppermute(x, 'fsdp', [(i, i ^ 1 << bit) for i in range(size)])  51.7 us
    ppermute x4, waiting for transfers between devices, on_device(): lax.ppermute(packed, 'tensor', [(i, i ^ step) for i in range(n_t)])  19.4 us
    convert_element_type x21, other arithmetic, slot_sum(): return (a.astype(F32) + b.astype(F32)).astype(BF16)  16.7 us
    unnamed x153, local copies, waits for them, and re-layouts  16 us
  transfers between devices with their start and end apart: 116, of which 57 were waited for; matrix products, arithmetic and copies ran while one was open for 15% of the time, Pallas kernels for 28%

profile of v1, /device:TPU:0, one launch (start us, length us, event | category | flops | bytes accessed | tf_op | source)
XLA Modules:
  0.0 772.9 jit_solution(2021627241588593827)
XLA Ops:
  8.5 7.6 constant_dynamic-slice_fusion.49
  40.1 8.5 %collective-permute-done.4 = bf16[17,1024]{1,0:T(8,128)(2,1)S(1)} collective-permute-done((bf16[17,1024]{1,0:T(8,128)(2,1)S(1)}, bf16[17,1024]{1,0:T(8,128)(2,1)S(1)}, u32[]{:S(2)}, u32[]{:S(2)}) %collective-permute-start.4) | collective-permute-done | bytes 34848 | tf_op jit(solution)/shard_map/ppermute | solution.py:485
  58.8 14.4 %collective-permute-done.15 = bf16[256,256]{1,0:T(8,128)(2,1)} collective-permute-done((bf16[256,256]{1,0:T(8,128)(2,1)S(1)}, bf16[256,256]{1,0:T(8,128)(2,1)}, u32[]{:S(2)}, u32[]{:S(2)}) %collective-permute-start.15) | collective-permute-done | bytes 131104 | tf_op jit(solution)/shard_map/ppermute | solution.py:437
  76.7 4.9 collective-permute-done.16
  81.6 9.8 %collective-permute-done.9 = bf16[256,384]{1,0:T(8,128)(2,1)S(1)} collective-permute-done((bf16[256,384]{1,0:T(8,128)(2,1)S(1)}, bf16[256,384]{1,0:T(8,128)(2,1)S(1)}, u32[]{:S(2)}, u32[]{:S(2)}) %collective-permute-start.9) | collective-permute-done | bytes 196640 | tf_op jit(solution)/shard_map/ppermute | solution.py:437
  119.6 5.1 collective-permute-done.17.refs_2_
  132.2 11.8 %collective-permute-done.11.refs_3_ = bf16[4,256,384]{2,1,0:T(8,128)(2,1)S(1)} collective-permute-done((bf16[4,256,384]{2,1,0:T(8,128)(2,1)S(1)}, bf16[4,256,384]{2,1,0:T(8,128)(2,1)S(1)}, u32[]{:S(2)}, u32[]{:S(2)}) %collective-permute-start.11) | collective-permute-done | bytes 786464 | tf_op jit(solution)/shard_map/ppermute | solution.py:433
  148.0 12.9 %collective-permute-done.12.refs_4_ = bf16[4,256,384]{2,1,0:T(8,128)(2,1)S(1)} collective-permute-done((bf16[4,256,384]{2,1,0:T(8,128)(2,1)S(1)}, bf16[4,256,384]{2,1,0:T(8,128)(2,1)S(1)}, u32[]{:S(2)}, u32[]{:S(2)}) %collective-permute-start.12) | collective-permute-done | bytes 786464 | tf_op jit(solution)/shard_map/ppermute | solution.py:433
  170.2 6.0 qkv.1.refs_0_
  176.2 7.7 self_attention.1
  184.8 4.7 self_out.1.refs_1_
  205.7 7.7 %cross_kv.1.refs_1_ = bf16[1536,1024]{1,0:T(8,128)(2,1)} custom-call(s32[1]{0:T(128)} %bitcast.1.g_ref, bf16[1536,1024]{1,0:T(8,128)(2,1)} %bitcast.277, bf16[4,256,384]{2,1,0:T(8,128)(2,1)} %copy-done.5, bf16[4,256,384]{2,1,0:T(8,128)(2,1)} %copy-done.10, bf16[4,256,384]{2,1,0:T(8,128)(2,1)} %collective-permute-done.27.refs_3_, ...), custom_call_target="tpu_custom_call" | custom-call | flops 3221225472 | bytes 9441284 | tf_op jit(solution)/shard_map/cross_kv/pallas_call | solution.py:32
  217.7 4.6 cross_q.1.refs_0_
  222.3 13.0 %cross_attention.1 = (bf16[448,512]{1,0:T(8,128)(2,1)}, f32[8,8,448]{2,1,0:T(8,128)}) custom-call(bf16[448,512]{1,0:T(8,128)(2,1)} %cross_q.1.refs_0_, bf16[1536,1024]{1,0:T(8,128)(2,1)} %cross_kv.1.refs_1_), custom_call_target="tpu_custom_call" | custom-call | flops 1409286144 | bytes 4177920 | tf_op jit(solution)/shard_map/cross_attention/pallas_call | solution.py:32
  235.3 4.8 cross_out.1.refs_1_
  249.1 11.2 %collective-permute-done.36.refs_4_ = bf16[4,256,512]{2,1,0:T(8,128)(2,1)} collective-permute-done((bf16[4,256,512]{2,1,0:T(8,128)(2,1)}, bf16[4,256,512]{2,1,0:T(8,128)(2,1)}, u32[]{:S(2)}, u32[]{:S(2)}) %collective-permute-start.36) | collective-permute-done | bytes 1048608 | tf_op jit(solution)/shard_map/ppermute | solution.py:433
  260.3 7.6 hidden.1
  268.0 20.5 %collective-permute-done.43.refs_4_ = bf16[4,256,512]{2,1,0:T(8,128)(2,1)} collective-permute-done((bf16[4,256,512]{2,1,0:T(8,128)(2,1)}, bf16[4,256,512]{2,1,0:T(8,128)(2,1)}, u32[]{:S(2)}, u32[]{:S(2)}) %collective-permute-start.43) | collective-permute-done | bytes 1048608 | tf_op jit(solution)/shard_map/ppermute | solution.py:433
  288.5 6.9 expanded_grad.1
  295.4 6.4 normed_three_grad.1.own
  301.8 6.6 reduce.1.refs_1_
  309.8 6.2 hidden_grad.1
  318.0 6.1 reduce_grad.1
  326.2 5.5 norm_three_back.1
  331.7 4.5 mixed_two_grad.1.refs_2_
  336.2 34.8 %cross_attention_back.1 = (bf16[448,512]{1,0:T(8,128)(2,1)}, bf16[1536,1024]{1,0:T(8,128)(2,1)}, f32[4,8,128]{2,1,0:T(8,128)}) custom-call(bf16[448,512]{1,0:T(8,128)(2,1)} %cross_q.1.refs_0_, bf16[1536,1024]{1,0:T(8,128)(2,1)} %cross_kv.1.refs_1_, bf16[448,512]{1,0:T(8,128)(2,1)} %mixed_two_grad.1.refs_2_, f32[8,8,448]{2,1,0:T(8,128)} %get-tuple-element.79.refs_3_), custom_call_target="tpu_custom_call" | custom-call | flops 3523215360 | bytes 7798784 | tf_op jit(solution)/shard_map/cross_attention_back/pallas_call | solution.py:32
  371.8 4.5 cross_q_grad.1
  376.3 4.7 normed_two_grad.1.own
  388.4 7.6 cross_kv_grad.1
  396.0 9.5 %memory_grad.1 = bf16[1536,1024]{1,0:T(8,128)(2,1)} custom-call(s32[1]{0:T(128)} %bitcast.1.g_ref, bf16[1536,1024]{1,0:T(8,128)(2,1)} %get-tuple-element.87.refs_0_.y_ref, bf16[4,256,384]{2,1,0:T(8,128)(2,1)} %copy-done.5, bf16[4,256,384]{2,1,0:T(8,128)(2,1)} %copy-done.10, bf16[4,256,384]{2,1,0:T(8,128)(2,1)} %collective-permute-done.27.refs_3_, ...), custom_call_target="tpu_custom_call" | custom-call | flops 3221225472 | bytes 9437188 | tf_op jit(solution)/shard_map/memory_grad/pallas_call | solution.py:32
  408.3 4.7 cross_out_grad.1
  446.3 8.1 %collective-permute-done.88 = bf16[4,256,256]{2,1,0:T(8,128)(2,1)S(1)} collective-permute-done((bf16[4,256,256]{2,1,0:T(8,128)(2,1)S(1)}, bf16[4,256,256]{2,1,0:T(8,128)(2,1)S(1)}, u32[]{:S(2)}, u32[]{:S(2)}) %collective-permute-start.88) | collective-permute-done | bytes 524320 | tf_op jit(solution)/shard_map/ppermute | solution.py:433
  454.7 7.8 %collective-permute-done.97 = bf16[4,256,128]{2,1,0:T(8,128)(2,1)S(1)} collective-permute-done((bf16[4,256,128]{2,1,0:T(8,128)(2,1)S(1)}, bf16[4,256,128]{2,1,0:T(8,128)(2,1)S(1)}, u32[]{:S(2)}, u32[]{:S(2)}) %collective-permute-start.97) | collective-permute-done | bytes 262176 | tf_op jit(solution)/shard_map/ppermute | solution.py:433
  462.5 18.0 %collective-permute-done.83 = bf16[4,256,128]{2,1,0:T(8,128)(2,1)S(1)} collective-permute-done((bf16[4,256,128]{2,1,0:T(8,128)(2,1)S(1)}, bf16[4,256,128]{2,1,0:T(8,128)(2,1)S(1)}, u32[]{:S(2)}, u32[]{:S(2)}) %collective-permute-start.83) | collective-permute-done | bytes 262176 | tf_op jit(solution)/shard_map/ppermute | solution.py:433
  520.4 5.6 norm_two_back.1
  526.0 4.6 mixed_one_grad.1.refs_1_
  530.6 14.1 %self_attention_back.1 = (bf16[448,1536]{1,0:T(8,128)(2,1)}, f32[4,8,128]{2,1,0:T(8,128)}) custom-call(bf16[448,1536]{1,0:T(8,128)(2,1)} %qkv.1.refs_0_, bf16[448,512]{1,0:T(8,128)(2,1)} %mixed_one_grad.1.refs_1_, f32[8,8,448]{2,1,0:T(8,128)} %get-tuple-element.83.refs_2_), custom_call_target="tpu_custom_call" | custom-call | flops 1027604480 | bytes 3342336 | tf_op jit(solution)/shard_map/self_attention_back/pallas_call | solution.py:32
  545.4 4.6 self_out_grad.1
  551.3 5.8 qkv_grad.1
  557.2 6.2 normed_one_grad.1.own
  572.3 6.0 collective-permute-done.74
  578.3 9.4 %collective-permute-done.46 = bf16[224,1024]{1,0:T(8,128)(2,1)S(1)} collective-permute-done((bf16[224,1024]{1,0:T(8,128)(2,1)}, bf16[224,1024]{1,0:T(8,128)(2,1)S(1)}, u32[]{:S(2)}, u32[]{:S(2)}) %collective-permute-start.46) | collective-permute-done | bytes 458784 | tf_op jit(solution)/shard_map/ppermute | solution.py:437
  595.1 10.0 %collective-permute-done.92 = bf16[256,256]{1,0:T(8,128)(2,1)S(1)} collective-permute-done((bf16[256,256]{1,0:T(8,128)(2,1)S(1)}, bf16[256,256]{1,0:T(8,128)(2,1)S(1)}, u32[]{:S(2)}, u32[]{:S(2)}) %collective-permute-start.92) | collective-permute-done | bytes 131104 | tf_op jit(solution)/shard_map/ppermute | solution.py:437
  614.0 6.2 collective-permute-done.105
  668.7 5.1 norm_one_back.1
  680.2 7.4 collective-permute-done.59
  691.5 10.9 %collective-permute-done.107 = bf16[256,512]{1,0:T(8,128)(2,1)S(1)} collective-permute-done((bf16[256,512]{1,0:T(8,128)(2,1)S(1)}, bf16[256,512]{1,0:T(8,128)(2,1)S(1)}, u32[]{:S(2)}, u32[]{:S(2)}) %collective-permute-start.107) | collective-permute-done | bytes 262176 | tf_op jit(solution)/shard_map/ppermute | solution.py:437
  758.3 4.5 collective-permute-done.67
  (560 shorter events, 364.9 us)
Async XLA Ops:
  4.0 20.6 %collective-permute-start.1 = (bf16[17,1024]{1,0:T(8,128)(2,1)S(1)}, bf16[17,1024]{1,0:T(8,128)(2,1)S(1)}, u32[]{:S(2)}, u32[]{:S(2)}) collective-permute-start(bf16[17,1024]{1,0:T(8,128)(2,1)S(1)} %reshape.884), channel_id=1, source_target_pairs={{0,4},{4,0},{8,12},{12,8},{16,20},{20,16},{24,28},{28,24},{1,5},{5... | collective-permute-start | bytes 104456 | tf_op jit(solution)/shard_map/ppermute | solution.py:433
  6.1 23.7 %collective-permute-start.6 = (bf16[128,384]{1,0:T(8,128)(2,1)S(1)}, bf16[128,384]{1,0:T(8,128)(2,1)S(1)}, u32[]{:S(2)}, u32[]{:S(2)}) collective-permute-start(bf16[128,384]{1,0:T(8,128)(2,1)S(1)} %pad_maximum_fusion.17), channel_id=1, source_target_pairs={{0,4},{4,0},{8,12},{12,8},{16,20},{20,16},{24,28},{28,24},{1,5},{5... | collective-permute-start | bytes 294920 | tf_op jit(solution)/shard_map/ppermute | solution.py:433
  19.8 171.2 %collective-permute-start.21 = (bf16[1500,1024]{1,0:T(8,128)(2,1)}, bf16[1500,1024]{1,0:T(8,128)(2,1)}, u32[]{:S(2)}, u32[]{:S(2)}) collective-permute-start(bf16[1500,1024]{1,0:T(8,128)(2,1)} %bitcast.273), channel_id=1, source_target_pairs={{0,4},{4,0},{8,12},{12,8},{16,20},{20,16},{24,28},{28,24},{1,5},{5... | collective-permute-start | bytes 9216008 | tf_op jit(solution)/shard_map/ppermute | solution.py:433
  29.8 24.0 %collective-permute-start.14 = (bf16[256,256]{1,0:T(8,128)(2,1)S(1)}, bf16[256,256]{1,0:T(8,128)(2,1)S(1)}, u32[]{:S(2)}, u32[]{:S(2)}) collective-permute-start(bf16[256,256]{1,0:T(8,128)(2,1)S(1)} %maximum_select_fusion.13), channel_id=1, source_target_pairs={{0,1},{1,2},{2,3},{3,0},{4,5},{5,6},{6,7},{7,4},{8,9},{9,10},{10,1... | collective-permute-start | bytes 393224 | tf_op jit(solution)/shard_map/ppermute | solution.py:437
  55.7 20.9 %collective-permute-start.8 = (bf16[256,384]{1,0:T(8,128)(2,1)S(1)}, bf16[256,384]{1,0:T(8,128)(2,1)S(1)}, u32[]{:S(2)}, u32[]{:S(2)}) collective-permute-start(bf16[256,384]{1,0:T(8,128)(2,1)S(1)} %collective-permute-done.7), channel_id=1, source_target_pairs={{0,1},{1,2},{2,3},{3,0},{4,5},{5,6},{6,7},{7,4},{8,9},{9,10},{10,1... | collective-permute-start | bytes 589832 | tf_op jit(solution)/shard_map/ppermute | solution.py:437
  73.3 34.8 %collective-permute-start = (bf16[448,1024]{1,0:T(8,128)(2,1)}, bf16[448,1024]{1,0:T(8,128)(2,1)S(1)}, u32[]{:S(2)}, u32[]{:S(2)}) collective-permute-start(bf16[448,1024]{1,0:T(8,128)(2,1)} %dynamic-slice_bitcast_fusion.1), channel_id=1, source_target_pairs={{0,4},{4,0},{8,12},{12,8},{16,20},{20,16},{24,28},{28,24},{1,5},{5... | collective-permute-start | bytes 2752520 | tf_op jit(solution)/shard_map/ppermute | solution.py:433
  73.4 21.8 %collective-permute-start.39 = (bf16[256,512]{1,0:T(8,128)(2,1)S(1)}, bf16[256,512]{1,0:T(8,128)(2,1)}, u32[]{:S(2)}, u32[]{:S(2)}) collective-permute-start(bf16[256,512]{1,0:T(8,128)(2,1)S(1)} %collective-permute-done.38), channel_id=1, source_target_pairs={{0,1},{1,2},{2,3},{3,0},{4,5},{5,6},{6,7},{7,4},{8,9},{9,10},{10,1... | collective-permute-start | bytes 786440 | tf_op jit(solution)/shard_map/ppermute | solution.py:437
  95.8 20.9 %collective-permute-start.10 = (bf16[4,256,384]{2,1,0:T(8,128)(2,1)S(1)}, bf16[4,256,384]{2,1,0:T(8,128)(2,1)S(1)}, u32[]{:S(2)}, u32[]{:S(2)}) collective-permute-start(bf16[4,256,384]{2,1,0:T(8,128)(2,1)S(1)} %pad_maximum_fusion.11.refs_1_), channel_id=1, source_target_pairs={{0,8},{4,12},{8,0},{12,4},{16,24},{20,28},{24,16},{28,20},{1,9},{5... | collective-permute-start | bytes 2359304 | tf_op jit(solution)/shard_map/ppermute | solution.py:433
  115.2 28.8 %collective-permute-start.11 = (bf16[4,256,384]{2,1,0:T(8,128)(2,1)S(1)}, bf16[4,256,384]{2,1,0:T(8,128)(2,1)S(1)}, u32[]{:S(2)}, u32[]{:S(2)}) collective-permute-start(bf16[4,256,384]{2,1,0:T(8,128)(2,1)S(1)} %pad_maximum_fusion.11.refs_1_), channel_id=1, source_target_pairs={{0,16},{4,20},{8,24},{12,28},{16,0},{20,4},{24,8},{28,12},{1,17},{... | collective-permute-start | bytes 2359304 | tf_op jit(solution)/shard_map/ppermute | solution.py:433
  116.7 44.2 %collective-permute-start.12 = (bf16[4,256,384]{2,1,0:T(8,128)(2,1)S(1)}, bf16[4,256,384]{2,1,0:T(8,128)(2,1)S(1)}, u32[]{:S(2)}, u32[]{:S(2)}) collective-permute-start(bf16[4,256,384]{2,1,0:T(8,128)(2,1)S(1)} %collective-permute-done.10.refs_2_), channel_id=1, source_target_pairs={{0,16},{4,20},{8,24},{12,28},{16,0},{20,4},{24,8},{28,12},{1,17},{... | collective-permute-start | bytes 2359304 | tf_op jit(solution)/shard_map/ppermute | solution.py:433
  124.8 64.7 %collective-permute-start.26 = (bf16[4,256,384]{2,1,0:T(8,128)(2,1)S(1)}, bf16[4,256,384]{2,1,0:T(8,128)(2,1)S(1)}, u32[]{:S(2)}, u32[]{:S(2)}) collective-permute-start(bf16[4,256,384]{2,1,0:T(8,128)(2,1)S(1)} %pad_maximum_fusion.12.refs_1_), channel_id=1, source_target_pairs={{0,8},{4,12},{8,0},{12,4},{16,24},{20,28},{24,16},{28,20},{1,9},{5... | collective-permute-start | bytes 2359304 | tf_op jit(solution)/shard_map/ppermute | solution.py:433
  127.2 56.7 %collective-permute-start.27 = (bf16[4,256,384]{2,1,0:T(8,128)(2,1)S(1)}, bf16[4,256,384]{2,1,0:T(8,128)(2,1)}, u32[]{:S(2)}, u32[]{:S(2)}) collective-permute-start(bf16[4,256,384]{2,1,0:T(8,128)(2,1)S(1)} %pad_maximum_fusion.12.refs_1_), channel_id=1, source_target_pairs={{0,16},{4,20},{8,24},{12,28},{16,0},{20,4},{24,8},{28,12},{1,17},{... | collective-permute-start | bytes 2359304 | tf_op jit(solution)/shard_map/ppermute | solution.py:433
  144.9 39.0 %collective-permute-start.19 = (bf16[4,256,256]{2,1,0:T(8,128)(2,1)S(1)}, bf16[4,256,256]{2,1,0:T(8,128)(2,1)S(1)}, u32[]{:S(2)}, u32[]{:S(2)}) collective-permute-start(bf16[4,256,256]{2,1,0:T(8,128)(2,1)S(1)} %collective-permute-done.18.refs_3_), channel_id=1, source_target_pairs={{0,8},{4,12},{8,0},{12,4},{16,24},{20,28},{24,16},{28,20},{1,9},{5... | collective-permute-start | bytes 1572872 | tf_op jit(solution)/shard_map/ppermute | solution.py:433
  161.8 39.8 %collective-permute-start.34 = (bf16[4,256,512]{2,1,0:T(8,128)(2,1)}, bf16[4,256,512]{2,1,0:T(8,128)(2,1)}, u32[]{:S(2)}, u32[]{:S(2)}) collective-permute-start(bf16[4,256,512]{2,1,0:T(8,128)(2,1)} %pad_maximum_fusion.7.refs_1_), channel_id=1, source_target_pairs={{0,8},{4,12},{8,0},{12,4},{16,24},{20,28},{24,16},{28,20},{1,9},{5... | collective-permute-start | bytes 3145736 | tf_op jit(solution)/shard_map/ppermute | solution.py:433
  183.9 56.2 %collective-permute-start.49 = (bf16[448,1024]{1,0:T(8,128)(2,1)}, bf16[448,1024]{1,0:T(8,128)(2,1)}, u32[]{:S(2)}, u32[]{:S(2)}) collective-permute-start(bf16[448,1024]{1,0:T(8,128)(2,1)} %dynamic-slice_bitcast_fusion), channel_id=1, source_target_pairs={{0,4},{4,0},{8,12},{12,8},{16,20},{20,16},{24,28},{28,24},{1,5},{5... | collective-permute-start | bytes 2752520 | tf_op jit(solution)/shard_map/ppermute | solution.py:433
  189.5 51.0 %collective-permute-start.42 = (bf16[4,256,512]{2,1,0:T(8,128)(2,1)}, bf16[4,256,512]{2,1,0:T(8,128)(2,1)}, u32[]{:S(2)}, u32[]{:S(2)}) collective-permute-start(bf16[4,256,512]{2,1,0:T(8,128)(2,1)} %pad_maximum_fusion.8.refs_1_), channel_id=1, source_target_pairs={{0,16},{4,20},{8,24},{12,28},{16,0},{20,4},{24,8},{28,12},{1,17},{... | collective-permute-start | bytes 3145736 | tf_op jit(solution)/shard_map/ppermute | solution.py:433
  191.0 22.4 %collective-permute-start.20 = (bf16[448,1024]{1,0:T(8,128)(2,1)}, bf16[448,1024]{1,0:T(8,128)(2,1)}, u32[]{:S(2)}, u32[]{:S(2)}) collective-permute-start(bf16[448,1024]{1,0:T(8,128)(2,1)} %self_out.1.refs_1_), channel_id=1, source_target_pairs={{0,4},{4,0},{8,12},{12,8},{16,20},{20,16},{24,28},{28,24},{1,5},{5... | collective-permute-start | bytes 2752520 | tf_op jit(solution)/shard_map/ppermute | solution.py:433
  201.6 47.5 %collective-permute-start.35 = (bf16[4,256,512]{2,1,0:T(8,128)(2,1)}, bf16[4,256,512]{2,1,0:T(8,128)(2,1)}, u32[]{:S(2)}, u32[]{:S(2)}) collective-permute-start(bf16[4,256,512]{2,1,0:T(8,128)(2,1)} %pad_maximum_fusion.7.refs_1_), channel_id=1, source_target_pairs={{0,16},{4,20},{8,24},{12,28},{16,0},{20,4},{24,8},{28,12},{1,17},{... | collective-permute-start | bytes 3145736 | tf_op jit(solution)/shard_map/ppermute | solution.py:433
  204.2 56.1 %collective-permute-start.36 = (bf16[4,256,512]{2,1,0:T(8,128)(2,1)}, bf16[4,256,512]{2,1,0:T(8,128)(2,1)}, u32[]{:S(2)}, u32[]{:S(2)}) collective-permute-start(bf16[4,256,512]{2,1,0:T(8,128)(2,1)} %collective-permute-done.34.refs_2_), channel_id=1, source_target_pairs={{0,16},{4,20},{8,24},{12,28},{16,0},{20,4},{24,8},{28,12},{1,17},{... | collective-permute-start | bytes 3145736 | tf_op jit(solution)/shard_map/ppermute | solution.py:433
  240.1 27.8 %collective-permute-start.41 = (bf16[4,256,512]{2,1,0:T(8,128)(2,1)}, bf16[4,256,512]{2,1,0:T(8,128)(2,1)S(1)}, u32[]{:S(2)}, u32[]{:S(2)}) collective-permute-start(bf16[4,256,512]{2,1,0:T(8,128)(2,1)} %pad_maximum_fusion.8.refs_1_), channel_id=1, source_target_pairs={{0,8},{4,12},{8,0},{12,4},{16,24},{20,28},{24,16},{28,20},{1,9},{5... | collective-permute-start | bytes 3145736 | tf_op jit(solution)/shard_map/ppermute | solution.py:433
  240.5 48.0 %collective-permute-start.43 = (bf16[4,256,512]{2,1,0:T(8,128)(2,1)}, bf16[4,256,512]{2,1,0:T(8,128)(2,1)}, u32[]{:S(2)}, u32[]{:S(2)}) collective-permute-start(bf16[4,256,512]{2,1,0:T(8,128)(2,1)} %collective-permute-done.42.refs_3_), channel_id=1, source_target_pairs={{0,8},{4,12},{8,0},{12,4},{16,24},{20,28},{24,16},{28,20},{1,9},{5... | collective-permute-start | bytes 3145736 | tf_op jit(solution)/shard_map/ppermute | solution.py:433
  301.8 22.8 %collective-permute-start.50 = (bf16[448,1024]{1,0:T(8,128)(2,1)}, bf16[448,1024]{1,0:T(8,128)(2,1)S(1)}, u32[]{:S(2)}, u32[]{:S(2)}) collective-permute-start(bf16[448,1024]{1,0:T(8,128)(2,1)} %normed_three_grad.1.own), channel_id=1, source_target_pairs={{0,4},{4,0},{8,12},{12,8},{16,20},{20,16},{24,28},{28,24},{1,5},{5... | collective-permute-start | bytes 2752520 | tf_op jit(solution)/shard_map/ppermute | solution.py:433
  308.4 73.3 %collective-permute-start.44 = (bf16[448,1024]{1,0:T(8,128)(2,1)}, bf16[448,1024]{1,0:T(8,128)(2,1)S(1)}, u32[]{:S(2)}, u32[]{:S(2)}) collective-permute-start(bf16[448,1024]{1,0:T(8,128)(2,1)} %reduce.1.refs_1_), channel_id=1, source_target_pairs={{0,4},{4,0},{8,12},{12,8},{16,20},{20,16},{24,28},{28,24},{1,5},{5... | collective-permute-start | bytes 2752520 | tf_op jit(solution)/shard_map/ppermute | solution.py:433
  316.0 97.9 %collective-permute-start.103 = (bf16[4,256,512]{2,1,0:T(8,128)(2,1)}, bf16[4,256,512]{2,1,0:T(8,128)(2,1)}, u32[]{:S(2)}, u32[]{:S(2)}) collective-permute-start(bf16[4,256,512]{2,1,0:T(8,128)(2,1)} %get-tuple-element.117), channel_id=1, source_target_pairs={{0,8},{4,12},{8,0},{12,4},{16,24},{20,28},{24,16},{28,20},{1,9},{5... | collective-permute-start | bytes 3145736 | tf_op jit(solution)/shard_map/ppermute | solution.py:433
  316.3 100.2 %collective-permute-start.102 = (bf16[4,256,512]{2,1,0:T(8,128)(2,1)}, bf16[4,256,512]{2,1,0:T(8,128)(2,1)}, u32[]{:S(2)}, u32[]{:S(2)}) collective-permute-start(bf16[4,256,512]{2,1,0:T(8,128)(2,1)} %get-tuple-element.115), channel_id=1, source_target_pairs={{0,8},{4,12},{8,0},{12,4},{16,24},{20,28},{24,16},{28,20},{1,9},{5... | collective-permute-start | bytes 3145736 | tf_op jit(solution)/shard_map/ppermute | solution.py:433
  324.1 94.9 %collective-permute-start.110 = (bf16[4,256,512]{2,1,0:T(8,128)(2,1)}, bf16[4,256,512]{2,1,0:T(8,128)(2,1)}, u32[]{:S(2)}, u32[]{:S(2)}) collective-permute-start(bf16[4,256,512]{2,1,0:T(8,128)(2,1)} %get-tuple-element.121), channel_id=1, source_target_pairs={{0,16},{4,20},{8,24},{12,28},{16,0},{20,4},{24,8},{28,12},{1,17},{... | collective-permute-start | bytes 3145736 | tf_op jit(solution)/shard_map/ppermute | solution.py:433
  324.7 97.6 %collective-permute-start.109 = (bf16[4,256,512]{2,1,0:T(8,128)(2,1)}, bf16[4,256,512]{2,1,0:T(8,128)(2,1)S(1)}, u32[]{:S(2)}, u32[]{:S(2)}) collective-permute-start(bf16[4,256,512]{2,1,0:T(8,128)(2,1)} %get-tuple-element.119), channel_id=1, source_target_pairs={{0,16},{4,20},{8,24},{12,28},{16,0},{20,4},{24,8},{28,12},{1,17},{... | collective-permute-start | bytes 3145736 | tf_op jit(solution)/shard_map/ppermute | solution.py:433
  381.6 138.8 %collective-permute-start.51 = (bf16[448,1024]{1,0:T(8,128)(2,1)}, bf16[448,1024]{1,0:T(8,128)(2,1)}, u32[]{:S(2)}, u32[]{:S(2)}) collective-permute-start(bf16[448,1024]{1,0:T(8,128)(2,1)} %normed_two_grad.1.own), channel_id=1, source_target_pairs={{0,4},{4,0},{8,12},{12,8},{16,20},{20,16},{24,28},{28,24},{1,5},{5... | collective-permute-start | bytes 2752520 | tf_op jit(solution)/shard_map/ppermute | solution.py:433
  413.9 157.9 %collective-permute-start.45 = (bf16[224,1024]{1,0:T(8,128)(2,1)}, bf16[224,1024]{1,0:T(8,128)(2,1)}, u32[]{:S(2)}, u32[]{:S(2)}) collective-permute-start(bf16[224,1024]{1,0:T(8,128)(2,1)} %constant_dynamic-slice_fusion.42), channel_id=1, source_target_pairs={{0,1},{1,2},{2,3},{3,0},{4,5},{5,6},{6,7},{7,4},{8,9},{9,10},{10,1... | collective-permute-start | bytes 1376264 | tf_op jit(solution)/shard_map/ppermute | solution.py:437
  416.5 27.8 %collective-permute-start.89 = (bf16[4,256,256]{2,1,0:T(8,128)(2,1)S(1)}, bf16[4,256,256]{2,1,0:T(8,128)(2,1)S(1)}, u32[]{:S(2)}, u32[]{:S(2)}) collective-permute-start(bf16[4,256,256]{2,1,0:T(8,128)(2,1)S(1)} %copy-done.62), channel_id=1, source_target_pairs={{0,16},{4,20},{8,24},{12,28},{16,0},{20,4},{24,8},{28,12},{1,17},{... | collective-permute-start | bytes 1572872 | tf_op jit(solution)/shard_map/ppermute | solution.py:433
  443.1 146.0 %collective-permute-start.104 = (bf16[4,256,512]{2,1,0:T(8,128)(2,1)}, bf16[4,256,512]{2,1,0:T(8,128)(2,1)}, u32[]{:S(2)}, u32[]{:S(2)}) collective-permute-start(bf16[4,256,512]{2,1,0:T(8,128)(2,1)} %add_convert_fusion.3), channel_id=1, source_target_pairs={{0,16},{4,20},{8,24},{12,28},{16,0},{20,4},{24,8},{28,12},{1,17},{... | collective-permute-start | bytes 3145736 | tf_op jit(solution)/shard_map/ppermute | solution.py:433
  444.3 36.2 %collective-permute-start.83 = (bf16[4,256,128]{2,1,0:T(8,128)(2,1)S(1)}, bf16[4,256,128]{2,1,0:T(8,128)(2,1)S(1)}, u32[]{:S(2)}, u32[]{:S(2)}) collective-permute-start(bf16[4,256,128]{2,1,0:T(8,128)(2,1)S(1)} %add_convert_fusion.19), channel_id=1, source_target_pairs={{0,16},{4,20},{8,24},{12,28},{16,0},{20,4},{24,8},{28,12},{1,17},{... | collective-permute-start | bytes 786440 | tf_op jit(solution)/shard_map/ppermute | solution.py:433
  462.4 127.8 %collective-permute-start.111 = (bf16[4,256,512]{2,1,0:T(8,128)(2,1)}, bf16[4,256,512]{2,1,0:T(8,128)(2,1)}, u32[]{:S(2)}, u32[]{:S(2)}) collective-permute-start(bf16[4,256,512]{2,1,0:T(8,128)(2,1)} %add_convert_fusion.1), channel_id=1, source_target_pairs={{0,8},{4,12},{8,0},{12,4},{16,24},{20,28},{24,16},{28,20},{1,9},{5... | collective-permute-start | bytes 3145736 | tf_op jit(solution)/shard_map/ppermute | solution.py:433
  519.1 45.2 %collective-permute-start.90 = (bf16[4,256,256]{2,1,0:T(8,128)(2,1)}, bf16[4,256,256]{2,1,0:T(8,128)(2,1)S(1)}, u32[]{:S(2)}, u32[]{:S(2)}) collective-permute-start(bf16[4,256,256]{2,1,0:T(8,128)(2,1)} %add_convert_fusion.7), channel_id=1, source_target_pairs={{0,8},{4,12},{8,0},{12,4},{16,24},{20,28},{24,16},{28,20},{1,9},{5... | collective-permute-start | bytes 1572872 | tf_op jit(solution)/shard_map/ppermute | solution.py:433
  549.9 21.9 %collective-permute-start.75 = (bf16[4,256,128]{2,1,0:T(8,128)(2,1)}, bf16[4,256,128]{2,1,0:T(8,128)(2,1)S(1)}, u32[]{:S(2)}, u32[]{:S(2)}) collective-permute-start(bf16[4,256,128]{2,1,0:T(8,128)(2,1)} %get-tuple-element.101), channel_id=1, source_target_pairs={{0,8},{4,12},{8,0},{12,4},{16,24},{20,28},{24,16},{28,20},{1,9},{5... | collective-permute-start | bytes 786440 | tf_op jit(solution)/shard_map/ppermute | solution.py:433
  571.7 68.7 %collective-permute-start.57 = (bf16[1536,512]{1,0:T(8,128)(2,1)}, bf16[1536,512]{1,0:T(8,128)(2,1)S(1)}, u32[]{:S(2)}, u32[]{:S(2)}) collective-permute-start(bf16[1536,512]{1,0:T(8,128)(2,1)} %constant_dynamic-slice_fusion.32), channel_id=1, source_target_pairs={{0,4},{4,0},{8,12},{12,8},{16,20},{20,16},{24,28},{28,24},{1,5},{5... | collective-permute-start | bytes 4718600 | tf_op jit(solution)/shard_map/ppermute | solution.py:433
  578.2 90.4 %collective-permute-start.52 = (bf16[448,1024]{1,0:T(8,128)(2,1)}, bf16[448,1024]{1,0:T(8,128)(2,1)}, u32[]{:S(2)}, u32[]{:S(2)}) collective-permute-start(bf16[448,1024]{1,0:T(8,128)(2,1)} %normed_one_grad.1.own), channel_id=1, source_target_pairs={{0,4},{4,0},{8,12},{12,8},{16,20},{20,16},{24,28},{28,24},{1,5},{5... | collective-permute-start | bytes 2752520 | tf_op jit(solution)/shard_map/ppermute | solution.py:433
  587.7 71.8 %collective-permute-start.63 = (bf16[4,256,384]{2,1,0:T(8,128)(2,1)}, bf16[4,256,384]{2,1,0:T(8,128)(2,1)}, u32[]{:S(2)}, u32[]{:S(2)}) collective-permute-start(bf16[4,256,384]{2,1,0:T(8,128)(2,1)} %get-tuple-element.91), channel_id=1, source_target_pairs={{0,8},{4,12},{8,0},{12,4},{16,24},{20,28},{24,16},{28,20},{1,9},{5... | collective-permute-start | bytes 2359304 | tf_op jit(solution)/shard_map/ppermute | solution.py:433
  620.2 45.2 %collective-permute-start.62 = (bf16[4,256,384]{2,1,0:T(8,128)(2,1)}, bf16[4,256,384]{2,1,0:T(8,128)(2,1)}, u32[]{:S(2)}, u32[]{:S(2)}) collective-permute-start(bf16[4,256,384]{2,1,0:T(8,128)(2,1)} %get-tuple-element.89), channel_id=1, source_target_pairs={{0,8},{4,12},{8,0},{12,4},{16,24},{20,28},{24,16},{28,20},{1,9},{5... | collective-permute-start | bytes 2359304 | tf_op jit(solution)/shard_map/ppermute | solution.py:433
  652.8 26.4 %collective-permute-start.60 = (bf16[384,512]{1,0:T(8,128)(2,1)}, bf16[384,512]{1,0:T(8,128)(2,1)}, u32[]{:S(2)}, u32[]{:S(2)}) collective-permute-start(bf16[384,512]{1,0:T(8,128)(2,1)} %get-tuple-element.167), channel_id=1, source_target_pairs={{0,3},{1,0},{2,1},{3,2},{4,7},{5,4},{6,5},{7,6},{8,11},{9,8},{10,9... | collective-permute-start | bytes 1179656 | tf_op jit(solution)/shard_map/ppermute | solution.py:437
  656.1 31.4 %collective-permute-start.59 = (bf16[384,512]{1,0:T(8,128)(2,1)}, bf16[384,512]{1,0:T(8,128)(2,1)}, u32[]{:S(2)}, u32[]{:S(2)}) collective-permute-start(bf16[384,512]{1,0:T(8,128)(2,1)} %get-tuple-element.168), channel_id=1, source_target_pairs={{0,2},{1,3},{2,0},{3,1},{4,6},{5,7},{6,4},{7,5},{8,10},{9,11},{10,... | collective-permute-start | bytes 1179656 | tf_op jit(solution)/shard_map/ppermute | solution.py:437
  659.5 28.0 %collective-permute-start.58 = (bf16[384,512]{1,0:T(8,128)(2,1)}, bf16[384,512]{1,0:T(8,128)(2,1)}, u32[]{:S(2)}, u32[]{:S(2)}) collective-permute-start(bf16[384,512]{1,0:T(8,128)(2,1)} %get-tuple-element.169), channel_id=1, source_target_pairs={{0,1},{1,2},{2,3},{3,0},{4,5},{5,6},{6,7},{7,4},{8,9},{9,10},{10,1... | collective-permute-start | bytes 1179656 | tf_op jit(solution)/shard_map/ppermute | solution.py:437
  665.3 58.8 %collective-permute-start.64 = (bf16[4,256,384]{2,1,0:T(8,128)(2,1)}, bf16[4,256,384]{2,1,0:T(8,128)(2,1)}, u32[]{:S(2)}, u32[]{:S(2)}) collective-permute-start(bf16[4,256,384]{2,1,0:T(8,128)(2,1)} %add_convert_fusion.5), channel_id=1, source_target_pairs={{0,16},{4,20},{8,24},{12,28},{16,0},{20,4},{24,8},{28,12},{1,17},{... | collective-permute-start | bytes 2359304 | tf_op jit(solution)/shard_map/ppermute | solution.py:433
  678.6 23.8 %collective-permute-start.107 = (bf16[256,512]{1,0:T(8,128)(2,1)S(1)}, bf16[256,512]{1,0:T(8,128)(2,1)S(1)}, u32[]{:S(2)}, u32[]{:S(2)}) collective-permute-start(bf16[256,512]{1,0:T(8,128)(2,1)S(1)} %copy-done.46), channel_id=1, source_target_pairs={{0,3},{1,0},{2,1},{3,2},{4,7},{5,4},{6,5},{7,6},{8,11},{9,8},{10,9... | collective-permute-start | bytes 786440 | tf_op jit(solution)/shard_map/ppermute | solution.py:437
  679.2 29.7 %collective-permute-start.114 = (bf16[256,512]{1,0:T(8,128)(2,1)S(1)}, bf16[256,512]{1,0:T(8,128)(2,1)S(1)}, u32[]{:S(2)}, u32[]{:S(2)}) collective-permute-start(bf16[256,512]{1,0:T(8,128)(2,1)S(1)} %copy-done.45), channel_id=1, source_target_pairs={{0,3},{1,0},{2,1},{3,2},{4,7},{5,4},{6,5},{7,6},{8,11},{9,8},{10,9... | collective-permute-start | bytes 786440 | tf_op jit(solution)/shard_map/ppermute | solution.py:437
  687.6 42.2 %collective-permute-start.53 = (bf16[224,1024]{1,0:T(8,128)(2,1)}, bf16[224,1024]{1,0:T(8,128)(2,1)}, u32[]{:S(2)}, u32[]{:S(2)}) collective-permute-start(bf16[224,1024]{1,0:T(8,128)(2,1)} %constant_dynamic-slice_fusion.37), channel_id=1, source_target_pairs={{0,1},{1,2},{2,3},{3,0},{4,5},{5,6},{6,7},{7,4},{8,9},{9,10},{10,1... | collective-permute-start | bytes 1376264 | tf_op jit(solution)/shard_map/ppermute | solution.py:437
  702.4 50.7 %collective-permute-start.61 = (bf16[2,384,512]{2,1,0:T(8,128)(2,1)}, bf16[2,384,512]{2,1,0:T(8,128)(2,1)}, u32[]{:S(2)}, u32[]{:S(2)}) collective-permute-start(bf16[2,384,512]{2,1,0:T(8,128)(2,1)} %pad_maximum_fusion.13), channel_id=1, source_target_pairs={{0,4},{4,0},{8,12},{12,8},{16,20},{20,16},{24,28},{28,24},{1,5},{5... | collective-permute-start | bytes 2359304 | tf_op jit(solution)/shard_map/ppermute | solution.py:433
  708.9 33.4 %collective-permute-start.108 = (f32[128,512]{1,0:T(8,128)}, f32[128,512]{1,0:T(8,128)}, u32[]{:S(2)}, u32[]{:S(2)}) collective-permute-start(f32[128,512]{1,0:T(8,128)} %get-tuple-element.173), channel_id=1, source_target_pairs={{0,4},{4,0},{8,12},{12,8},{16,20},{20,16},{24,28},{28,24},{1,5},{5... | collective-permute-start | bytes 786440 | tf_op jit(solution)/shard_map/ppermute | solution.py:433
  (135 other events, 1730.2 us)

commit v2 on v0

v2 whole, which is shorter than its diff:
```python
import functools
import math

import jax
import jax.numpy as jnp
from jax import lax
from jax.experimental import pallas as pl
from jax.experimental.pallas import tpu as pltpu
from jax.sharding import PartitionSpec as P

HEAD_DIM = 64
PAIR = 2 * HEAD_DIM
GROUPS = 4
EPSILON = 1e-05
MASKED = -1e9
SCALE = HEAD_DIM**-0.5
F32 = jnp.float32
BF16 = jnp.bfloat16
VMEM_LIMIT = 63 * 1024 * 1024
NT = (((1,), (1,)), ((), ()))
TN = (((0,), (0,)), ((), ()))


def call(kernel, name, outs, args, scratch=(), flops=0, grid=(1,), specs=None, out_specs=None):
    def whole(shape):
        return pl.BlockSpec(shape, lambda *_: (0,) * len(shape))

    in_specs = [whole(a.shape) for a in args[1:]] if specs is None else specs(whole)
    out_shape = [jax.ShapeDtypeStruct(shape, dtype) for shape, dtype in outs]
    moved = sum(a.size * a.dtype.itemsize for a in args) + sum(
        math.prod(o.shape) * jnp.dtype(o.dtype).itemsize for o in out_shape
    )
    return pl.pallas_call(
        kernel,
        name=name,
        out_shape=out_shape,
        grid_spec=pltpu.PrefetchScalarGridSpec(
            num_scalar_prefetch=1,
            grid=grid,
            in_specs=in_specs,
            out_specs=[whole(o.shape) for o in out_shape] if out_specs is None else out_specs(whole),
            scratch_shapes=list(scratch),
        ),
        compiler_params=pltpu.CompilerParams(vmem_limit_bytes=VMEM_LIMIT),
        cost_estimate=pl.CostEstimate(flops=int(flops), bytes_accessed=int(moved), transcendentals=0),
    )(*args)


def dot(a, b, dims=None):
    if dims is None:
        return jnp.dot(a, b, preferred_element_type=F32)
    return lax.dot_general(a, b, dims, preferred_element_type=F32)


def part_rows(g, j, rows):
    return pl.ds(pl.multiple_of((g ^ j) * rows, rows), rows)


def fill(g, halves, buffer, columns):
    rows = buffer.shape[0] // GROUPS
    for at_half, pieces in enumerate(halves):
        for j, piece in enumerate(pieces):
            to = part_rows(g, j, rows)
            for i in range(2):
                s = 2 * at_half + i
                for which, at in columns:
                    buffer[to, at + s * PAIR : at + (s + 1) * PAIR] = piece[
                        i, :rows, which * PAIR : (which + 1) * PAIR
                    ]


def unfill(g, halves, buffer, columns):
    rows = buffer.shape[0] // GROUPS
    for at_half, pieces in enumerate(halves):
        for j, piece in enumerate(pieces):
            to = part_rows(g, j, rows)
            for i in range(2):
                s = 2 * at_half + i
                for which, at in columns:
                    piece[i, :, which * PAIR : (which + 1) * PAIR] = buffer[
                        to, at + s * PAIR : at + (s + 1) * PAIR
                    ]


def row_step(m):
    return m // 4 if m % 64 == 0 else m


def over_rows(m, body):
    step = row_step(m)

    def run(i, carry):
        return body(pl.ds(pl.multiple_of(i * step, step), step), carry)

    return lambda carry: lax.fori_loop(0, m // step, run, carry)


def normal(values):
    centre = values - jnp.mean(values, axis=-1, keepdims=True)
    inverse = lax.rsqrt(jnp.mean(centre * centre, axis=-1, keepdims=True) + EPSILON)
    return centre * inverse, inverse


def norm_rows(value_at, gain, shift, normed, kept=None):
    gain_row, shift_row = gain[...], shift[...]

    def body(at, carry):
        value = value_at(at)
        if kept is not None:
            kept[at, :] = value
        normed[at, :] = (normal(value)[0] * gain_row + shift_row).astype(BF16)
        return carry

    over_rows(normed.shape[0], body)(0)


def norm_back_rows(own, came, values, gain, upstream, grad_ref, low_ref, sums):
    gain_row = gain[...]
    wide = values.shape[1]

    def body(at, carry):
        q = own[at, :].astype(F32) + came[at, :].astype(F32)
        n, inverse = normal(values[at, :].astype(F32))
        up = upstream[at, :].astype(F32)
        v = q * gain_row
        back = inverse * (v - jnp.mean(v, axis=-1, keepdims=True) - n * jnp.mean(v * n, axis=-1, keepdims=True))
        grad = up + back
        grad_ref[at, :] = grad.astype(grad_ref.dtype)
        if low_ref is not None:
            low_ref[at, :] = grad.astype(BF16)
        terms = (q * n, q, grad, up)
        return tuple(c + jnp.sum(t, axis=0, keepdims=True) for c, t in zip(carry, terms))

    totals = over_rows(values.shape[0], body)(tuple(jnp.zeros((1, wide), F32) for _ in range(4)))
    row = lax.broadcasted_iota(jnp.int32, sums.shape, 0)
    value = jnp.zeros(sums.shape, F32)
    for at, total in enumerate(totals):
        value = jnp.where(row == at, total, value)
    sums[...] = value


def lane_mask(shape, h):
    return (lax.broadcasted_iota(jnp.int32, shape, 1) // HEAD_DIM) == h


def mask_scores(scores, causal, valid):
    size = scores.shape[0]
    if causal:
        key_at = lax.broadcasted_iota(jnp.int32, scores.shape, 0)
        query_at = lax.broadcasted_iota(jnp.int32, scores.shape, 1)
        return jnp.where(key_at <= query_at, scores, MASKED)
    if valid < size:
        edge = valid // 8 * 8
        tail = scores[edge:, :]
        key_at = lax.broadcasted_iota(jnp.int32, tail.shape, 0) + edge
        return jnp.concatenate([scores[:edge, :], jnp.where(key_at < valid, tail, -jnp.inf)], axis=0)
    return scores


def attend(q_ref, k_ref, v_ref, mixed_ref, log_ref, score_buf, causal, blocks, valid):
    size = k_ref.shape[0] // blocks
    pairs = q_ref.shape[1] // PAIR

    def one_pair(p, carry):
        at = pl.ds(pl.multiple_of(p * PAIR, PAIR), PAIR)
        q_all = q_ref[:, at].astype(F32) * SCALE
        result = None
        for h in range(2):
            queries = jnp.where(lane_mask(q_all.shape, h), q_all, 0.0).astype(BF16)
            top = None
            for i in range(blocks):
                rows = slice(i * size, (i + 1) * size)
                scores = mask_scores(dot(k_ref[rows, at], queries, NT), causal, valid)
                score_buf[rows, :] = scores
                now = jnp.max(scores, axis=0, keepdims=True)
                top = now if top is None else jnp.maximum(top, now)
            total, mixed = None, None
            for i in range(blocks):
                rows = slice(i * size, (i + 1) * size)
                raised = jnp.exp(score_buf[rows, :] - top)
                now = jnp.sum(raised, axis=0, keepdims=True)
                total = now if total is None else total + now
                now = dot(v_ref[rows, at], raised.astype(BF16), TN)
                mixed = now if mixed is None else mixed + now
            log_ref[2 * p + h] = jnp.broadcast_to(top + jnp.log(total), log_ref.shape[1:])
            mixed = mixed / total
            if result is None:
                result = mixed
            else:
                row = lax.broadcasted_iota(jnp.int32, mixed.shape, 0)
                result = jnp.where(row < HEAD_DIM, result, mixed)
        mixed_ref[:, at] = jnp.transpose(result).astype(BF16)
        return carry

    lax.fori_loop(0, pairs, one_pair, 0)


def attend_back(q_ref, k_ref, v_ref, up_ref, mixed_ref, log_ref, dq_ref, dk_ref, dv_ref, sums, causal, blocks, valid):
    size = k_ref.shape[0] // blocks
    pairs = q_ref.shape[1] // PAIR

    def one_pair(p, carry):
        at = pl.ds(pl.multiple_of(p * PAIR, PAIR), PAIR)
        q_all = q_ref[:, at].astype(F32) * SCALE
        up_all = up_ref[:, at].astype(F32)
        product = up_all * mixed_ref[:, at].astype(F32)
        queries, upstream, inner, logs = [], [], [], []
        for h in range(2):
            chosen = lane_mask(q_all.shape, h)
            queries.append(jnp.where(chosen, q_all, 0.0).astype(BF16))
            upstream.append(jnp.where(chosen, up_all, 0.0).astype(BF16))
            ones = jnp.where(lane_mask((8, PAIR), h), 1.0, 0.0)
            inner.append(
                lax.dot_general(ones, product, NT, precision=lax.Precision.HIGHEST, preferred_element_type=F32)[0:1, :]
            )
            logs.append(log_ref[2 * p + h][0:1, :])
        query_grads = [None, None]
        value_sum = None
        for i in range(blocks):
            rows = slice(i * size, (i + 1) * size)
            keys, values = k_ref[rows, at], v_ref[rows, at]
            key_grad, value_grad = None, None
            for h in range(2):
                chance = jnp.exp(mask_scores(dot(keys, queries[h], NT), causal, valid) - logs[h])
                now = dot(chance.astype(BF16), upstream[h])
                value_grad = now if value_grad is None else value_grad + now
                grad = dot(values, upstream[h], NT)
                score_grad = (chance * (grad - inner[h])).astype(BF16)
                now = dot(score_grad, queries[h])
                key_grad = now if key_grad is None else key_grad + now
                now = dot(keys, score_grad, TN)
                query_grads[h] = now if query_grads[h] is None else query_grads[h] + now
            dk_ref[rows, at] = key_grad.astype(BF16)
            dv_ref[rows, at] = value_grad.astype(BF16)
            now = jnp.sum(value_grad, axis=0, keepdims=True)
            value_sum = now if value_sum is None else value_sum + now
        row = lax.broadcasted_iota(jnp.int32, query_grads[0].shape, 0)
        query_grad = jnp.transpose(jnp.where(row < HEAD_DIM, query_grads[0], query_grads[1])) * SCALE
        dq_ref[:, at] = query_grad.astype(BF16)
        query_sum = jnp.sum(query_grad, axis=0, keepdims=True)
        row = lax.broadcasted_iota(jnp.int32, (8, PAIR), 0)
        sums[:, at] = jnp.where(row == 0, query_sum, jnp.where(row == 1, value_sum, 0.0))
        return carry

    lax.fori_loop(0, pairs, one_pair, 0)


def self_forward_kernel(g_ref, start, gain, shift, bias, *refs):
    halves, (normed, qkv, mixed, logs, part), (w_in, w_out, score_buf) = (refs[0:4], refs[4:8]), refs[8:13], refs[13:]
    g, wide = g_ref[0], mixed.shape[1]
    norm_rows(lambda at: start[at, :].astype(F32), gain, shift, normed)
    fill(g, halves, w_in, [(0, 0), (1, wide), (2, 2 * wide)])
    fill(g, halves, w_out, [(3, 0)])
    qkv[...] = (dot(normed[...], w_in[...]) + bias[...]).astype(BF16)
    q, k, v = (qkv.at[:, i * wide : (i + 1) * wide] for i in range(3))
    attend(q, k, v, mixed, logs, score_buf, True, 1, start.shape[0])
    part[...] = dot(mixed[...], w_out[...], NT).astype(BF16)


def self_forward(g, start, gain, shift, bias, weights):
    m, d = start.shape
    wide = bias.shape[1] // 3
    heads = wide // HEAD_DIM
    return call(
        self_forward_kernel, "self_forward",
        [((m, d), BF16), ((m, 3 * wide), BF16), ((m, wide), BF16), ((heads, 8, m), F32), ((m, d), BF16)],
        [g, start, gain, shift, bias, *weights[0], *weights[1]],
        scratch=[pltpu.VMEM((d, 3 * wide), BF16), pltpu.VMEM((d, wide), BF16), pltpu.VMEM((m, m), F32)],
        flops=2 * m * d * 4 * wide + 4 * m * m * wide * 2,
    )


def cross_kv_kernel(g_ref, memory, bias, *refs):
    halves, kv, w_in = (refs[0:4], refs[4:8]), refs[8], refs[9]
    wide = kv.shape[1] // 2

    @pl.when(pl.program_id(0) == 0)
    def _():
        fill(g_ref[0], halves, w_in, [(1, 0), (2, wide)])

    kv[...] = (dot(memory[...], w_in[...]) + bias[...]).astype(BF16)


def cross_kv(g, memory, bias, weights, blocks):
    n, d = memory.shape
    wide = bias.shape[1]
    block = pl.BlockSpec((n // blocks, d), lambda i, _: (i, 0))
    return call(
        cross_kv_kernel, "cross_kv", [((n, wide), BF16)], [g, memory, bias, *weights[0], *weights[1]],
        scratch=[pltpu.VMEM((d, wide), BF16)], flops=2 * n * d * wide, grid=(blocks,),
        specs=lambda whole: [block, whole(bias.shape)] + [whole(w.shape) for w in (*weights[0], *weights[1])],
        out_specs=lambda whole: [pl.BlockSpec((n // blocks, wide), lambda i, _: (i, 0))],
    )[0]


def cross_forward_kernel(blocks, valid, g_ref, start, own, came, branch, gain, shift, bias, kv, *refs):
    halves, (middle, normed, q, mixed, logs, part), (w_in, w_out, score_buf) = (
        (refs[0:4], refs[4:8]), refs[8:14], refs[14:],
    )
    g, wide = g_ref[0], mixed.shape[1]
    branch_row = branch[...]
    norm_rows(
        lambda at: start[at, :].astype(F32) + (own[at, :].astype(F32) + came[at, :].astype(F32)) + branch_row,
        gain, shift, normed, middle,
    )
    fill(g, halves, w_in, [(0, 0)])
    fill(g, halves, w_out, [(3, 0)])
    q[...] = (dot(normed[...], w_in[...]) + bias[...]).astype(BF16)
    attend(q, kv.at[:, :wide], kv.at[:, wide:], mixed, logs, score_buf, False, blocks, valid)
    part[...] = dot(mixed[...], w_out[...], NT).astype(BF16)


def cross_forward(g, start, own, came, branch, gain, shift, bias, kv, weights, blocks, valid):
    m, d = start.shape
    n, wide = kv.shape[0], bias.shape[1]
    heads = wide // HEAD_DIM
    return call(
        functools.partial(cross_forward_kernel, blocks, valid), "cross_forward",
        [((m, d), F32), ((m, d), BF16), ((m, wide), BF16), ((m, wide), BF16), ((heads, 8, m), F32), ((m, d), BF16)],
        [g, start, own, came, branch, gain, shift, bias, kv, *weights[0], *weights[1]],
        scratch=[pltpu.VMEM((d, wide), BF16), pltpu.VMEM((d, wide), BF16), pltpu.VMEM((n, m), F32)],
        flops=2 * m * d * 2 * wide + 4 * m * n * wide * 2,
    )


def feed_kernel(slots, g_ref, middle, own, came, branch, gain, shift, upstream, bias, *refs):
    hidden, reduce = refs[0:4], refs[4:8]
    later, out_part, grad_part, sums = refs[8:12]
    g_hidden, g_reduce = refs[12:16], refs[16:20]
    normed, w_hidden, w_reduce, out_acc, grad_acc, result = refs[20:]
    g, s = g_ref[0], pl.program_id(0)
    rows = w_hidden.shape[0] // GROUPS

    @pl.when(s == 0)
    def _():
        branch_row = branch[...]
        norm_rows(
            lambda at: middle[at, :] + (own[at, :].astype(F32) + came[at, :].astype(F32)) + branch_row,
            gain, shift, normed, later,
        )

    for j in range(GROUPS):
        to = part_rows(g, j, rows)
        w_hidden[to, :] = hidden[j][...]
        w_reduce[to, :] = reduce[j][...]
    expanded = dot(normed[...], w_hidden[...]) + bias[...]
    phi = 0.5 * (1.0 + lax.erf(expanded * (0.5**0.5)))
    activated = (expanded * phi).astype(BF16)
    density = jnp.exp(expanded * expanded * -0.5) * ((2.0 * math.pi) ** -0.5)
    slope = phi + expanded * density
    expanded_grad = dot(upstream[...], w_reduce[...]) * slope
    expanded_low = expanded_grad.astype(BF16)
    sums[...] = jnp.broadcast_to(jnp.sum(expanded_grad, axis=0, keepdims=True), sums.shape)
    out_now = dot(activated, w_reduce[...], NT)
    grad_now = dot(expanded_low, w_hidden[...], NT)

    @pl.when(s == 0)
    def _():
        out_acc[...] = out_now
        grad_acc[...] = grad_now

    @pl.when(jnp.logical_and(s > 0, s < slots - 1))
    def _():
        out_acc[...] += out_now
        grad_acc[...] += grad_now

    @pl.when(s == slots - 1)
    def _():
        out_part[...] = (out_acc[...] + out_now).astype(BF16)
        grad_part[...] = (grad_acc[...] + grad_now).astype(BF16)

    result[...] = dot(normed[...], expanded_low, TN).astype(BF16)
    for j in range(GROUPS):
        g_hidden[j][...] = result[part_rows(g, j, rows), :]
    result[...] = dot(upstream[...], activated, TN).astype(BF16)
    for j in range(GROUPS):
        g_reduce[j][...] = result[part_rows(g, j, rows), :]


def feed(g, middle, own, came, branch, gain, shift, upstream, bias, hidden, reduce):
    m, d = middle.shape
    slots, _, width = bias.shape
    rows = d // GROUPS
    piece = pl.BlockSpec((None, rows, width), lambda s, _: (s, 0, 0))
    args = [middle, own, came, branch, gain, shift, upstream]
    return call(
        functools.partial(feed_kernel, slots), "feed_forward_and_back",
        [((m, d), F32), ((m, d), BF16), ((m, d), BF16), ((slots, 8, width), F32)]
        + [((slots, rows, width), BF16)] * (2 * GROUPS),
        [g, *args, bias, *hidden, *reduce],
        scratch=[
            pltpu.VMEM((m, d), BF16), pltpu.VMEM((d, width), BF16), pltpu.VMEM((d, width), BF16),
            pltpu.VMEM((m, d), F32), pltpu.VMEM((m, d), F32), pltpu.VMEM((d, width), BF16),
        ],
        flops=12 * m * d * slots * width, grid=(slots,),
        specs=lambda whole: [whole(a.shape) for a in args]
        + [pl.BlockSpec((None, 1, width), lambda s, _: (s, 0, 0))] + [piece] * (2 * GROUPS),
        out_specs=lambda whole: [whole((m, d))] * 3
        + [pl.BlockSpec((None, 8, width), lambda s, _: (s, 0, 0))] + [piece] * (2 * GROUPS),
    )


def output_kernel(g_ref, later, own, came, branch, out):
    branch_row = branch[...]

    def body(at, carry):
        out[at, :] = (later[at, :] + (own[at, :].astype(F32) + came[at, :].astype(F32)) + branch_row).astype(BF16)
        return carry

    over_rows(out.shape[0], body)(0)


def cross_back_kernel(blocks, valid, g_ref, own, came, later, gain, upstream, q, kv, mixed, logs, *refs):
    halves = (refs[0:4], refs[4:8])
    later_grad, later_low, sums, dq, dkv, head_sums, part = refs[8:15]
    w_out, w_in, mixed_grad = refs[15:]
    g, wide = g_ref[0], q.shape[1]
    fill(g, halves, w_out, [(3, 0)])
    fill(g, halves, w_in, [(0, 0)])
    norm_back_rows(own, came, later, gain, upstream, later_grad, later_low, sums)
    mixed_grad[...] = dot(later_low[...], w_out[...]).astype(BF16)
    attend_back(
        q, kv.at[:, :wide], kv.at[:, wide:], mixed_grad, mixed, logs, dq, dkv.at[:, :wide], dkv.at[:, wide:],
        head_sums, False, blocks, valid,
    )
    part[...] = dot(dq[...], w_in[...], NT).astype(BF16)


def cross_back(g, own, came, later, gain, upstream, q, kv, mixed, logs, weights, blocks, valid):
    m, d = later.shape
    n, wide = kv.shape[0], q.shape[1]
    return call(
        functools.partial(cross_back_kernel, blocks, valid), "cross_back",
        [((m, d), F32), ((m, d), BF16), ((8, d), F32), ((m, wide), BF16), ((n, 2 * wide), BF16), ((8, wide), F32),
         ((m, d), BF16)],
        [g, own, came, later, gain, upstream, q, kv, mixed, logs, *weights[0], *weights[1]],
        scratch=[pltpu.VMEM((d, wide), BF16), pltpu.VMEM((d, wide), BF16), pltpu.VMEM((m, wide), BF16)],
        flops=4 * m * d * wide + 10 * m * n * wide * 2,
    )


def cross_grads_kernel(blocks, g_ref, later_low, mixed, normed, dq, memory, dkv, *refs):
    halves, grads = (refs[0:4], refs[4:8]), (refs[8:12], refs[12:16])
    keep, send, w_in, result, piece = refs[16:]
    g, core, wide = g_ref[0], g_ref[1], dq.shape[1]
    n, d = memory.shape
    fill(g, halves, w_in, [(1, 0), (2, wide)])
    size = n // blocks
    for i in range(blocks):
        rows = slice(i * size, (i + 1) * size)
        piece[...] = dot(dkv[rows, :], w_in[...], NT).astype(BF16)
        keep[rows, :] = piece[:, pl.ds(pl.multiple_of(core * (d // 2), d // 2), d // 2)]
        send[rows, :] = piece[:, pl.ds(pl.multiple_of((1 - core) * (d // 2), d // 2), d // 2)]
    for which, left, right in (
        (3, later_low[...], mixed[...]), (0, normed[...], dq[...]),
        (1, memory[...], dkv[:, :wide]), (2, memory[...], dkv[:, wide:]),
    ):
        result[...] = dot(left, right, TN).astype(BF16)
        unfill(g, grads, result, [(which, 0)])


def cross_grads(g, later_low, mixed, normed, dq, memory, dkv, weights, blocks):
    m, d = later_low.shape
    n, wide = memory.shape[0], dq.shape[1]
    rows = d // GROUPS
    return call(
        functools.partial(cross_grads_kernel, blocks), "cross_grads",
        [((2, rows, 4 * PAIR), BF16)] * (2 * GROUPS) + [((n, d // 2), BF16)] * 2,
        [g, later_low, mixed, normed, dq, memory, dkv, *weights[0], *weights[1]],
        scratch=[pltpu.VMEM((d, 2 * wide), BF16), pltpu.VMEM((d, wide), BF16), pltpu.VMEM((n // blocks, d), BF16)],
        flops=4 * m * d * wide + 8 * n * d * wide,
    )


def self_back_kernel(g_ref, own, came, middle, gain, upstream, qkv, mixed, logs, *refs):
    halves = (refs[0:4], refs[4:8])
    middle_grad, middle_low, sums, dqkv, head_sums, part = refs[8:14]
    w_in, w_out, mixed_grad = refs[14:]
    g, wide = g_ref[0], mixed.shape[1]
    fill(g, halves, w_in, [(0, 0), (1, wide), (2, 2 * wide)])
    fill(g, halves, w_out, [(3, 0)])
    norm_back_rows(own, came, middle, gain, upstream, middle_grad, middle_low, sums)
    mixed_grad[...] = dot(middle_low[...], w_out[...]).astype(BF16)
    cut = [slice(i * wide, (i + 1) * wide) for i in range(3)]
    attend_back(
        *(qkv.at[:, c] for c in cut), mixed_grad, mixed, logs, *(dqkv.at[:, c] for c in cut), head_sums, True, 1,
        middle.shape[0],
    )
    part[...] = dot(dqkv[...], w_in[...], NT).astype(BF16)


def self_back(g, own, came, middle, gain, upstream, qkv, mixed, logs, weights):
    m, d = middle.shape
    wide = mixed.shape[1]
    return call(
        self_back_kernel, "self_back",
        [((m, d), F32), ((m, d), BF16), ((8, d), F32), ((m, 3 * wide), BF16), ((8, wide), F32), ((m, d), BF16)],
        [g, own, came, middle, gain, upstream, qkv, mixed, logs, *weights[0], *weights[1]],
        scratch=[pltpu.VMEM((d, 3 * wide), BF16), pltpu.VMEM((d, wide), BF16), pltpu.VMEM((m, wide), BF16)],
        flops=8 * m * d * wide + 10 * m * m * wide * 2,
    )


def self_grads_kernel(g_ref, middle_low, mixed, normed, dqkv, *refs):
    grads, result = (refs[0:4], refs[4:8]), refs[8]
    g, wide = g_ref[0], mixed.shape[1]
    result[...] = dot(middle_low[...], mixed[...], TN).astype(BF16)
    unfill(g, grads, result, [(3, 0)])
    for which in range(3):
        result[...] = dot(normed[...], dqkv[:, which * wide : (which + 1) * wide], TN).astype(BF16)
        unfill(g, grads, result, [(which, 0)])


def self_grads(g, middle_low, mixed, normed, dqkv):
    m, d = middle_low.shape
    wide = mixed.shape[1]
    return call(
        self_grads_kernel, "self_grads", [((2, d // GROUPS, 4 * PAIR), BF16)] * (2 * GROUPS),
        [g, middle_low, mixed, normed, dqkv], scratch=[pltpu.VMEM((d, wide), BF16)], flops=8 * m * d * wide,
    )


def start_back_kernel(g_ref, own, came, start, gain, upstream, grad, sums):
    norm_back_rows(own, came, start, gain, upstream, grad, None, sums)


def flip(x, bit, size):
    return lax.ppermute(x, "fsdp", [(i, i ^ (1 << bit)) for i in range(size)])


def turn(x, step, size):
    return lax.ppermute(x, "tensor", [(i, (i + step) % size) for i in range(size)])


def half(x, index, axis):
    size = x.shape[axis] // 2
    return lax.dynamic_slice_in_dim(x, index * size, size, axis=axis)


def after(x, *waits):
    return lax.optimization_barrier((x, *waits))[0]


def after_all(xs, waits):
    return lax.optimization_barrier((*xs, *waits))[: len(xs)]


def add(a, b):
    return (a.astype(F32) + b.astype(F32)).astype(BF16)


def on_device(
    n_f, n_t,
    tokens, encoder, cotangent, self_weights, self_biases, self_output, cross_query, cross_memory,
    cross_biases, cross_output, hidden_weight, hidden_bias, reduce_weight, norm_gains, norm_shifts, branch_biases,
):
    bits = n_f.bit_length() - 1
    x_bit, y_bit = bits - 2, bits - 1
    f = lax.axis_index("fsdp")
    z = lax.axis_index("tensor")
    core = f % 2
    group = f >> x_bit
    g = jnp.stack([group, core]).astype(jnp.int32)
    length, d = tokens.shape[1], tokens.shape[2]
    frames = encoder.shape[1]
    own_clips = tokens.shape[0]
    assert own_clips * 2 == n_t == 4 and bits >= 3
    per = d // n_f
    units_here = hidden_bias.shape[1]
    units = units_here * n_f
    heads_here = self_biases.shape[2]
    inner = n_f // GROUPS

    def begin(weights, extra=None, waits=()):
        keep = jnp.concatenate([half(w, core, 1) for w in weights], axis=1)
        send = jnp.concatenate([half(w, 1 - core, 1) for w in weights], axis=1)
        width = keep.shape[1]
        now, more = keep, extra
        for bit in range(bits - 2):
            rows = now.shape[0]
            out = send if bit == 0 else now
            if more is not None:
                out = jnp.concatenate([out, more.reshape(-1, width)])
            if waits:
                out = after(out, *waits)
            came = flip(out, bit, n_f)
            low = (f >> bit) % 2 == 0
            a, b = now, came[:rows]
            now = jnp.where(low, jnp.concatenate([a, b]), jnp.concatenate([b, a]))
            if more is not None:
                b = came[rows:]
                more = jnp.where(low, jnp.concatenate([more, b]), jnp.concatenate([b, more]))
        return now if more is None else jnp.concatenate([now, more])

    def around(now):
        return [now] + [turn(now, s, n_t) for s in range(1, n_t)]

    def gather_xy(a, b):
        a1, b2 = flip(a, x_bit, n_f), flip(b, y_bit, n_f)
        b1, a2 = flip(b, x_bit, n_f), flip(a, y_bit, n_f)
        a3, b3 = flip(a1, y_bit, n_f), flip(b2, x_bit, n_f)
        return (a, a1, a2, a3), (b, b1, b2, b3)

    small = jnp.concatenate(
        [v.reshape(-1) for v in (norm_gains, norm_shifts, branch_biases, hidden_bias, self_biases, cross_biases)]
    )
    lanes = 4 * PAIR
    small_rows = -(-small.shape[0] // (16 * lanes)) * 16
    small = jnp.pad(small, (0, small_rows * lanes - small.shape[0])).reshape(small_rows, lanes)

    first = around(begin([self_weights[0], self_weights[1], self_weights[2], self_output.T], small))
    w_self = gather_xy(jnp.stack(first[:2]), jnp.stack(first[2:]))
    second = begin([cross_query, cross_memory[0], cross_memory[1], cross_output.T], waits=first[:1])
    second = around(after(second, *first[1:]))
    w_cross = gather_xy(
        *after_all([jnp.stack(second[:2]), jnp.stack(second[2:])], w_self[0][1:3] + w_self[1][1:3])
    )
    third = begin([hidden_weight, reduce_weight.T], waits=first[:1])
    third = around(after(third, *second[1:]))
    wide_half = units // 2
    w_hidden, w_reduce = gather_xy(
        *after_all(
            [jnp.stack([t[:, :wide_half] for t in third]), jnp.stack([t[:, wide_half:] for t in third])],
            w_cross[0][1:3] + w_cross[1][1:3],
        )
    )

    rows = d // GROUPS
    table = jnp.stack(
        [
            jnp.concatenate([w_self[0][j][:, rows:], w_self[1][j][:, rows:]]).reshape(n_t, inner, -1)
            for j in range(GROUPS)
        ]
    )
    table = jnp.concatenate(
        [lax.dynamic_index_in_dim(table, group ^ j, axis=0, keepdims=False) for j in range(GROUPS)], axis=1
    ).astype(F32)
    features = table[0, :, : 9 * per].reshape(n_f, 9, per).transpose(1, 0, 2).reshape(9, d)
    at = 9 * per
    hidden_slots = half(table[:, :, at : at + units_here].reshape(n_t, 1, units), core, 2)
    at += units_here

    def head_slots(at):
        v = table[:, :, at : at + 2 * heads_here].reshape(n_t, n_f, 2, heads_here).transpose(2, 0, 1, 3)
        return half(v.reshape(2, n_t, n_f * heads_here), core, 2).reshape(2, 1, -1)

    self_bias = head_slots(at)
    cross_bias = head_slots(at + 2 * heads_here)
    zero = jnp.zeros_like(self_bias[0])
    qkv_bias = jnp.concatenate([self_bias[0], zero, self_bias[1]], axis=1)
    kv_bias = jnp.concatenate([zero, cross_bias[1]], axis=1)
    gain, shift, branch = ([features[3 * i + j : 3 * i + j + 1] for j in range(3)] for i in range(3))

    mine = core == z // own_clips

    def take_clip(x):
        x = lax.dynamic_index_in_dim(x, z % own_clips, axis=0, keepdims=False)
        return jnp.where(mine, x, flip(x, 0, n_f))

    part_frames = frames // n_t
    part_pad = -(-part_frames // 128) * 128
    start = take_clip(after(tokens, first[0]))
    upstream = take_clip(after(cotangent, w_self[0][1]))
    memory = jnp.pad(
        take_clip(after(encoder, first[1])).reshape(n_t, part_frames, d), ((0, 0), (0, part_pad - part_frames), (0, 0))
    ).reshape(n_t * part_pad, d)

    def scatter_one(pieces, y_first):
        bit = y_bit if y_first else x_bit
        zero, one, two, three = pieces
        out = (two, three) if y_first else (one, three)
        return [flip(p, bit, n_f) for p in out]

    def scatter_two(pieces, came, y_first):
        zero, one, two, three = pieces
        rest = (zero, one) if y_first else (zero, two)
        stay, go = add(rest[0], came[0]), add(rest[1], came[1])
        return stay, flip(go, x_bit if y_first else y_bit, n_f)

    def scatter_z(slots):
        return slots[0], [turn(slots[s], -s, n_t) for s in range(1, n_t)]

    def scatter_end(own, came):
        now = own.astype(F32)
        for other in came:
            now = now + other.astype(F32)
        for bit in range(bits - 3, 0, -1):
            up = (f >> bit) % 2
            now = half(now, up, 0) + flip(half(now, 1 - up, 0).astype(BF16), bit, n_f).astype(F32)
        return half(now, core, 0), flip(half(now, 1 - core, 0), 0, n_f)

    def unpack(shares, widths):
        keep, came = shares
        result, at = [], 0
        for width in widths:
            a, b = keep[:, at : at + width], came[:, at : at + width]
            result.append(jnp.where(core == 0, jnp.concatenate([a, b], 1), jnp.concatenate([b, a], 1)))
            at += width
        return result

    normed_one, qkv, mixed_one, log_one, part = self_forward(g, start, gain[0], shift[0], qkv_bias, w_self)
    part_came = flip(part, 0, n_f)
    kv = cross_kv(g, memory, kv_bias, w_cross, n_t)
    middle, normed_two, cross_q, mixed_two, log_two, part = cross_forward(
        g, start, part, part_came, branch[0], gain[1], shift[1], cross_bias[0], kv, w_cross, n_t, part_frames
    )
    later, out_part, part, hidden_sums, *g_feed = feed(
        g, middle, part, flip(part, 0, n_f), branch[1], gain[2], shift[2], upstream, hidden_slots, w_hidden, w_reduce
    )
    g_hidden, g_reduce = g_feed[:GROUPS], g_feed[GROUPS:]

    part_came = flip(part, 0, n_f)
    hidden_came, reduce_came = scatter_one(g_hidden, True), scatter_one(g_reduce, False)
    (output,) = call(
        output_kernel, "output", [((length, d), BF16)], [g, later, out_part, flip(out_part, 0, n_f), branch[2]]
    )
    output_half = half(output, core, 0)
    later_grad, later_low, sums_three, dq, dkv, cross_sums, part = cross_back(
        g, part, part_came, after(later, output_half), gain[2], upstream, cross_q, kv, mixed_two, log_two, w_cross,
        n_t, part_frames,
    )
    part_came = flip(part, 0, n_f)
    *g_cross, memory_keep, memory_send = cross_grads(
        g, later_low, mixed_two, normed_two, dq, memory, dkv, w_cross, n_t
    )
    g_cross = (g_cross[:GROUPS], g_cross[GROUPS:])
    memory_came = flip(memory_send, 0, n_f)
    hidden_came, reduce_came = after_all(hidden_came, [memory_keep]), after_all(reduce_came, [memory_keep])
    hidden_two = scatter_two(g_hidden, hidden_came, True)
    reduce_two = scatter_two(g_reduce, reduce_came, False)
    cross_one = (scatter_one(g_cross[0], True), scatter_one(g_cross[1], False))
    memory_sum = add(memory_keep, memory_came)
    middle_grad, middle_low, sums_two, dqkv, self_sums, part = self_back(
        g, part, part_came, after(middle, hidden_two[0], reduce_two[0], memory_sum), gain[1], later_grad, qkv,
        mixed_one, log_one, w_self,
    )
    part_came = flip(part, 0, n_f)
    hidden_last, reduce_last = after_all([hidden_two[1], reduce_two[1]], [middle_low])
    feed_slots = [
        jnp.concatenate([add(hidden_two[0][s], hidden_last[s]), add(reduce_two[0][s], reduce_last[s])], axis=1)
        for s in range(n_t)
    ]
    g_self = self_grads(g, after(middle_low, *feed_slots), mixed_one, normed_one, dqkv)
    g_self = (g_self[:GROUPS], g_self[GROUPS:])
    feed_own, feed_came = scatter_z(feed_slots)
    self_one = (scatter_one(g_self[0], True), scatter_one(g_self[1], False))
    start_grad, sums_one = call(
        start_back_kernel, "start_back", [((length, d), BF16), ((8, d), F32)],
        [g, part, part_came, after(start, g_self[0][0]), gain[0], middle_grad],
    )
    start_half = half(start_grad, core, 0)

    def attention_slots(grads, came, waits):
        came = (after_all(came[0], waits), after_all(came[1], waits))
        two = (scatter_two(grads[0], came[0], True), scatter_two(grads[1], came[1], False))
        return [add(t[0][i], t[1][i]) for t in two for i in range(2)]

    cross_own, cross_came = scatter_z(attention_slots(g_cross, cross_one, [start_half]))
    self_own, self_came = scatter_z(attention_slots(g_self, self_one, [start_half]))
    feed_came = after_all(feed_came, [start_half])
    hidden_share, reduce_t = unpack(scatter_end(feed_own, feed_came), [wide_half, wide_half])
    cq_share, ck_share, cv_share, cross_out_t = unpack(scatter_end(cross_own, cross_came), [PAIR] * 4)
    q_share, k_share, v_share, self_out_t = unpack(scatter_end(self_own, self_came), [PAIR] * 4)

    lead = jnp.where(core == 0, 1.0, 0.0).astype(F32)
    feature_sums = jnp.stack(
        [sums_one[0], sums_two[0], sums_three[0], sums_one[1], sums_two[1], sums_three[1],
         sums_two[2], sums_three[2], sums_three[3]]
    ) * lead

    def from_slots(v):
        natural = jnp.stack(
            [lax.dynamic_index_in_dim(v, (z - at) % n_t, axis=0, keepdims=False) for at in range(n_t)], axis=1
        )
        wide = jnp.zeros((*natural.shape[:2], 2 * natural.shape[2]), F32)
        return lax.dynamic_update_slice(wide, natural, (0, 0, core * natural.shape[2]))

    def by_slot(v):
        return v[:2].reshape(2, n_t, -1).transpose(1, 0, 2)

    unit_sums = [from_slots(hidden_sums[:, :1]), from_slots(by_slot(self_sums)), from_slots(by_slot(cross_sums))]
    packed = jnp.concatenate([feature_sums.reshape(-1)] + [u.reshape(-1) for u in unit_sums]).reshape(-1, 1024)
    for bit in range(bits):
        packed = packed + flip(packed, bit, n_f)
    for step in (1, 2):
        packed = packed + lax.ppermute(packed, "tensor", [(i, i ^ step) for i in range(n_t)])
    packed = packed.reshape(-1)
    feature_share = lax.dynamic_slice(packed[: 9 * d].reshape(9, d), (0, f * per), (9, per))

    def unit_share(at, count, total):
        block = packed[at : at + count * n_t * total].reshape(count, n_t, total)
        return lax.dynamic_slice(block, (0, z, f * (total // n_f)), (count, 1, total // n_f))

    at = 9 * d
    hidden_bias_share = unit_share(at, 1, units)[0]
    at += n_t * units
    self_bias_share = unit_share(at, 2, heads_here * n_f)
    at += 2 * n_t * heads_here * n_f
    cross_bias_share = unit_share(at, 2, heads_here * n_f)

    def own_of(slots, c):
        stacked = jnp.stack(slots)
        return jnp.stack(
            [
                lax.dynamic_index_in_dim(stacked, (z - c * own_clips - i) % n_t, axis=0, keepdims=False)
                for i in range(own_clips)
            ]
        )

    def join(slots, axis):
        keep, came = own_of(slots, core), flip(own_of(slots, 1 - core), 0, n_f)
        return jnp.where(core == 0, jnp.concatenate([keep, came], axis), jnp.concatenate([came, keep], axis))

    def spread_clip(x):
        return join(around(x), 1)

    summed = memory_sum.reshape(n_t, part_pad, d // 2)
    slots = []
    for s in range(n_t):
        block = lax.dynamic_index_in_dim(summed, (z + s) % n_t, axis=0, keepdims=False)
        slots.append(turn(block, s, n_t) if s else block)
    memory_share = join(slots, 2)

    return (
        spread_clip(output_half),
        spread_clip(start_half),
        memory_share[:, :part_frames],
        jnp.stack([q_share, k_share, v_share]),
        self_bias_share,
        self_out_t.T,
        cq_share,
        jnp.stack([ck_share, cv_share]),
        cross_bias_share,
        cross_out_t.T,
        hidden_share,
        hidden_bias_share,
        reduce_t.T,
        feature_share[0:3],
        feature_share[3:6],
        feature_share[6:9],
    )


def solution(mesh):
    n_f, n_t = mesh.shape["fsdp"], mesh.shape["tensor"]
    clips = P("fsdp", None, None)
    stacked = P(None, "fsdp", "tensor")
    biases = P(None, "tensor", "fsdp")
    up, down, rows = P("fsdp", "tensor"), P("tensor", "fsdp"), P(None, "fsdp")
    return jax.shard_map(
        functools.partial(on_device, n_f, n_t),
        mesh=mesh,
        in_specs=(
            clips, clips, clips, stacked, biases, down, up, stacked, biases, down, up, down, down, rows, rows, rows,
        ),
        out_specs=(
            clips, clips, P("fsdp", "tensor", None), stacked, biases, down, up, stacked, biases, down, up, down,
            down, rows, rows, rows,
        ),
        check_vma=False,
    )
```

time: 2050 us -> 661 us (0.32)
  waiting for transfers between devices: 1300 us -> 231 us
  blocking collectives: 289 us -> 0 us
  matrix products: 215 us -> 0 us
  Pallas kernels: 0 us -> 147 us
  starting transfers between devices: 7.86 us -> 128 us
  local copies, waits for them, and re-layouts: 108 us -> 70.3 us
  other arithmetic: 105 us -> 72.7 us
    reduce_scatter x14 -> x0, waiting for transfers between devices: 621 us -> none  [the longest x2 107 us: step(): lax.psum_scatter(grads[7], 'fsdp', scatter_dimension=0, tiled=True)]
    psum x10 -> x0, waiting for transfers between devices: 357 us -> none  [the longest x6 271 us: input_total(): lax.psum(partial_sum.astype(jnp.bfloat16), 'tensor').astype(jnp.float32)]
    ppermute x0 -> x87, waiting for transfers between devices: none -> 231 us  [the longest x58 114 us: flip(): return lax.ppermute(x, 'fsdp', [(i, i ^ 1 << bit) for i in range(size)])]
    while x58 -> x0, waiting for transfers between devices: 224 us -> none
    dot_general x84 -> x0, matrix products: 215 us -> none  [the longest x20 60.9 us: product(): return jnp.dot(left, right, preferred_element_type=jnp.float32)]
    all_gather x18 -> x0, blocking collectives: 172 us -> none  [the longest x2 22.9 us: fetch(): lax.all_gather(self_output, 'fsdp', axis=1, tiled=True)]
    pallas_call x0 -> x10, Pallas kernels: none -> 147 us  [call(): pl.pallas_call(kernel, name=name, out_shape=out_shape, grid_spec=pltpu.Pr...]
    ppermute x0 -> x87, starting transfers between devices: none -> 128 us  [the longest x27 75.3 us: turn(): lax.ppermute(x, 'tensor', [(i, (i + step) % size) for i in range(size)])]
  transfers between devices with their start and end apart: 46 -> 87, of which waited for: 36 -> 29; matrix products, arithmetic and copies ran while one was open for 19% -> 20% of each run, Pallas kernels for 0% -> 19%
where the time goes in v2:
time: 661 us; the launch traced here: 652 us
  waiting for transfers between devices  231 us (35%)
  Pallas kernels  147 us (22%)
  starting transfers between devices  128 us (19%)
  other arithmetic  72.7 us (11%)
  local copies, waits for them, and re-layouts  70.3 us (11%)
    pallas_call x10, Pallas kernels, call(): pl.pallas_call(kernel, name=name, out_shape=out_shape, grid_spec=pltpu.Pr...  147 us
    ppermute x58, waiting for transfers between devices, flip(): return lax.ppermute(x, 'fsdp', [(i, i ^ 1 << bit) for i in range(size)])  114 us
    ppermute x27, waiting for transfers between devices, turn(): lax.ppermute(x, 'tensor', [(i, (i + step) % size) for i in range(size)])  112 us
    ppermute x27, starting transfers between devices, turn(): lax.ppermute(x, 'tensor', [(i, (i + step) % size) for i in range(size)])  75.3 us
    ppermute x58, starting transfers between devices, flip(): return lax.ppermute(x, 'fsdp', [(i, i ^ 1 << bit) for i in range(size)])  45.5 us
    convert_element_type x19, other arithmetic, add(): return (a.astype(F32) + b.astype(F32)).astype(BF16)  31.2 us
    unnamed x104, local copies, waits for them, and re-layouts  14.1 us
  transfers between devices with their start and end apart: 87, of which 29 were waited for; matrix products, arithmetic and copies ran while one was open for 20% of the time, Pallas kernels for 19%

profile of v2, /device:TPU:0, one launch (start us, length us, event | category | flops | bytes accessed | tf_op | source)
XLA Modules:
  0.0 651.9 jit_solution(17170546416387108293)
XLA Ops:
  4.1 2.8 concatenate.257
  13.6 3.1 collective-permute-start.2
  16.7 2.6 collective-permute-start.3
  26.9 12.0 %collective-permute-done.3 = bf16[288,512]{1,0:T(8,128)(2,1)S(1)} collective-permute-done((bf16[288,512]{1,0:T(8,128)(2,1)}, bf16[288,512]{1,0:T(8,128)(2,1)S(1)}, u32[]{:S(2)}, u32[]{:S(2)}) %collective-permute-start.3) | collective-permute-done | bytes 294944 | tf_op jit(solution)/shard_map/ppermute | solution.py:532
  38.9 6.8 %collective-permute-start.14 = (bf16[256,512]{1,0:T(8,128)(2,1)S(1)}, bf16[256,512]{1,0:T(8,128)(2,1)}, u32[]{:S(2)}, u32[]{:S(2)}) collective-permute-start(bf16[256,512]{1,0:T(8,128)(2,1)S(1)} %maximum_select_fusion.6), channel_id=1, source_target_pairs={{0,1},{1,2},{2,3},{3,0},{4,5},{5,6},{6,7},{7,4},{8,9},{9,10},{10,1... | collective-permute-start | bytes 786440 | tf_op jit(solution)/shard_map/ppermute | solution.py:532
  52.8 4.7 copy.48
  58.2 5.6 collective-permute-done.15
  71.1 4.8 collective-permute-start.26
  75.9 3.5 collective-permute-start.27
  97.4 16.5 %collective-permute-done.27 = bf16[256,1024]{1,0:T(8,128)(2,1)S(1)} collective-permute-done((bf16[256,1024]{1,0:T(8,128)(2,1)S(1)}, bf16[256,1024]{1,0:T(8,128)(2,1)S(1)}, u32[]{:S(2)}, u32[]{:S(2)}) %collective-permute-start.27) | collective-permute-done | bytes 524320 | tf_op jit(solution)/shard_map/ppermute | solution.py:532
  121.3 7.4 %collective-permute-done.21.refs_6_ = bf16[2,256,512]{2,1,0:T(8,128)(2,1)S(1)} collective-permute-done((bf16[2,256,512]{2,1,0:T(8,128)(2,1)S(1)}, bf16[2,256,512]{2,1,0:T(8,128)(2,1)S(1)}, u32[]{:S(2)}, u32[]{:S(2)}) %collective-permute-start.21) | collective-permute-done | bytes 524320 | tf_op jit(solution)/shard_map/ppermute | solution.py:528
  132.0 9.3 %collective-permute-done.9.refs_3_ = bf16[2,288,512]{2,1,0:T(8,128)(2,1)S(1)} collective-permute-done((bf16[2,288,512]{2,1,0:T(8,128)(2,1)S(1)}, bf16[2,288,512]{2,1,0:T(8,128)(2,1)S(1)}, u32[]{:S(2)}, u32[]{:S(2)}) %collective-permute-start.9) | collective-permute-done | bytes 589856 | tf_op jit(solution)/shard_map/ppermute | solution.py:528
  146.4 12.3 %self_forward.1 = (bf16[448,1024]{1,0:T(8,128)(2,1)}, bf16[448,1536]{1,0:T(8,128)(2,1)}, bf16[448,512]{1,0:T(8,128)(2,1)}, f32[8,8,448]{2,1,0:T(8,128)}, bf16[448,1024]{1,0:T(8,128)(2,1)}) custom-call(s32[2]{0:T(128)} %pad_add_fusion.g_ref, bf16[448,1024]{1,0:T(8,128)(2,1)} %broadcast_select_fusion.2.start, f32[1,1024]{1,0:T(1,128)} %bitcast.224, ...), custom_call_target="tpu_custom_call" | custom-call | flops 2701131776 | bytes 9435144 | tf_op jit(solution)/shard_map/self_forward/pallas_call | solution.py:33
  159.9 14.3 %collective-permute-done.19.refs_3_ = bf16[2,256,512]{2,1,0:T(8,128)(2,1)} collective-permute-done((bf16[2,256,512]{2,1,0:T(8,128)(2,1)}, bf16[2,256,512]{2,1,0:T(8,128)(2,1)}, u32[]{:S(2)}, u32[]{:S(2)}) %collective-permute-start.19) | collective-permute-done | bytes 524320 | tf_op jit(solution)/shard_map/ppermute | solution.py:528
  180.4 4.1 pad.10
  184.5 3.1 collective-permute-done.22.refs_7_
  188.1 9.1 %cross_kv.1.kv = bf16[1536,1024]{1,0:T(8,128)(2,1)} custom-call(s32[2]{0:T(128)} %pad_add_fusion.g_ref, bf16[1536,1024]{1,0:T(8,128)(2,1)} %bitcast.199, f32[1,1024]{1,0:T(1,128)} %concatenate.270.bias, bf16[2,256,512]{2,1,0:T(8,128)(2,1)} %pad_maximum_fusion.14.refs_0_, bf16[2,256,512]{2,1,0:T(8,128)(2,1)} %collective-permute-done.17.refs_1_, ...), custom_call_target="tpu_custom_call" | custom-call | flops 3221225472 | bytes 10489864 | tf_op jit(solution)/shard_map/cross_kv/pallas_call | solution.py:33
  200.7 18.2 %cross_forward.1 = (f32[448,1024]{1,0:T(8,128)}, bf16[448,1024]{1,0:T(8,128)(2,1)}, bf16[448,512]{1,0:T(8,128)(2,1)}, bf16[448,512]{1,0:T(8,128)(2,1)}, f32[8,8,448]{2,1,0:T(8,128)}, /*index=5*/bf16[448,1024]{1,0:T(8,128)(2,1)}) custom-call(s32[2]{0:T(128)} %pad_add_fusion.g_ref, bf16[448,1024]{1,0:T(8,128)(2,1)} %broadcast_select_fusion.2.start, ...), custom_call_target="tpu_custom_call" | custom-call | flops 3758096384 | bytes 14809096 | tf_op jit(solution)/shard_map/cross_forward/pallas_call | solution.py:33
  223.5 10.3 %collective-permute-done.31.refs_3_ = bf16[4,256,512]{2,1,0:T(8,128)(2,1)} collective-permute-done((bf16[4,256,512]{2,1,0:T(8,128)(2,1)}, bf16[4,256,512]{2,1,0:T(8,128)(2,1)}, u32[]{:S(2)}, u32[]{:S(2)}) %collective-permute-start.31) | collective-permute-done | bytes 1048608 | tf_op jit(solution)/shard_map/ppermute | solution.py:528
  233.8 9.3 %collective-permute-done.34.refs_7_ = bf16[4,256,512]{2,1,0:T(8,128)(2,1)} collective-permute-done((bf16[4,256,512]{2,1,0:T(8,128)(2,1)}, bf16[4,256,512]{2,1,0:T(8,128)(2,1)}, u32[]{:S(2)}, u32[]{:S(2)}) %collective-permute-start.34) | collective-permute-done | bytes 1048608 | tf_op jit(solution)/shard_map/ppermute | solution.py:528
  243.1 22.5 %feed_forward_and_back.1 = (f32[448,1024]{1,0:T(8,128)}, bf16[448,1024]{1,0:T(8,128)(2,1)}, bf16[448,1024]{1,0:T(8,128)(2,1)}, f32[4,8,512]{2,1,0:T(8,128)}, bf1...) custom-call(s32[2]{0:T(128)} %pad_add_fusion.g_ref, ...), custom_call_target="tpu_custom_call" | custom-call | flops 11274289152 | bytes 25120776 | tf_op jit(solution)/shard_map/feed_forward_and_back/pallas_call | solution.py:33
  270.2 4.1 output.1
  276.1 7.7 %collective-permute-start.36 = (bf16[224,1024]{1,0:T(8,128)(2,1)}, bf16[224,1024]{1,0:T(8,128)(2,1)}, u32[]{:S(2)}, u32[]{:S(2)}) collective-permute-start(bf16[224,1024]{1,0:T(8,128)(2,1)} %constant_dynamic-slice_fusion.36), channel_id=1, source_target_pairs={{0,1},{1,2},{2,3},{3,0},{4,5},{5,6},{6,7},{7,4},{8,9},{9,10},{10,1... | collective-permute-start | bytes 1376264 | tf_op jit(solution)/shard_map/ppermute | solution.py:532
  283.8 3.1 collective-permute-start.37
  286.9 31.5 %cross_back.1 = (f32[448,1024]{1,0:T(8,128)}, bf16[448,1024]{1,0:T(8,128)(2,1)}, f32[8,1024]{1,0:T(8,128)}, bf16[448,512]{1,0:T(8,128)(2,1)}, bf16[1536,1024]{1,...) custom-call(s32[2]{0:T(128)} %pad_add_fusion.g_ref, bf16[448,1024]{1,0:T(8,128)(2,1)} %get-tuple-element.120.own, ...), custom_call_target="tpu_custom_call" | custom-call | flops 7985954816 | bytes 20287496 | tf_op jit(solution)/shard_map/cross_back/pallas_call | solution.py:33
  319.9 17.3 %cross_grads.1 = (bf16[2,256,512]{2,1,0:T(8,128)(2,1)}, bf16[2,256,512]{2,1,0:T(8,128)(2,1)}, bf16[2,256,512]{2,1,0:T(8,128)(2,1)}, bf16[2,256,512]{2,1,0:T(8,12...) custom-call(s32[2]{0:T(128)} %pad_add_fusion.g_ref, ...), custom_call_target="tpu_custom_call" | custom-call | flops 7381975040 | bytes 20578312 | tf_op jit(solution)/shard_map/cross_grads/pallas_call | solution.py:33
  346.3 17.3 %collective-permute-done.42 = bf16[4,256,512]{2,1,0:T(8,128)(2,1)S(1)} collective-permute-done((bf16[4,256,512]{2,1,0:T(8,128)(2,1)}, bf16[4,256,512]{2,1,0:T(8,128)(2,1)S(1)}, u32[]{:S(2)}, u32[]{:S(2)}) %collective-permute-start.42) | collective-permute-done | bytes 1048608 | tf_op jit(solution)/shard_map/ppermute | solution.py:528
  365.1 21.0 %collective-permute-done.43 = bf16[4,256,512]{2,1,0:T(8,128)(2,1)S(1)} collective-permute-done((bf16[4,256,512]{2,1,0:T(8,128)(2,1)}, bf16[4,256,512]{2,1,0:T(8,128)(2,1)S(1)}, u32[]{:S(2)}, u32[]{:S(2)}) %collective-permute-start.43) | collective-permute-done | bytes 1048608 | tf_op jit(solution)/shard_map/ppermute | solution.py:528
  388.8 2.6 add_convert_fusion.3
  398.7 19.2 %self_back.1 = (f32[448,1024]{1,0:T(8,128)}, bf16[448,1024]{1,0:T(8,128)(2,1)}, f32[8,1024]{1,0:T(8,128)}, bf16[448,1536]{1,0:T(8,128)(2,1)}, f32[8,512]{1,0:T(8,128)}, /*index=5*/bf16[448,1024]{1,0:T(8,128)(2,1)}) custom-call(s32[2]{0:T(128)} %pad_add_fusion.g_ref, bf16[448,1024]{1,0:T(8,128)(2,1)} %get-tuple-element.125.own, ...), custom_call_target="tpu_custom_call" | custom-call | flops 3934257152 | bytes 17272840 | tf_op jit(solution)/shard_map/self_back/pallas_call | solution.py:33
  434.3 7.3 %self_grads.1 = (bf16[2,256,512]{2,1,0:T(8,128)(2,1)}, bf16[2,256,512]{2,1,0:T(8,128)(2,1)}, bf16[2,256,512]{2,1,0:T(8,128)(2,1)}, bf16[2,256,512]{2,1,0:T(8,128...) custom-call(s32[2]{0:T(128)} %pad_add_fusion.g_ref, ...), custom_call_target="tpu_custom_call" | custom-call | flops 1879048192 | bytes 7864328 | tf_op jit(solution)/shard_map/self_grads/pallas_call | solution.py:33
  442.4 2.9 collective-permute-start.83
  445.2 30.1 %collective-permute-done.55 = bf16[384,512]{1,0:T(8,128)(2,1)} collective-permute-done((bf16[384,512]{1,0:T(8,128)(2,1)}, bf16[384,512]{1,0:T(8,128)(2,1)}, u32[]{:S(2)}, u32[]{:S(2)}) %collective-permute-start.55) | collective-permute-done | bytes 393248 | tf_op jit(solution)/shard_map/ppermute | solution.py:532
  476.3 18.5 %collective-permute-done.56 = bf16[384,512]{1,0:T(8,128)(2,1)S(1)} collective-permute-done((bf16[384,512]{1,0:T(8,128)(2,1)}, bf16[384,512]{1,0:T(8,128)(2,1)S(1)}, u32[]{:S(2)}, u32[]{:S(2)}) %collective-permute-start.56) | collective-permute-done | bytes 393248 | tf_op jit(solution)/shard_map/ppermute | solution.py:532
  502.8 5.9 start_back.1
  511.4 11.8 %collective-permute-start.50 = (bf16[224,1024]{1,0:T(8,128)(2,1)}, bf16[224,1024]{1,0:T(8,128)(2,1)}, u32[]{:S(2)}, u32[]{:S(2)}) collective-permute-start(bf16[224,1024]{1,0:T(8,128)(2,1)} %constant_dynamic-slice_fusion.31), channel_id=1, source_target_pairs={{0,1},{1,2},{2,3},{3,0},{4,5},{5,6},{6,7},{7,4},{8,9},{9,10},{10,1... | collective-permute-start | bytes 1376264 | tf_op jit(solution)/shard_map/ppermute | solution.py:532
  523.3 9.1 %collective-permute-start.51 = (bf16[224,1024]{1,0:T(8,128)(2,1)}, bf16[224,1024]{1,0:T(8,128)(2,1)}, u32[]{:S(2)}, u32[]{:S(2)}) collective-permute-start(bf16[224,1024]{1,0:T(8,128)(2,1)} %constant_dynamic-slice_fusion.31), channel_id=1, source_target_pairs={{0,2},{1,3},{2,0},{3,1},{4,6},{5,7},{6,4},{7,5},{8,10},{9,11},{10,... | collective-permute-start | bytes 1376264 | tf_op jit(solution)/shard_map/ppermute | solution.py:532
  533.7 3.3 collective-permute-start.52
  553.5 3.8 collective-permute-done.69
  562.0 6.3 collective-permute-start.71
  568.3 2.6 collective-permute-done.71
  574.0 2.7 copy.53
  588.6 5.7 collective-permute-done.75
  608.1 2.5 collective-permute-start.61
  611.8 3.7 collective-permute-start.65
  615.4 16.2 %collective-permute-done.80 = bf16[256,512]{1,0:T(8,128)(2,1)} collective-permute-done((bf16[256,512]{1,0:T(8,128)(2,1)}, bf16[256,512]{1,0:T(8,128)(2,1)}, u32[]{:S(2)}, u32[]{:S(2)}) %collective-permute-start.80) | collective-permute-done | bytes 262176 | tf_op jit(solution)/shard_map/ppermute | solution.py:532
  633.1 10.6 %collective-permute-done.65 = bf16[256,512]{1,0:T(8,128)(2,1)S(1)} collective-permute-done((bf16[256,512]{1,0:T(8,128)(2,1)S(1)}, bf16[256,512]{1,0:T(8,128)(2,1)S(1)}, u32[]{:S(2)}, u32[]{:S(2)}) %collective-permute-start.65) | collective-permute-done | bytes 262176 | tf_op jit(solution)/shard_map/ppermute | solution.py:532
  648.6 2.8 maximum_select_fusion.1
  (419 shorter events, 197.6 us)
Async XLA Ops:
  50.5 25.4 %collective-permute-start.8 = (bf16[2,288,512]{2,1,0:T(8,128)(2,1)}, bf16[2,288,512]{2,1,0:T(8,128)(2,1)}, u32[]{:S(2)}, u32[]{:S(2)}) collective-permute-start(bf16[2,288,512]{2,1,0:T(8,128)(2,1)} %pad_maximum_fusion.13.refs_4_), channel_id=1, source_target_pairs={{0,16},{4,20},{8,24},{12,28},{16,0},{20,4},{24,8},{28,12},{1,17},{... | collective-permute-start | bytes 1769480 | tf_op jit(solution)/shard_map/ppermute | solution.py:528
  67.3 26.3 %collective-permute-start.1 = (bf16[448,1024]{1,0:T(8,128)(2,1)}, bf16[448,1024]{1,0:T(8,128)(2,1)}, u32[]{:S(2)}, u32[]{:S(2)}) collective-permute-start(bf16[448,1024]{1,0:T(8,128)(2,1)} %dynamic-slice_bitcast_fusion.2), channel_id=1, source_target_pairs={{0,4},{4,0},{8,12},{12,8},{16,20},{20,16},{24,28},{28,24},{1,5},{5... | collective-permute-start | bytes 2752520 | tf_op jit(solution)/shard_map/ppermute | solution.py:528
  75.9 38.1 %collective-permute-start.27 = (bf16[256,1024]{1,0:T(8,128)(2,1)S(1)}, bf16[256,1024]{1,0:T(8,128)(2,1)S(1)}, u32[]{:S(2)}, u32[]{:S(2)}) collective-permute-start(bf16[256,1024]{1,0:T(8,128)(2,1)S(1)} %maximum_select_fusion.2), channel_id=1, source_target_pairs={{0,2},{1,3},{2,0},{3,1},{4,6},{5,7},{6,4},{7,5},{8,10},{9,11},{10,... | collective-permute-start | bytes 1572872 | tf_op jit(solution)/shard_map/ppermute | solution.py:532
  79.4 35.1 %collective-permute-start.28 = (bf16[256,1024]{1,0:T(8,128)(2,1)S(1)}, bf16[256,1024]{1,0:T(8,128)(2,1)}, u32[]{:S(2)}, u32[]{:S(2)}) collective-permute-start(bf16[256,1024]{1,0:T(8,128)(2,1)S(1)} %maximum_select_fusion.2), channel_id=1, source_target_pairs={{0,3},{1,0},{2,1},{3,2},{4,7},{5,4},{6,5},{7,6},{8,11},{9,8},{10,9... | collective-permute-start | bytes 1572872 | tf_op jit(solution)/shard_map/ppermute | solution.py:532
  79.4 36.5 %collective-permute-start.17 = (bf16[2,256,512]{2,1,0:T(8,128)(2,1)}, bf16[2,256,512]{2,1,0:T(8,128)(2,1)}, u32[]{:S(2)}, u32[]{:S(2)}) collective-permute-start(bf16[2,256,512]{2,1,0:T(8,128)(2,1)} %pad_maximum_fusion.14.refs_0_), channel_id=1, source_target_pairs={{0,8},{4,12},{8,0},{12,4},{16,24},{20,28},{24,16},{28,20},{1,9},{5... | collective-permute-start | bytes 1572872 | tf_op jit(solution)/shard_map/ppermute | solution.py:528
  93.6 27.2 %collective-permute-start.18 = (bf16[2,256,512]{2,1,0:T(8,128)(2,1)}, bf16[2,256,512]{2,1,0:T(8,128)(2,1)S(1)}, u32[]{:S(2)}, u32[]{:S(2)}) collective-permute-start(bf16[2,256,512]{2,1,0:T(8,128)(2,1)} %pad_maximum_fusion.14.refs_0_), channel_id=1, source_target_pairs={{0,16},{4,20},{8,24},{12,28},{16,0},{20,4},{24,8},{28,12},{1,17},{... | collective-permute-start | bytes 1572872 | tf_op jit(solution)/shard_map/ppermute | solution.py:528
  115.9 25.4 %collective-permute-start.9 = (bf16[2,288,512]{2,1,0:T(8,128)(2,1)S(1)}, bf16[2,288,512]{2,1,0:T(8,128)(2,1)S(1)}, u32[]{:S(2)}, u32[]{:S(2)}) collective-permute-start(bf16[2,288,512]{2,1,0:T(8,128)(2,1)S(1)} %copy-done.37), channel_id=1, source_target_pairs={{0,16},{4,20},{8,24},{12,28},{16,0},{20,4},{24,8},{28,12},{1,17},{... | collective-permute-start | bytes 1769480 | tf_op jit(solution)/shard_map/ppermute | solution.py:528
  120.8 54.9 %collective-permute-start.12 = (bf16[1500,1024]{1,0:T(8,128)(2,1)}, bf16[1500,1024]{1,0:T(8,128)(2,1)}, u32[]{:S(2)}, u32[]{:S(2)}) collective-permute-start(bf16[1500,1024]{1,0:T(8,128)(2,1)} %dynamic-slice_bitcast_fusion), channel_id=1, source_target_pairs={{0,4},{4,0},{8,12},{12,8},{16,20},{20,16},{24,28},{28,24},{1,5},{5... | collective-permute-start | bytes 9216008 | tf_op jit(solution)/shard_map/ppermute | solution.py:528
  120.8 98.1 %collective-permute-start.24 = (bf16[448,1024]{1,0:T(8,128)(2,1)}, bf16[448,1024]{1,0:T(8,128)(2,1)}, u32[]{:S(2)}, u32[]{:S(2)}) collective-permute-start(bf16[448,1024]{1,0:T(8,128)(2,1)} %dynamic-slice_bitcast_fusion.1), channel_id=1, source_target_pairs={{0,4},{4,0},{8,12},{12,8},{16,20},{20,16},{24,28},{28,24},{1,5},{5... | collective-permute-start | bytes 2752520 | tf_op jit(solution)/shard_map/ppermute | solution.py:528
  128.7 69.9 %collective-permute-start.29 = (bf16[4,256,512]{2,1,0:T(8,128)(2,1)}, bf16[4,256,512]{2,1,0:T(8,128)(2,1)}, u32[]{:S(2)}, u32[]{:S(2)}) collective-permute-start(bf16[4,256,512]{2,1,0:T(8,128)(2,1)} %pad_maximum_fusion.7.refs_0_), channel_id=1, source_target_pairs={{0,8},{4,12},{8,0},{12,4},{16,24},{20,28},{24,16},{28,20},{1,9},{5... | collective-permute-start | bytes 3145736 | tf_op jit(solution)/shard_map/ppermute | solution.py:528
  130.2 70.0 %collective-permute-start.33 = (bf16[4,256,512]{2,1,0:T(8,128)(2,1)}, bf16[4,256,512]{2,1,0:T(8,128)(2,1)}, u32[]{:S(2)}, u32[]{:S(2)}) collective-permute-start(bf16[4,256,512]{2,1,0:T(8,128)(2,1)} %pad_maximum_fusion.8.refs_4_), channel_id=1, source_target_pairs={{0,16},{4,20},{8,24},{12,28},{16,0},{20,4},{24,8},{28,12},{1,17},{... | collective-permute-start | bytes 3145736 | tf_op jit(solution)/shard_map/ppermute | solution.py:528
  141.4 32.9 %collective-permute-start.19 = (bf16[2,256,512]{2,1,0:T(8,128)(2,1)}, bf16[2,256,512]{2,1,0:T(8,128)(2,1)}, u32[]{:S(2)}, u32[]{:S(2)}) collective-permute-start(bf16[2,256,512]{2,1,0:T(8,128)(2,1)} %collective-permute-done.17.refs_1_), channel_id=1, source_target_pairs={{0,16},{4,20},{8,24},{12,28},{16,0},{20,4},{24,8},{28,12},{1,17},{... | collective-permute-start | bytes 1572872 | tf_op jit(solution)/shard_map/ppermute | solution.py:528
  187.6 34.4 %collective-permute-start.30 = (bf16[4,256,512]{2,1,0:T(8,128)(2,1)}, bf16[4,256,512]{2,1,0:T(8,128)(2,1)}, u32[]{:S(2)}, u32[]{:S(2)}) collective-permute-start(bf16[4,256,512]{2,1,0:T(8,128)(2,1)} %pad_maximum_fusion.7.refs_0_), channel_id=1, source_target_pairs={{0,16},{4,20},{8,24},{12,28},{16,0},{20,4},{24,8},{28,12},{1,17},{... | collective-permute-start | bytes 3145736 | tf_op jit(solution)/shard_map/ppermute | solution.py:528
  197.2 26.3 %collective-permute-start.32 = (bf16[4,256,512]{2,1,0:T(8,128)(2,1)}, bf16[4,256,512]{2,1,0:T(8,128)(2,1)}, u32[]{:S(2)}, u32[]{:S(2)}) collective-permute-start(bf16[4,256,512]{2,1,0:T(8,128)(2,1)} %pad_maximum_fusion.8.refs_4_), channel_id=1, source_target_pairs={{0,8},{4,12},{8,0},{12,4},{16,24},{20,28},{24,16},{28,20},{1,9},{5... | collective-permute-start | bytes 3145736 | tf_op jit(solution)/shard_map/ppermute | solution.py:528
  198.7 35.1 %collective-permute-start.31 = (bf16[4,256,512]{2,1,0:T(8,128)(2,1)}, bf16[4,256,512]{2,1,0:T(8,128)(2,1)}, u32[]{:S(2)}, u32[]{:S(2)}) collective-permute-start(bf16[4,256,512]{2,1,0:T(8,128)(2,1)} %collective-permute-done.29.refs_1_), channel_id=1, source_target_pairs={{0,16},{4,20},{8,24},{12,28},{16,0},{20,4},{24,8},{28,12},{1,17},{... | collective-permute-start | bytes 3145736 | tf_op jit(solution)/shard_map/ppermute | solution.py:528
  200.2 42.9 %collective-permute-start.34 = (bf16[4,256,512]{2,1,0:T(8,128)(2,1)}, bf16[4,256,512]{2,1,0:T(8,128)(2,1)}, u32[]{:S(2)}, u32[]{:S(2)}) collective-permute-start(bf16[4,256,512]{2,1,0:T(8,128)(2,1)} %collective-permute-done.33.refs_6_), channel_id=1, source_target_pairs={{0,8},{4,12},{8,0},{12,4},{16,24},{20,28},{24,16},{28,20},{1,9},{5... | collective-permute-start | bytes 3145736 | tf_op jit(solution)/shard_map/ppermute | solution.py:528
  266.2 71.0 %collective-permute-start.44 = (bf16[4,256,512]{2,1,0:T(8,128)(2,1)}, bf16[4,256,512]{2,1,0:T(8,128)(2,1)}, u32[]{:S(2)}, u32[]{:S(2)}) collective-permute-start(bf16[4,256,512]{2,1,0:T(8,128)(2,1)} %get-tuple-element.136), channel_id=1, source_target_pairs={{0,8},{4,12},{8,0},{12,4},{16,24},{20,28},{24,16},{28,20},{1,9},{5... | collective-permute-start | bytes 3145736 | tf_op jit(solution)/shard_map/ppermute | solution.py:528
  267.7 71.2 %collective-permute-start.45 = (bf16[4,256,512]{2,1,0:T(8,128)(2,1)}, bf16[4,256,512]{2,1,0:T(8,128)(2,1)}, u32[]{:S(2)}, u32[]{:S(2)}) collective-permute-start(bf16[4,256,512]{2,1,0:T(8,128)(2,1)} %get-tuple-element.137), channel_id=1, source_target_pairs={{0,8},{4,12},{8,0},{12,4},{16,24},{20,28},{24,16},{28,20},{1,9},{5... | collective-permute-start | bytes 3145736 | tf_op jit(solution)/shard_map/ppermute | solution.py:528
  276.1 64.1 %collective-permute-start.36 = (bf16[224,1024]{1,0:T(8,128)(2,1)}, bf16[224,1024]{1,0:T(8,128)(2,1)}, u32[]{:S(2)}, u32[]{:S(2)}) collective-permute-start(bf16[224,1024]{1,0:T(8,128)(2,1)} %constant_dynamic-slice_fusion.36), channel_id=1, source_target_pairs={{0,1},{1,2},{2,3},{3,0},{4,5},{5,6},{6,7},{7,4},{8,9},{9,10},{10,1... | collective-permute-start | bytes 1376264 | tf_op jit(solution)/shard_map/ppermute | solution.py:532
  283.8 56.6 %collective-permute-start.37 = (bf16[224,1024]{1,0:T(8,128)(2,1)}, bf16[224,1024]{1,0:T(8,128)(2,1)}, u32[]{:S(2)}, u32[]{:S(2)}) collective-permute-start(bf16[224,1024]{1,0:T(8,128)(2,1)} %constant_dynamic-slice_fusion.36), channel_id=1, source_target_pairs={{0,2},{1,3},{2,0},{3,1},{4,6},{5,7},{6,4},{7,5},{8,10},{9,11},{10,... | collective-permute-start | bytes 1376264 | tf_op jit(solution)/shard_map/ppermute | solution.py:532
  286.9 54.0 %collective-permute-start.38 = (bf16[224,1024]{1,0:T(8,128)(2,1)}, bf16[224,1024]{1,0:T(8,128)(2,1)}, u32[]{:S(2)}, u32[]{:S(2)}) collective-permute-start(bf16[224,1024]{1,0:T(8,128)(2,1)} %constant_dynamic-slice_fusion.36), channel_id=1, source_target_pairs={{0,3},{1,0},{2,1},{3,2},{4,7},{5,4},{6,5},{7,6},{8,11},{9,8},{10,9... | collective-permute-start | bytes 1376264 | tf_op jit(solution)/shard_map/ppermute | solution.py:532
  337.3 26.3 %collective-permute-start.42 = (bf16[4,256,512]{2,1,0:T(8,128)(2,1)}, bf16[4,256,512]{2,1,0:T(8,128)(2,1)S(1)}, u32[]{:S(2)}, u32[]{:S(2)}) collective-permute-start(bf16[4,256,512]{2,1,0:T(8,128)(2,1)} %get-tuple-element.127), channel_id=1, source_target_pairs={{0,16},{4,20},{8,24},{12,28},{16,0},{20,4},{24,8},{28,12},{1,17},{... | collective-permute-start | bytes 3145736 | tf_op jit(solution)/shard_map/ppermute | solution.py:528
  338.9 47.2 %collective-permute-start.43 = (bf16[4,256,512]{2,1,0:T(8,128)(2,1)}, bf16[4,256,512]{2,1,0:T(8,128)(2,1)S(1)}, u32[]{:S(2)}, u32[]{:S(2)}) collective-permute-start(bf16[4,256,512]{2,1,0:T(8,128)(2,1)} %get-tuple-element.128), channel_id=1, source_target_pairs={{0,16},{4,20},{8,24},{12,28},{16,0},{20,4},{24,8},{28,12},{1,17},{... | collective-permute-start | bytes 3145736 | tf_op jit(solution)/shard_map/ppermute | solution.py:528
  340.3 55.8 %collective-permute-start.46 = (bf16[1536,512]{1,0:T(8,128)(2,1)}, bf16[1536,512]{1,0:T(8,128)(2,1)S(1)}, u32[]{:S(2)}, u32[]{:S(2)}) collective-permute-start(bf16[1536,512]{1,0:T(8,128)(2,1)} %get-tuple-element.139), channel_id=1, source_target_pairs={{0,4},{4,0},{8,12},{12,8},{16,20},{20,16},{24,28},{28,24},{1,5},{5... | collective-permute-start | bytes 4718600 | tf_op jit(solution)/shard_map/ppermute | solution.py:528
  340.3 57.9 %collective-permute-start.41 = (bf16[448,1024]{1,0:T(8,128)(2,1)}, bf16[448,1024]{1,0:T(8,128)(2,1)}, u32[]{:S(2)}, u32[]{:S(2)}) collective-permute-start(bf16[448,1024]{1,0:T(8,128)(2,1)} %get-tuple-element.125.own), channel_id=1, source_target_pairs={{0,4},{4,0},{8,12},{12,8},{16,20},{20,16},{24,28},{28,24},{1,5},{5... | collective-permute-start | bytes 2752520 | tf_op jit(solution)/shard_map/ppermute | solution.py:528
  342.7 50.0 %collective-permute-start.39 = (bf16[2,224,1024]{2,1,0:T(8,128)(2,1)S(1)}, bf16[2,224,1024]{2,1,0:T(8,128)(2,1)S(1)}, u32[]{:S(2)}, u32[]{:S(2)}) collective-permute-start(bf16[2,224,1024]{2,1,0:T(8,128)(2,1)S(1)} %pad_maximum_fusion.9), channel_id=1, source_target_pairs={{0,4},{4,0},{8,12},{12,8},{16,20},{20,16},{24,28},{28,24},{1,5},{5... | collective-permute-start | bytes 2752520 | tf_op jit(solution)/shard_map/ppermute | solution.py:528
  363.6 65.9 %collective-permute-start.73 = (bf16[2,256,512]{2,1,0:T(8,128)(2,1)}, bf16[2,256,512]{2,1,0:T(8,128)(2,1)S(1)}, u32[]{:S(2)}, u32[]{:S(2)}) collective-permute-start(bf16[2,256,512]{2,1,0:T(8,128)(2,1)} %get-tuple-element.178), channel_id=1, source_target_pairs={{0,16},{4,20},{8,24},{12,28},{16,0},{20,4},{24,8},{28,12},{1,17},{... | collective-permute-start | bytes 1572872 | tf_op jit(solution)/shard_map/ppermute | solution.py:528
  386.1 33.8 %collective-permute-start.49 = (bf16[4,256,512]{2,1,0:T(8,128)(2,1)}, bf16[4,256,512]{2,1,0:T(8,128)(2,1)}, u32[]{:S(2)}, u32[]{:S(2)}) collective-permute-start(bf16[4,256,512]{2,1,0:T(8,128)(2,1)} %add_convert_fusion.1), channel_id=1, source_target_pairs={{0,16},{4,20},{8,24},{12,28},{16,0},{20,4},{24,8},{28,12},{1,17},{... | collective-permute-start | bytes 3145736 | tf_op jit(solution)/shard_map/ppermute | solution.py:528
  392.7 27.2 %collective-permute-start.48 = (bf16[4,256,512]{2,1,0:T(8,128)(2,1)}, bf16[4,256,512]{2,1,0:T(8,128)(2,1)}, u32[]{:S(2)}, u32[]{:S(2)}) collective-permute-start(bf16[4,256,512]{2,1,0:T(8,128)(2,1)} %add_convert_fusion.2), channel_id=1, source_target_pairs={{0,8},{4,12},{8,0},{12,4},{16,24},{20,28},{24,16},{28,20},{1,9},{5... | collective-permute-start | bytes 3145736 | tf_op jit(solution)/shard_map/ppermute | solution.py:528
  396.1 35.3 %collective-permute-start.74 = (bf16[2,256,512]{2,1,0:T(8,128)(2,1)}, bf16[2,256,512]{2,1,0:T(8,128)(2,1)}, u32[]{:S(2)}, u32[]{:S(2)}) collective-permute-start(bf16[2,256,512]{2,1,0:T(8,128)(2,1)} %get-tuple-element.179), channel_id=1, source_target_pairs={{0,16},{4,20},{8,24},{12,28},{16,0},{20,4},{24,8},{28,12},{1,17},{... | collective-permute-start | bytes 1572872 | tf_op jit(solution)/shard_map/ppermute | solution.py:528
  398.2 35.4 %collective-permute-start.77 = (bf16[2,256,512]{2,1,0:T(8,128)(2,1)}, bf16[2,256,512]{2,1,0:T(8,128)(2,1)}, u32[]{:S(2)}, u32[]{:S(2)}) collective-permute-start(bf16[2,256,512]{2,1,0:T(8,128)(2,1)} %get-tuple-element.184), channel_id=1, source_target_pairs={{0,8},{4,12},{8,0},{12,4},{16,24},{20,28},{24,16},{28,20},{1,9},{5... | collective-permute-start | bytes 1572872 | tf_op jit(solution)/shard_map/ppermute | solution.py:528
  419.9 80.4 %collective-permute-start.47 = (bf16[448,1024]{1,0:T(8,128)(2,1)}, bf16[448,1024]{1,0:T(8,128)(2,1)}, u32[]{:S(2)}, u32[]{:S(2)}) collective-permute-start(bf16[448,1024]{1,0:T(8,128)(2,1)} %get-tuple-element.145.own), channel_id=1, source_target_pairs={{0,4},{4,0},{8,12},{12,8},{16,20},{20,16},{24,28},{28,24},{1,5},{5... | collective-permute-start | bytes 2752520 | tf_op jit(solution)/shard_map/ppermute | solution.py:528
  429.5 45.8 %collective-permute-start.55 = (bf16[384,512]{1,0:T(8,128)(2,1)}, bf16[384,512]{1,0:T(8,128)(2,1)}, u32[]{:S(2)}, u32[]{:S(2)}) collective-permute-start(bf16[384,512]{1,0:T(8,128)(2,1)} %get-tuple-element.246), channel_id=1, source_target_pairs={{0,2},{1,3},{2,0},{3,1},{4,6},{5,7},{6,4},{7,5},{8,10},{9,11},{10,... | collective-permute-start | bytes 1179656 | tf_op jit(solution)/shard_map/ppermute | solution.py:532
  431.4 64.9 %collective-permute-start.85 = (bf16[256,1024]{1,0:T(8,128)(2,1)}, bf16[256,1024]{1,0:T(8,128)(2,1)}, u32[]{:S(2)}, u32[]{:S(2)}) collective-permute-start(bf16[256,1024]{1,0:T(8,128)(2,1)} %pad_maximum_fusion.19), channel_id=1, source_target_pairs={{0,1},{1,2},{2,3},{3,0},{4,5},{5,6},{6,7},{7,4},{8,9},{9,10},{10,1... | collective-permute-start | bytes 1572872 | tf_op jit(solution)/shard_map/ppermute | solution.py:532
  433.6 64.2 %collective-permute-start.84 = (bf16[256,1024]{1,0:T(8,128)(2,1)}, bf16[256,1024]{1,0:T(8,128)(2,1)}, u32[]{:S(2)}, u32[]{:S(2)}) collective-permute-start(bf16[256,1024]{1,0:T(8,128)(2,1)} %pad_maximum_fusion.18), channel_id=1, source_target_pairs={{0,2},{1,3},{2,0},{3,1},{4,6},{5,7},{6,4},{7,5},{8,10},{9,11},{10,... | collective-permute-start | bytes 1572872 | tf_op jit(solution)/shard_map/ppermute | solution.py:532
  442.4 57.3 %collective-permute-start.83 = (bf16[256,1024]{1,0:T(8,128)(2,1)}, bf16[256,1024]{1,0:T(8,128)(2,1)S(1)}, u32[]{:S(2)}, u32[]{:S(2)}) collective-permute-start(bf16[256,1024]{1,0:T(8,128)(2,1)} %pad_maximum_fusion.17), channel_id=1, source_target_pairs={{0,3},{1,0},{2,1},{3,2},{4,7},{5,4},{6,5},{7,6},{8,11},{9,8},{10,9... | collective-permute-start | bytes 1572872 | tf_op jit(solution)/shard_map/ppermute | solution.py:532
  497.8 25.4 %collective-permute-start.59 = (bf16[2,256,512]{2,1,0:T(8,128)(2,1)}, bf16[2,256,512]{2,1,0:T(8,128)(2,1)}, u32[]{:S(2)}, u32[]{:S(2)}) collective-permute-start(bf16[2,256,512]{2,1,0:T(8,128)(2,1)} %get-tuple-element.161), channel_id=1, source_target_pairs={{0,16},{4,20},{8,24},{12,28},{16,0},{20,4},{24,8},{28,12},{1,17},{... | collective-permute-start | bytes 1572872 | tf_op jit(solution)/shard_map/ppermute | solution.py:528
  499.7 34.0 %collective-permute-start.62 = (bf16[2,256,512]{2,1,0:T(8,128)(2,1)}, bf16[2,256,512]{2,1,0:T(8,128)(2,1)}, u32[]{:S(2)}, u32[]{:S(2)}) collective-permute-start(bf16[2,256,512]{2,1,0:T(8,128)(2,1)} %get-tuple-element.166), channel_id=1, source_target_pairs={{0,8},{4,12},{8,0},{12,4},{16,24},{20,28},{24,16},{28,20},{1,9},{5... | collective-permute-start | bytes 1572872 | tf_op jit(solution)/shard_map/ppermute | solution.py:528
  500.3 36.8 %collective-permute-start.63 = (bf16[2,256,512]{2,1,0:T(8,128)(2,1)}, bf16[2,256,512]{2,1,0:T(8,128)(2,1)}, u32[]{:S(2)}, u32[]{:S(2)}) collective-permute-start(bf16[2,256,512]{2,1,0:T(8,128)(2,1)} %get-tuple-element.167), channel_id=1, source_target_pairs={{0,8},{4,12},{8,0},{12,4},{16,24},{20,28},{24,16},{28,20},{1,9},{5... | collective-permute-start | bytes 1572872 | tf_op jit(solution)/shard_map/ppermute | solution.py:528
  510.5 60.4 %collective-permute-start.57 = (bf16[2,384,512]{2,1,0:T(8,128)(2,1)}, bf16[2,384,512]{2,1,0:T(8,128)(2,1)}, u32[]{:S(2)}, u32[]{:S(2)}) collective-permute-start(bf16[2,384,512]{2,1,0:T(8,128)(2,1)} %pad_maximum_fusion.11), channel_id=1, source_target_pairs={{0,4},{4,0},{8,12},{12,8},{16,20},{20,16},{24,28},{28,24},{1,5},{5... | collective-permute-start | bytes 2359304 | tf_op jit(solution)/shard_map/ppermute | solution.py:528
  511.4 71.9 %collective-permute-start.50 = (bf16[224,1024]{1,0:T(8,128)(2,1)}, bf16[224,1024]{1,0:T(8,128)(2,1)}, u32[]{:S(2)}, u32[]{:S(2)}) collective-permute-start(bf16[224,1024]{1,0:T(8,128)(2,1)} %constant_dynamic-slice_fusion.31), channel_id=1, source_target_pairs={{0,1},{1,2},{2,3},{3,0},{4,5},{5,6},{6,7},{7,4},{8,9},{9,10},{10,1... | collective-permute-start | bytes 1376264 | tf_op jit(solution)/shard_map/ppermute | solution.py:532
  523.3 61.6 %collective-permute-start.51 = (bf16[224,1024]{1,0:T(8,128)(2,1)}, bf16[224,1024]{1,0:T(8,128)(2,1)}, u32[]{:S(2)}, u32[]{:S(2)}) collective-permute-start(bf16[224,1024]{1,0:T(8,128)(2,1)} %constant_dynamic-slice_fusion.31), channel_id=1, source_target_pairs={{0,2},{1,3},{2,0},{3,1},{4,6},{5,7},{6,4},{7,5},{8,10},{9,11},{10,... | collective-permute-start | bytes 1376264 | tf_op jit(solution)/shard_map/ppermute | solution.py:532
  533.7 51.7 %collective-permute-start.52 = (bf16[224,1024]{1,0:T(8,128)(2,1)}, bf16[224,1024]{1,0:T(8,128)(2,1)}, u32[]{:S(2)}, u32[]{:S(2)}) collective-permute-start(bf16[224,1024]{1,0:T(8,128)(2,1)} %constant_dynamic-slice_fusion.31), channel_id=1, source_target_pairs={{0,3},{1,0},{2,1},{3,2},{4,7},{5,4},{6,5},{7,6},{8,11},{9,8},{10,9... | collective-permute-start | bytes 1376264 | tf_op jit(solution)/shard_map/ppermute | solution.py:532
  570.9 30.1 %collective-permute-start.86 = (f32[128,1024]{1,0:T(8,128)}, f32[128,1024]{1,0:T(8,128)}, u32[]{:S(2)}, u32[]{:S(2)}) collective-permute-start(f32[128,1024]{1,0:T(8,128)} %constant_dynamic-slice_fusion.4), channel_id=1, source_target_pairs={{0,4},{4,0},{8,12},{12,8},{16,20},{20,16},{24,28},{28,24},{1,5},{5... | collective-permute-start | bytes 1572872 | tf_op jit(solution)/shard_map/ppermute | solution.py:528
  594.3 54.3 %collective-permute-start.53 = (bf16[2,224,1024]{2,1,0:T(8,128)(2,1)}, bf16[2,224,1024]{2,1,0:T(8,128)(2,1)}, u32[]{:S(2)}, u32[]{:S(2)}) collective-permute-start(bf16[2,224,1024]{2,1,0:T(8,128)(2,1)} %pad_maximum_fusion.10), channel_id=1, source_target_pairs={{0,4},{4,0},{8,12},{12,8},{16,20},{20,16},{24,28},{28,24},{1,5},{5... | collective-permute-start | bytes 2752520 | tf_op jit(solution)/shard_map/ppermute | solution.py:528
  601.0 30.6 %collective-permute-start.80 = (bf16[256,512]{1,0:T(8,128)(2,1)}, bf16[256,512]{1,0:T(8,128)(2,1)}, u32[]{:S(2)}, u32[]{:S(2)}) collective-permute-start(bf16[256,512]{1,0:T(8,128)(2,1)} %get-tuple-element.250), channel_id=1, source_target_pairs={{0,2},{1,3},{2,0},{3,1},{4,6},{5,7},{6,4},{7,5},{8,10},{9,11},{10,... | collective-permute-start | bytes 786440 | tf_op jit(solution)/shard_map/ppermute | solution.py:532
  604.1 27.5 %collective-permute-start.81 = (bf16[256,512]{1,0:T(8,128)(2,1)}, bf16[256,512]{1,0:T(8,128)(2,1)}, u32[]{:S(2)}, u32[]{:S(2)}) collective-permute-start(bf16[256,512]{1,0:T(8,128)(2,1)} %get-tuple-element.251), channel_id=1, source_target_pairs={{0,1},{1,2},{2,3},{3,0},{4,5},{5,6},{6,7},{7,4},{8,9},{9,10},{10,1... | collective-permute-start | bytes 786440 | tf_op jit(solution)/shard_map/ppermute | solution.py:532
  611.8 32.0 %collective-permute-start.65 = (bf16[256,512]{1,0:T(8,128)(2,1)S(1)}, bf16[256,512]{1,0:T(8,128)(2,1)S(1)}, u32[]{:S(2)}, u32[]{:S(2)}) collective-permute-start(bf16[256,512]{1,0:T(8,128)(2,1)S(1)} %get-tuple-element.252), channel_id=1, source_target_pairs={{0,2},{1,3},{2,0},{3,1},{4,6},{5,7},{6,4},{7,5},{8,10},{9,11},{10,... | collective-permute-start | bytes 786440 | tf_op jit(solution)/shard_map/ppermute | solution.py:532
  (83 other events, 1052.6 us)

commit v3 on v2

v3 whole, which is shorter than its diff:
```python
import functools
import math

import jax
import jax.numpy as jnp
from jax import lax
from jax.experimental import pallas as pl
from jax.experimental.pallas import tpu as pltpu
from jax.sharding import PartitionSpec as P

HEAD_DIM = 64
PAIR = 2 * HEAD_DIM
GROUPS = 4
EPSILON = 1e-05
MASKED = -1e9
SCALE = HEAD_DIM**-0.5
F32 = jnp.float32
BF16 = jnp.bfloat16
VMEM_LIMIT = 63 * 1024 * 1024
MESH = pl.DeviceIdType.MESH
NT = (((1,), (1,)), ((), ()))
TN = (((0,), (0,)), ((), ()))


def call(kernel, name, outs, args, scratch=(), flops=0, grid=None, specs=None, out_specs=None, remote=None, anywhere=(0, 0)):
    out_shape = [jax.ShapeDtypeStruct(shape, dtype) for shape, dtype in outs]
    moved = sum(a.size * a.dtype.itemsize for a in args) + sum(
        math.prod(o.shape) * jnp.dtype(o.dtype).itemsize for o in out_shape
    )
    extra = {}
    if grid is None:
        here, there = pl.BlockSpec(memory_space=pltpu.VMEM), pl.BlockSpec(memory_space=pl.ANY)
        extra["in_specs"] = [there if i < anywhere[0] else here for i in range(len(args))]
        extra["out_specs"] = [there if i < anywhere[1] else here for i in range(len(outs))]
    else:
        extra["grid"] = grid
        extra["in_specs"], extra["out_specs"] = specs(block_whole), out_specs(block_whole)
    if remote is None:
        params = pltpu.CompilerParams(vmem_limit_bytes=VMEM_LIMIT)
    else:
        params = pltpu.CompilerParams(vmem_limit_bytes=VMEM_LIMIT, collective_id=remote, has_side_effects=True)
    return pl.pallas_call(
        kernel,
        name=name,
        out_shape=out_shape,
        scratch_shapes=list(scratch),
        compiler_params=params,
        cost_estimate=pl.CostEstimate(flops=int(flops), bytes_accessed=int(moved), transcendentals=0),
        **extra,
    )(*args)


def block_whole(shape):
    return pl.BlockSpec(shape, lambda *_: (0,) * len(shape))


def dot(a, b, dims=None):
    if dims is None:
        return jnp.dot(a, b, preferred_element_type=F32)
    return lax.dot_general(a, b, dims, preferred_element_type=F32)


def fill(weights, buffer, columns):
    rows, held = buffer.shape[0] // GROUPS, weights.shape[1] // GROUPS
    for s in range(weights.shape[0]):
        for g in range(GROUPS):
            for which, at in columns:
                buffer[g * rows : (g + 1) * rows, at + s * PAIR : at + (s + 1) * PAIR] = weights[
                    s, g * held : g * held + rows, which * PAIR : (which + 1) * PAIR
                ]


def unfill(grads, which, value):
    for s in range(grads.shape[0]):
        grads[s, :, which * PAIR : (which + 1) * PAIR] = value[:, s * PAIR : (s + 1) * PAIR]


class Place:
    def __init__(self, sizes):
        n_f, self.n_t = sizes
        self.x_size, self.y_size = n_f // 4, n_f // 2
        self.f, self.z = lax.axis_index("fsdp"), lax.axis_index("tensor")
        self.core = self.f % 2
        self.group = self.f // self.x_size
        x, y = self.group % 2, self.group // 2
        self.to_x = self.f + (1 - 2 * x) * self.x_size
        self.to_y = self.f + (1 - 2 * y) * self.y_size
        self.to_core = self.f + 1 - 2 * self.core
        self.group_x = self.group + 1 - 2 * x
        self.group_y = self.group + 2 - 4 * y
        self.group_xy = 3 - self.group

    def device(self, f, z):
        return {"fsdp": f, "tensor": z}

    def x(self):
        return self.device(self.to_x, self.z)

    def y(self):
        return self.device(self.to_y, self.z)

    def barrier(self):
        sem = pltpu.get_barrier_semaphore()
        for f in (self.to_x, self.to_y, self.to_core):
            pl.semaphore_signal(sem, inc=1, device_id=self.device(f, self.z), device_id_type=MESH)
        for step in (-1, 1):

            @pl.when(self.has(self.z + step))
            def _():
                pl.semaphore_signal(sem, inc=1, device_id=self.device(self.f, self.z + step), device_id_type=MESH)

        pl.semaphore_wait(sem, 3 + jnp.where(self.z > 0, 1, 0) + jnp.where(self.z < self.n_t - 1, 1, 0))

    def has(self, z):
        return jnp.logical_and(z >= 0, z < self.n_t)


def remote(src, dst, sems, at, device):
    return pltpu.make_async_remote_copy(
        src_ref=src, dst_ref=dst, send_sem=sems[0].at[at], recv_sem=sems[1].at[at], device_id=device, device_id_type=MESH
    )


def sem_pair(*shape):
    return [pltpu.SemaphoreType.DMA(shape), pltpu.SemaphoreType.DMA(shape)]


class Gather:
    steps = 6

    @staticmethod
    def scratch(n_t):
        return [
            pltpu.SemaphoreType.DMA((2, n_t)), pltpu.SemaphoreType.DMA((n_t,)),
            *sem_pair(n_t, 6), pltpu.SemaphoreType.DMA,
        ]

    def __init__(self, place, own, whole, scratch):
        self.place, self.own, self.whole = place, own, whole
        self.z_send, self.z_recv, s, r, self.local = scratch
        self.xy = (s, r)

    def rows(self, slot, group, half=None):
        size = self.own.shape[0]
        if half is None:
            return self.whole.at[slot, pl.ds(pl.multiple_of(group * size, 16), size)]
        return self.whole.at[slot, pl.ds(pl.multiple_of(group * size + half * (size // 2), 16), size // 2)]

    def along_z(self, slot, step, mine=False):
        p = self.place
        to = self.rows(slot, p.group)
        return pltpu.make_async_remote_copy(
            src_ref=self.own if mine else to, dst_ref=to, send_sem=self.z_send.at[(step + 1) // 2, slot],
            recv_sem=self.z_recv.at[slot], device_id=p.device(p.f, p.z + step), device_id_type=MESH,
        )

    def copy(self, slot, at, mine=False):
        p, size = self.place, self.own.shape[0]
        if at < 4:
            half = (0, 1, 1, 0)[at]
            to = self.rows(slot, p.group, half)
            src = self.own.at[pl.ds(half * (size // 2), size // 2)] if mine else to
        else:
            src = to = self.rows(slot, p.group_y, 1) if at == 4 else self.rows(slot, p.group_x, 0)
        return remote(src, to, self.xy, (slot, at), p.x() if at in (0, 1, 4) else p.y())

    def send_xy(self, slot, mine=False):
        for at in (0, 2, 1, 3):
            self.copy(slot, at, mine).start()

    def forward_xy(self, slot):
        self.copy(slot, 0).wait_recv()
        self.copy(slot, 5).start()
        self.copy(slot, 2).wait_recv()
        self.copy(slot, 4).start()

    def arrived(self, r, act):
        p = self.place
        for step in (-1, 1):
            slot = p.z + step * r
            pl.when(p.has(slot))(functools.partial(act, slot, step))

    def run(self, k):
        p = self.place
        if k == 0:
            for step in (-1, 1):
                pl.when(p.has(p.z + step))(lambda step=step: self.along_z(p.z, step, True).start())
            self.send_xy(p.z, True)
            pltpu.make_async_copy(self.own, self.rows(p.z, p.group), self.local).start()
            return
        if k <= 3:

            def passed(slot, step):
                copy = self.along_z(slot, -step)
                copy.wait_recv()
                pl.when(p.has(p.z - step))(copy.start)
                self.send_xy(slot)

            self.arrived(k, passed)
        if k == 1:
            self.forward_xy(p.z)
        elif k <= 4:
            self.arrived(k - 1, lambda slot, step: self.forward_xy(slot))
        else:
            for slot in range(p.n_t):
                for at in (1, 3, 4, 5):
                    self.copy(slot, at).wait_recv()
                for at in range(6):
                    self.copy(slot, at).wait_send()
                for step in (-1, 1):
                    sent = jnp.logical_and(p.has(p.z + step), (p.z - slot) * step >= 0)
                    pl.when(sent)(self.along_z(slot, step).wait_send)
            pltpu.make_async_copy(self.own, self.rows(p.z, p.group), self.local).wait()


class Scatter:
    steps = 7

    @staticmethod
    def scratch(n_t, size, wide):
        half = size // 2
        return [
            pltpu.VMEM((n_t, 2, half, wide), BF16), pltpu.VMEM((n_t, 2, half, wide), BF16),
            pltpu.VMEM((n_t, half, wide), BF16), pltpu.VMEM((n_t, half, wide), BF16),
            pltpu.VMEM((n_t, size, wide), BF16), pltpu.VMEM((2, n_t, size, wide), BF16),
            *sem_pair(n_t, 6), *sem_pair(2, n_t),
        ]

    def __init__(self, place, grads, own, scratch):
        self.place, self.grads, self.own = place, grads, own
        self.came_y, self.came_x, self.last_x, self.last_y, self.sums, self.came_z, a, b, c, d = scratch
        self.xy, self.zs = (a, b), (c, d)
        self.half = own.shape[0] // 2

    def slot(self, k):
        z = self.place.z
        last = self.place.n_t - 1
        low = z * 2 <= last
        far, near = jnp.where(low, last, 0), jnp.where(low, 0, last)
        edge = jnp.logical_or(z == 0, z == last)
        inward = jnp.where(low, 1, -1)
        if k == 0:
            return far
        if k == last:
            return z
        if k == last - 1:
            return z + inward
        return jnp.where(edge, z + 2 * inward, near)

    def at(self, group, half):
        return pl.ds(pl.multiple_of((2 * group + half) * self.half, 16), self.half)

    def copy(self, slot, at):
        p, g = self.place, self.grads
        by_y = at in (0, 2, 5)
        if at < 4:
            half = 0 if by_y else 1
            group = p.group_xy if at < 2 else (p.group_y if by_y else p.group_x)
            came = self.came_y if by_y else self.came_x
            src, to = g.at[slot, self.at(group, half)], came.at[slot, 1 if at < 2 else 0]
        else:
            src = self.came_x.at[slot, 1] if by_y else self.came_y.at[slot, 1]
            to = self.last_y.at[slot] if by_y else self.last_x.at[slot]
        return remote(src, to, self.xy, (slot, at), p.y() if by_y else p.x())

    def along_z(self, slot, way):
        p = self.place
        return remote(
            self.sums.at[slot], self.came_z.at[way, slot], self.zs, (way, slot), p.device(p.f, p.z + 2 * way - 1)
        )

    def over(self, rows, body):
        step = 32

        def one(i, carry):
            body(pl.multiple_of(i * step, step), step)
            return carry

        lax.fori_loop(0, rows // step, one, 0)

    def first(self, slot):
        for at in range(4):
            self.copy(slot, at).start()

    def second(self, slot):
        p = self.place
        self.copy(slot, 0).wait_recv()
        self.copy(slot, 1).wait_recv()

        def body(at, step):
            to = pl.ds(at, step)
            for came, group, half in ((self.came_y, p.group_x, 0), (self.came_x, p.group_y, 1)):
                own = self.grads[slot, pl.ds(pl.multiple_of((2 * group + half) * self.half + at, step), step)]
                came[slot, 1, to] = add(came[slot, 1, to], own)

        self.over(self.half, body)
        self.copy(slot, 4).start()
        self.copy(slot, 5).start()

    def third(self, slot):
        p = self.place
        for at in (2, 3, 4, 5):
            self.copy(slot, at).wait_recv()

        def body(at, step):
            to = pl.ds(at, step)
            for came, last, half in ((self.came_y, self.last_x, 0), (self.came_x, self.last_y, 1)):
                own = self.grads[slot, pl.ds(pl.multiple_of((2 * p.group + half) * self.half + at, step), step)]
                total = own.astype(F32) + came[slot, 0, to].astype(F32) + last[slot, to].astype(F32)
                self.sums[slot, pl.ds(pl.multiple_of(half * self.half + at, step), step)] = total.astype(BF16)

        self.over(self.half, body)
        for way in range(2):
            step = 2 * way - 1

            @pl.when((slot - p.z) * step > 0)
            def _():
                @pl.when(p.has(p.z - step))
                def _():
                    self.along_z(slot, way).wait_recv()

                    def body(at, step):
                        to = pl.ds(at, step)
                        self.sums[slot, to] = add(self.sums[slot, to], self.came_z[way, slot, to])

                    self.over(2 * self.half, body)

                self.along_z(slot, way).start()

    def run(self, k):
        p = self.place
        n = p.n_t
        if k == 0:
            self.first(self.slot(0))
            self.first(self.slot(1))
            return
        if k <= n:
            self.second(self.slot(k - 1))
        if k + 1 < n:
            self.first(self.slot(k + 1))
        if 2 <= k <= n + 1:
            self.third(self.slot(k - 2))
        if k == n + 2:
            z = p.z

            def begin(at, step):
                to = pl.ds(at, step)
                self.own[to] = self.sums[z, to].astype(F32)

            self.over(2 * self.half, begin)
            for way in range(2):
                step = 2 * way - 1

                @pl.when(p.has(z - step))
                def _():
                    self.along_z(z, way).wait_recv()

                    def body(at, step):
                        to = pl.ds(at, step)
                        self.own[to] += self.came_z[way, z, to].astype(F32)

                    self.over(2 * self.half, body)

            for slot in range(n):
                for at in range(6):
                    self.copy(slot, at).wait_send()
                for way in range(2):
                    pl.when((slot - z) * (2 * way - 1) > 0)(self.along_z(slot, way).wait_send)


def hook_of(job, first):
    def hook(p, pairs):
        for k in range(pairs):
            pl.when(p == k)(functools.partial(job.run, first + k))

    return hook


def swap(place, part, came, sems):
    return pltpu.make_async_remote_copy(
        src_ref=part, dst_ref=came, send_sem=sems.at[0], recv_sem=sems.at[1],
        device_id=place.device(place.to_core, place.z), device_id_type=MESH,
    )


def row_step(m):
    return m // 4 if m % 64 == 0 else m


def over_rows(m, body):
    step = row_step(m)

    def run(i, carry):
        return body(pl.ds(pl.multiple_of(i * step, step), step), carry)

    return lambda carry: lax.fori_loop(0, m // step, run, carry)


def normal(values):
    centre = values - jnp.mean(values, axis=-1, keepdims=True)
    inverse = lax.rsqrt(jnp.mean(centre * centre, axis=-1, keepdims=True) + EPSILON)
    return centre * inverse, inverse


def norm_rows(value_at, gain, shift, normed, kept=None):
    gain_row, shift_row = gain[...], shift[...]

    def body(at, carry):
        value = value_at(at)
        if kept is not None:
            kept[at, :] = value
        normed[at, :] = (normal(value)[0] * gain_row + shift_row).astype(BF16)
        return carry

    over_rows(normed.shape[0], body)(0)


def norm_back_rows(own, came, values, gain, upstream, grad_ref, low_ref, sums):
    gain_row = gain[...]
    wide = values.shape[1]

    def body(at, carry):
        q = own[at, :].astype(F32) + came[at, :].astype(F32)
        n, inverse = normal(values[at, :].astype(F32))
        up = upstream[at, :].astype(F32)
        v = q * gain_row
        back = inverse * (v - jnp.mean(v, axis=-1, keepdims=True) - n * jnp.mean(v * n, axis=-1, keepdims=True))
        grad = up + back
        grad_ref[at, :] = grad.astype(grad_ref.dtype)
        if low_ref is not None:
            low_ref[at, :] = grad.astype(BF16)
        terms = (q * n, q, grad, up)
        return tuple(c + jnp.sum(t, axis=0, keepdims=True) for c, t in zip(carry, terms))

    totals = over_rows(values.shape[0], body)(tuple(jnp.zeros((1, wide), F32) for _ in range(4)))
    row = lax.broadcasted_iota(jnp.int32, sums.shape, 0)
    value = jnp.zeros(sums.shape, F32)
    for at, total in enumerate(totals):
        value = jnp.where(row == at, total, value)
    sums[...] = value


def lane_mask(shape, h):
    return (lax.broadcasted_iota(jnp.int32, shape, 1) // HEAD_DIM) == h


def mask_scores(scores, causal, valid):
    size = scores.shape[0]
    if causal:
        key_at = lax.broadcasted_iota(jnp.int32, scores.shape, 0)
        query_at = lax.broadcasted_iota(jnp.int32, scores.shape, 1)
        return jnp.where(key_at <= query_at, scores, MASKED)
    if valid < size:
        edge = valid // 8 * 8
        tail = scores[edge:, :]
        key_at = lax.broadcasted_iota(jnp.int32, tail.shape, 0) + edge
        return jnp.concatenate([scores[:edge, :], jnp.where(key_at < valid, tail, -jnp.inf)], axis=0)
    return scores


def attend(q_ref, k_ref, v_ref, mixed_ref, log_ref, score_buf, causal, blocks, valid, hook):
    size = k_ref.shape[0] // blocks
    pairs = q_ref.shape[1] // PAIR

    def one_pair(p, carry):
        at = pl.ds(pl.multiple_of(p * PAIR, PAIR), PAIR)
        q_all = q_ref[:, at].astype(F32) * SCALE
        result = None
        for h in range(2):
            queries = jnp.where(lane_mask(q_all.shape, h), q_all, 0.0).astype(BF16)
            top = None
            for i in range(blocks):
                rows = slice(i * size, (i + 1) * size)
                scores = mask_scores(dot(k_ref[rows, at], queries, NT), causal, valid)
                score_buf[rows, :] = scores
                now = jnp.max(scores, axis=0, keepdims=True)
                top = now if top is None else jnp.maximum(top, now)
            total, mixed = None, None
            for i in range(blocks):
                rows = slice(i * size, (i + 1) * size)
                raised = jnp.exp(score_buf[rows, :] - top)
                now = jnp.sum(raised, axis=0, keepdims=True)
                total = now if total is None else total + now
                now = dot(v_ref[rows, at], raised.astype(BF16), TN)
                mixed = now if mixed is None else mixed + now
            log_ref[2 * p + h] = jnp.broadcast_to(top + jnp.log(total), log_ref.shape[1:])
            mixed = mixed / total
            if result is None:
                result = mixed
            else:
                row = lax.broadcasted_iota(jnp.int32, mixed.shape, 0)
                result = jnp.where(row < HEAD_DIM, result, mixed)
        mixed_ref[:, at] = jnp.transpose(result).astype(BF16)
        hook(p, pairs)
        return carry

    lax.fori_loop(0, pairs, one_pair, 0)


def attend_back(q_ref, k_ref, v_ref, up_ref, mixed_ref, log_ref, dq_ref, dk_ref, dv_ref, sums, causal, blocks, valid, hook):
    size = k_ref.shape[0] // blocks
    pairs = q_ref.shape[1] // PAIR

    def one_pair(p, carry):
        at = pl.ds(pl.multiple_of(p * PAIR, PAIR), PAIR)
        q_all = q_ref[:, at].astype(F32) * SCALE
        up_all = up_ref[:, at].astype(F32)
        product = up_all * mixed_ref[:, at].astype(F32)
        queries, upstream, inner, logs = [], [], [], []
        for h in range(2):
            chosen = lane_mask(q_all.shape, h)
            queries.append(jnp.where(chosen, q_all, 0.0).astype(BF16))
            upstream.append(jnp.where(chosen, up_all, 0.0).astype(BF16))
            ones = jnp.where(lane_mask((8, PAIR), h), 1.0, 0.0)
            inner.append(
                lax.dot_general(ones, product, NT, precision=lax.Precision.HIGHEST, preferred_element_type=F32)[0:1, :]
            )
            logs.append(log_ref[2 * p + h][0:1, :])
        query_grads = [None, None]
        value_sum = None
        for i in range(blocks):
            rows = slice(i * size, (i + 1) * size)
            keys, values = k_ref[rows, at], v_ref[rows, at]
            key_grad, value_grad = None, None
            for h in range(2):
                chance = jnp.exp(mask_scores(dot(keys, queries[h], NT), causal, valid) - logs[h])
                now = dot(chance.astype(BF16), upstream[h])
                value_grad = now if value_grad is None else value_grad + now
                grad = dot(values, upstream[h], NT)
                score_grad = (chance * (grad - inner[h])).astype(BF16)
                now = dot(score_grad, queries[h])
                key_grad = now if key_grad is None else key_grad + now
                now = dot(keys, score_grad, TN)
                query_grads[h] = now if query_grads[h] is None else query_grads[h] + now
            dk_ref[rows, at] = key_grad.astype(BF16)
            dv_ref[rows, at] = value_grad.astype(BF16)
            now = jnp.sum(value_grad, axis=0, keepdims=True)
            value_sum = now if value_sum is None else value_sum + now
        row = lax.broadcasted_iota(jnp.int32, query_grads[0].shape, 0)
        query_grad = jnp.transpose(jnp.where(row < HEAD_DIM, query_grads[0], query_grads[1])) * SCALE
        dq_ref[:, at] = query_grad.astype(BF16)
        query_sum = jnp.sum(query_grad, axis=0, keepdims=True)
        row = lax.broadcasted_iota(jnp.int32, (8, PAIR), 0)
        sums[:, at] = jnp.where(row == 0, query_sum, jnp.where(row == 1, value_sum, 0.0))
        hook(p, pairs)
        return carry

    lax.fori_loop(0, pairs, one_pair, 0)


def gather_kernel(sizes, own, whole, *scratch):
    place = Place(sizes)
    job = Gather(place, own, whole, scratch)
    place.barrier()
    for k in range(Gather.steps):
        job.run(k)


def gather(sizes, own):
    n_t = sizes[1]
    return call(
        functools.partial(gather_kernel, sizes), "gather", [((n_t, GROUPS * own.shape[0], own.shape[1]), BF16)], [own],
        scratch=Gather.scratch(n_t), remote=0, anywhere=(1, 1),
    )[0]


def self_forward_kernel(
    sizes, own, start, gain, shift, bias, weights, whole, normed, qkv, mixed, logs, part, came, w_in, w_out, score_buf,
    sems, *scratch,
):
    place = Place(sizes)
    job = Gather(place, own, whole, scratch)
    place.barrier()
    job.run(0)
    wide = mixed.shape[1]
    norm_rows(lambda at: start[at, :].astype(F32), gain, shift, normed)
    fill(weights, w_in, [(0, 0), (1, wide), (2, 2 * wide)])
    fill(weights, w_out, [(3, 0)])
    qkv[...] = (dot(normed[...], w_in[...]) + bias[...]).astype(BF16)
    q, k, v = (qkv.at[:, i * wide : (i + 1) * wide] for i in range(3))
    attend(q, k, v, mixed, logs, score_buf, True, 1, start.shape[0], hook_of(job, 1))
    part[...] = dot(mixed[...], w_out[...], NT).astype(BF16)
    job.run(5)
    exchange = swap(place, part, came, sems)
    exchange.start()
    exchange.wait()


def self_forward(sizes, own, start, gain, shift, bias, weights):
    m, d = start.shape
    n_t = sizes[1]
    wide = bias.shape[1] // 3
    heads = wide // HEAD_DIM
    return call(
        functools.partial(self_forward_kernel, sizes), "self_forward",
        [((n_t, GROUPS * own.shape[0], own.shape[1]), BF16), ((m, d), BF16), ((m, 3 * wide), BF16), ((m, wide), BF16),
         ((heads, 8, m), F32), ((m, d), BF16), ((m, d), BF16)],
        [own, start, gain, shift, bias, weights],
        scratch=[
            pltpu.VMEM((d, 3 * wide), BF16), pltpu.VMEM((d, wide), BF16), pltpu.VMEM((m, m), F32),
            pltpu.SemaphoreType.DMA((2,)), *Gather.scratch(n_t),
        ],
        flops=2 * m * d * 4 * wide + 4 * m * m * wide * 2, remote=1, anywhere=(1, 1),
    )


def cross_forward_kernel(
    sizes, blocks, valid, own_weights, start, own, came, branch, gain, shift, bias, bias_kv, memory, weights,
    whole, middle, normed, q, kv, mixed, logs, part, part_came, w_in, w_kv, w_out, score_buf, sems, *scratch,
):
    place = Place(sizes)
    job = Gather(place, own_weights, whole, scratch)
    place.barrier()
    job.run(0)
    wide = mixed.shape[1]
    fill(weights, w_kv, [(1, 0), (2, wide)])
    size = memory.shape[0] // blocks

    def one_block(i, carry):
        at = pl.ds(pl.multiple_of(i * size, size), size)
        kv[at, :] = (dot(memory[at, :], w_kv[...]) + bias_kv[...]).astype(BF16)
        return carry

    lax.fori_loop(0, blocks, one_block, 0)
    job.run(1)
    branch_row = branch[...]
    norm_rows(
        lambda at: start[at, :].astype(F32) + (own[at, :].astype(F32) + came[at, :].astype(F32)) + branch_row,
        gain, shift, normed, middle,
    )
    fill(weights, w_in, [(0, 0)])
    fill(weights, w_out, [(3, 0)])
    q[...] = (dot(normed[...], w_in[...]) + bias[...]).astype(BF16)

    def hook(p, pairs):
        for k in range(3):
            pl.when(p == k)(functools.partial(job.run, 2 + k))

    attend(q, kv.at[:, :wide], kv.at[:, wide:], mixed, logs, score_buf, False, blocks, valid, hook)
    part[...] = dot(mixed[...], w_out[...], NT).astype(BF16)
    job.run(5)
    exchange = swap(place, part, part_came, sems)
    exchange.start()
    exchange.wait()


def cross_forward(sizes, own_weights, start, own, came, branch, gain, shift, bias, bias_kv, memory, weights, blocks, valid):
    m, d = start.shape
    n_t = sizes[1]
    n, wide = memory.shape[0], bias.shape[1]
    heads = wide // HEAD_DIM
    return call(
        functools.partial(cross_forward_kernel, sizes, blocks, valid), "cross_forward",
        [((n_t, GROUPS * own_weights.shape[0], own_weights.shape[1]), BF16), ((m, d), F32), ((m, d), BF16),
         ((m, wide), BF16), ((n, 2 * wide), BF16), ((m, wide), BF16), ((heads, 8, m), F32), ((m, d), BF16),
         ((m, d), BF16)],
        [own_weights, start, own, came, branch, gain, shift, bias, bias_kv, memory, weights],
        scratch=[
            pltpu.VMEM((d, wide), BF16), pltpu.VMEM((d, 2 * wide), BF16), pltpu.VMEM((d, wide), BF16),
            pltpu.VMEM((n, m), F32), pltpu.SemaphoreType.DMA((2,)), *Gather.scratch(n_t),
        ],
        flops=2 * m * d * 2 * wide + 4 * n * d * wide + 4 * m * n * wide * 2, remote=2, anywhere=(1, 1),
    )


def feed_kernel(
    slots, middle, own, came, branch, gain, shift, upstream, bias, weights,
    later, out_part, grad_part, sums, grads, normed, out_acc, grad_acc,
):
    s = pl.program_id(0)
    width = bias.shape[1]
    w_hidden, w_reduce = weights.at[:, :width], weights.at[:, width:]

    @pl.when(s == 0)
    def _():
        branch_row = branch[...]
        norm_rows(
            lambda at: middle[at, :] + (own[at, :].astype(F32) + came[at, :].astype(F32)) + branch_row,
            gain, shift, normed, later,
        )

    expanded = dot(normed[...], w_hidden[...]) + bias[...]
    phi = 0.5 * (1.0 + lax.erf(expanded * (0.5**0.5)))
    activated = (expanded * phi).astype(BF16)
    density = jnp.exp(expanded * expanded * -0.5) * ((2.0 * math.pi) ** -0.5)
    slope = phi + expanded * density
    expanded_grad = dot(upstream[...], w_reduce[...]) * slope
    expanded_low = expanded_grad.astype(BF16)
    sums[...] = jnp.broadcast_to(jnp.sum(expanded_grad, axis=0, keepdims=True), sums.shape)
    out_now = dot(activated, w_reduce[...], NT)
    grad_now = dot(expanded_low, w_hidden[...], NT)

    @pl.when(s == 0)
    def _():
        out_acc[...] = out_now
        grad_acc[...] = grad_now

    @pl.when(jnp.logical_and(s > 0, s < slots - 1))
    def _():
        out_acc[...] += out_now
        grad_acc[...] += grad_now

    @pl.when(s == slots - 1)
    def _():
        out_part[...] = (out_acc[...] + out_now).astype(BF16)
        grad_part[...] = (grad_acc[...] + grad_now).astype(BF16)

    grads[:, :width] = dot(normed[...], expanded_low, TN).astype(BF16)
    grads[:, width:] = dot(upstream[...], activated, TN).astype(BF16)


def feed(middle, own, came, branch, gain, shift, upstream, bias, weights):
    m, d = middle.shape
    slots, _, width = bias.shape
    piece = pl.BlockSpec((None, d, 2 * width), lambda s: (s, 0, 0))
    args = [middle, own, came, branch, gain, shift, upstream]
    return call(
        functools.partial(feed_kernel, slots), "feed_forward_and_back",
        [((m, d), F32), ((m, d), BF16), ((m, d), BF16), ((slots, 8, width), F32), ((slots, d, 2 * width), BF16)],
        [*args, bias, weights],
        scratch=[pltpu.VMEM((m, d), BF16), pltpu.VMEM((m, d), F32), pltpu.VMEM((m, d), F32)],
        flops=12 * m * d * slots * width, grid=(slots,),
        specs=lambda whole: [whole(a.shape) for a in args]
        + [pl.BlockSpec((None, 1, width), lambda s: (s, 0, 0)), piece],
        out_specs=lambda whole: [whole((m, d))] * 3 + [pl.BlockSpec((None, 8, width), lambda s: (s, 0, 0)), piece],
    )


def output_kernel(later, own, came, branch, out):
    branch_row = branch[...]

    def body(at, carry):
        out[at, :] = (later[at, :] + (own[at, :].astype(F32) + came[at, :].astype(F32)) + branch_row).astype(BF16)
        return carry

    over_rows(out.shape[0], body)(0)


def cross_back_kernel(
    sizes, blocks, valid, own, came, later, gain, upstream, q, kv, mixed, logs, weights, normed, memory, feed_grads,
    later_grad, sums, head_sums, part, part_came, grads, keep, send, feed_own,
    later_low, dq, dkv, w_one, w_two, w_kv, mixed_grad, piece, sems, *scratch,
):
    place = Place(sizes)
    job = Scatter(place, feed_grads, feed_own, scratch)
    place.barrier()
    job.run(0)
    wide = q.shape[1]
    n, d = memory.shape
    fill(weights, w_one, [(3, 0)])
    fill(weights, w_two, [(0, 0)])
    norm_back_rows(own, came, later, gain, upstream, later_grad, later_low, sums)
    mixed_grad[...] = dot(later_low[...], w_one[...]).astype(BF16)
    attend_back(
        q, kv.at[:, :wide], kv.at[:, wide:], mixed_grad, mixed, logs, dq, dkv.at[:, :wide], dkv.at[:, wide:],
        head_sums, False, blocks, valid, hook_of(job, 1),
    )
    part[...] = dot(dq[...], w_two[...], NT).astype(BF16)
    fill(weights, w_kv, [(1, 0), (2, wide)])
    unfill(grads, 3, dot(later_low[...], mixed[...], TN).astype(BF16))
    exchange = swap(place, part, part_came, sems)
    exchange.start()
    unfill(grads, 0, dot(normed[...], dq[...], TN).astype(BF16))
    job.run(5)
    size = n // blocks
    own_half = pl.ds(pl.multiple_of(place.core * (d // 2), d // 2), d // 2)
    other_half = pl.ds(pl.multiple_of((1 - place.core) * (d // 2), d // 2), d // 2)

    def one_block(i, carry):
        rows = pl.ds(pl.multiple_of(i * size, size), size)
        piece[...] = dot(dkv[rows, :], w_kv[...], NT).astype(BF16)
        keep[rows, :] = piece[:, own_half]
        send[rows, :] = piece[:, other_half]
        return carry

    lax.fori_loop(0, blocks, one_block, 0)
    unfill(grads, 1, dot(memory[...], dkv[:, :wide], TN).astype(BF16))
    unfill(grads, 2, dot(memory[...], dkv[:, wide:], TN).astype(BF16))
    job.run(6)
    exchange.wait()


def cross_back(
    sizes, own, came, later, gain, upstream, q, kv, mixed, logs, weights, normed, memory, feed_grads, blocks, valid
):
    m, d = later.shape
    n_t = sizes[1]
    n, wide = memory.shape[0], q.shape[1]
    size, feed_wide = d // GROUPS, feed_grads.shape[2]
    return call(
        functools.partial(cross_back_kernel, sizes, blocks, valid), "cross_back",
        [((m, d), F32), ((8, d), F32), ((8, wide), F32), ((m, d), BF16), ((m, d), BF16), ((n_t, d, 4 * PAIR), BF16),
         ((n, d // 2), BF16), ((n, d // 2), BF16), ((size, feed_wide), F32)],
        [own, came, later, gain, upstream, q, kv, mixed, logs, weights, normed, memory, feed_grads],
        scratch=[
            pltpu.VMEM((m, d), BF16), pltpu.VMEM((m, wide), BF16), pltpu.VMEM((n, 2 * wide), BF16),
            pltpu.VMEM((d, wide), BF16), pltpu.VMEM((d, wide), BF16), pltpu.VMEM((d, 2 * wide), BF16),
            pltpu.VMEM((m, wide), BF16), pltpu.VMEM((n // blocks, d), BF16), pltpu.SemaphoreType.DMA((2,)),
            *Scatter.scratch(n_t, size, feed_wide),
        ],
        flops=8 * m * d * wide + 10 * m * n * wide * 2 + 8 * n * d * wide, remote=3,
    )


def self_back_kernel(
    sizes, own, came, middle, gain, upstream, qkv, mixed, logs, weights, normed, cross_grads,
    middle_grad, sums, head_sums, part, part_came, grads, cross_own,
    middle_low, dqkv, w_in, w_out, mixed_grad, sems, *scratch,
):
    place = Place(sizes)
    job = Scatter(place, cross_grads, cross_own, scratch)
    place.barrier()
    job.run(0)
    wide = mixed.shape[1]
    fill(weights, w_in, [(0, 0), (1, wide), (2, 2 * wide)])
    fill(weights, w_out, [(3, 0)])
    norm_back_rows(own, came, middle, gain, upstream, middle_grad, middle_low, sums)
    mixed_grad[...] = dot(middle_low[...], w_out[...]).astype(BF16)
    cut = [slice(i * wide, (i + 1) * wide) for i in range(3)]
    attend_back(
        *(qkv.at[:, c] for c in cut), mixed_grad, mixed, logs, *(dqkv.at[:, c] for c in cut), head_sums, True, 1,
        middle.shape[0], hook_of(job, 1),
    )
    part[...] = dot(dqkv[...], w_in[...], NT).astype(BF16)
    unfill(grads, 3, dot(middle_low[...], mixed[...], TN).astype(BF16))
    exchange = swap(place, part, part_came, sems)
    exchange.start()
    for which in range(3):
        unfill(grads, which, dot(normed[...], dqkv[:, cut[which]], TN).astype(BF16))
    job.run(5)
    job.run(6)
    exchange.wait()


def self_back(sizes, own, came, middle, gain, upstream, qkv, mixed, logs, weights, normed, cross_grads):
    m, d = middle.shape
    n_t = sizes[1]
    wide = mixed.shape[1]
    size, cross_wide = d // GROUPS, cross_grads.shape[2]
    return call(
        functools.partial(self_back_kernel, sizes), "self_back",
        [((m, d), F32), ((8, d), F32), ((8, wide), F32), ((m, d), BF16), ((m, d), BF16), ((n_t, d, 4 * PAIR), BF16),
         ((size, cross_wide), F32)],
        [own, came, middle, gain, upstream, qkv, mixed, logs, weights, normed, cross_grads],
        scratch=[
            pltpu.VMEM((m, d), BF16), pltpu.VMEM((m, 3 * wide), BF16), pltpu.VMEM((d, 3 * wide), BF16),
            pltpu.VMEM((d, wide), BF16), pltpu.VMEM((m, wide), BF16), pltpu.SemaphoreType.DMA((2,)),
            *Scatter.scratch(n_t, size, cross_wide),
        ],
        flops=16 * m * d * wide + 10 * m * m * wide * 2, remote=4,
    )


def start_back_kernel(sizes, own, came, start, gain, upstream, self_grads, grad, sums, self_own, *scratch):
    place = Place(sizes)
    job = Scatter(place, self_grads, self_own, scratch)
    place.barrier()
    job.run(0)
    norm_back_rows(own, came, start, gain, upstream, grad, None, sums)
    for k in range(1, Scatter.steps):
        job.run(k)


def flip(x, bit, size):
    return lax.ppermute(x, "fsdp", [(i, i ^ (1 << bit)) for i in range(size)])


def turn(x, step, size):
    return lax.ppermute(x, "tensor", [(i, (i + step) % size) for i in range(size)])


def half(x, index, axis):
    size = x.shape[axis] // 2
    return lax.dynamic_slice_in_dim(x, index * size, size, axis=axis)


def after(x, *waits):
    return lax.optimization_barrier((x, *waits))[0]


def after_all(xs, waits):
    return lax.optimization_barrier((*xs, *waits))[: len(xs)]


def add(a, b):
    return (a.astype(F32) + b.astype(F32)).astype(BF16)


def on_device(
    n_f, n_t,
    tokens, encoder, cotangent, self_weights, self_biases, self_output, cross_query, cross_memory,
    cross_biases, cross_output, hidden_weight, hidden_bias, reduce_weight, norm_gains, norm_shifts, branch_biases,
):
    bits = n_f.bit_length() - 1
    x_bit, y_bit = bits - 2, bits - 1
    f = lax.axis_index("fsdp")
    z = lax.axis_index("tensor")
    core = f % 2
    sizes = (n_f, n_t)
    length, d = tokens.shape[1], tokens.shape[2]
    frames = encoder.shape[1]
    own_clips = tokens.shape[0]
    assert own_clips * 2 == n_t == 4 and bits >= 3
    per = d // n_f
    units_here = hidden_bias.shape[1]
    units = units_here * n_f
    heads_here = self_biases.shape[2]
    inner = n_f // GROUPS

    def begin(weights, extra=None, waits=()):
        keep = jnp.concatenate([half(w, core, 1) for w in weights], axis=1)
        send = jnp.concatenate([half(w, 1 - core, 1) for w in weights], axis=1)
        width = keep.shape[1]
        now, more = keep, extra
        for bit in range(bits - 2):
            rows = now.shape[0]
            out = send if bit == 0 else now
            if more is not None:
                out = jnp.concatenate([out, more.reshape(-1, width)])
            if waits:
                out = after(out, *waits)
            came = flip(out, bit, n_f)
            low = (f >> bit) % 2 == 0
            a, b = now, came[:rows]
            now = jnp.where(low, jnp.concatenate([a, b]), jnp.concatenate([b, a]))
            if more is not None:
                b = came[rows:]
                more = jnp.where(low, jnp.concatenate([more, b]), jnp.concatenate([b, more]))
        return now if more is None else jnp.concatenate([now, more])

    def around(now):
        return [now] + [turn(now, s, n_t) for s in range(1, n_t)]

    small = jnp.concatenate(
        [v.reshape(-1) for v in (norm_gains, norm_shifts, branch_biases, hidden_bias, self_biases, cross_biases)]
    )
    lanes = 4 * PAIR
    small_rows = -(-small.shape[0] // (16 * lanes)) * 16
    small = jnp.pad(small, (0, small_rows * lanes - small.shape[0])).reshape(small_rows, lanes)

    first = begin([self_weights[0], self_weights[1], self_weights[2], self_output.T], small)
    second = begin([cross_query, cross_memory[0], cross_memory[1], cross_output.T])
    third = begin([hidden_weight, reduce_weight.T])
    wide_half = units // 2
    w_self = gather(sizes, first)

    rows = d // GROUPS
    table = w_self.reshape(n_t, GROUPS, -1, lanes)[:, :, rows:].reshape(n_t, n_f, -1).astype(F32)
    features = table[0, :, : 9 * per].reshape(n_f, 9, per).transpose(1, 0, 2).reshape(9, d)
    at = 9 * per
    hidden_slots = half(table[:, :, at : at + units_here].reshape(n_t, 1, units), core, 2)
    at += units_here

    def head_slots(at):
        v = table[:, :, at : at + 2 * heads_here].reshape(n_t, n_f, 2, heads_here).transpose(2, 0, 1, 3)
        return half(v.reshape(2, n_t, n_f * heads_here), core, 2).reshape(2, 1, -1)

    self_bias = head_slots(at)
    cross_bias = head_slots(at + 2 * heads_here)
    zero = jnp.zeros_like(self_bias[0])
    qkv_bias = jnp.concatenate([self_bias[0], zero, self_bias[1]], axis=1)
    kv_bias = jnp.concatenate([zero, cross_bias[1]], axis=1)
    gain, shift, branch = ([features[3 * i + j : 3 * i + j + 1] for j in range(3)] for i in range(3))

    mine = core == z // own_clips

    def take_clip(x):
        x = lax.dynamic_index_in_dim(x, z % own_clips, axis=0, keepdims=False)
        return jnp.where(mine, x, flip(x, 0, n_f))

    part_frames = frames // n_t
    part_pad = -(-part_frames // 128) * 128
    start = take_clip(tokens)
    upstream = take_clip(cotangent)
    memory = jnp.pad(
        take_clip(encoder).reshape(n_t, part_frames, d), ((0, 0), (0, part_pad - part_frames), (0, 0))
    ).reshape(n_t * part_pad, d)

    def scatter_end(now):
        for bit in range(bits - 3, 0, -1):
            up = (f >> bit) % 2
            now = half(now, up, 0) + flip(half(now, 1 - up, 0).astype(BF16), bit, n_f).astype(F32)
        return half(now, core, 0), flip(half(now, 1 - core, 0), 0, n_f)

    def unpack(shares, widths):
        keep, came = shares
        result, at = [], 0
        for width in widths:
            a, b = keep[:, at : at + width], came[:, at : at + width]
            result.append(jnp.where(core == 0, jnp.concatenate([a, b], 1), jnp.concatenate([b, a], 1)))
            at += width
        return result

    w_cross, normed_one, qkv, mixed_one, log_one, part, came = self_forward(
        sizes, second, start, gain[0], shift[0], qkv_bias, w_self
    )
    w_feed, middle, normed_two, cross_q, kv, mixed_two, log_two, part, came = cross_forward(
        sizes, third, start, part, came, branch[0], gain[1], shift[1], cross_bias[0], kv_bias, memory, w_cross, n_t,
        part_frames,
    )
    later, out_part, part, hidden_sums, g_feed = feed(
        middle, part, came, branch[1], gain[2], shift[2], upstream, hidden_slots, w_feed
    )

    came = flip(part, 0, n_f)
    (output,) = call(output_kernel, "output", [((length, d), BF16)], [later, out_part, flip(out_part, 0, n_f), branch[2]])
    output_half = half(output, core, 0)
    later_grad, sums_three, cross_sums, part, part_came, g_cross, memory_keep, memory_send, feed_own = cross_back(
        sizes, part, came, later, gain[2], upstream, cross_q, kv, mixed_two, log_two, w_cross, normed_two, memory,
        g_feed, n_t, part_frames,
    )
    memory_sum = add(memory_keep, flip(memory_send, 0, n_f))
    middle_grad, sums_two, self_sums, part, part_came, g_self, cross_own = self_back(
        sizes, part, part_came, middle, gain[1], later_grad, qkv, mixed_one, log_one, w_self, normed_one, g_cross
    )
    size = d // GROUPS
    start_grad, sums_one, self_own = call(
        functools.partial(start_back_kernel, sizes), "start_back",
        [((length, d), BF16), ((8, d), F32), ((size, 4 * PAIR), F32)],
        [part, part_came, start, gain[0], middle_grad, g_self], scratch=Scatter.scratch(n_t, size, 4 * PAIR), remote=5,
    )
    start_half = half(start_grad, core, 0)

    hidden_share, reduce_t = unpack(scatter_end(feed_own), [wide_half, wide_half])
    cq_share, ck_share, cv_share, cross_out_t = unpack(scatter_end(cross_own), [PAIR] * 4)
    q_share, k_share, v_share, self_out_t = unpack(scatter_end(self_own), [PAIR] * 4)

    lead = jnp.where(core == 0, 1.0, 0.0).astype(F32)
    feature_sums = jnp.stack(
        [sums_one[0], sums_two[0], sums_three[0], sums_one[1], sums_two[1], sums_three[1],
         sums_two[2], sums_three[2], sums_three[3]]
    ) * lead

    def from_slots(v):
        natural = jnp.swapaxes(v, 0, 1)
        wide = jnp.zeros((*natural.shape[:2], 2 * natural.shape[2]), F32)
        return lax.dynamic_update_slice(wide, natural, (0, 0, core * natural.shape[2]))

    def by_slot(v):
        return v[:2].reshape(2, n_t, -1).transpose(1, 0, 2)

    unit_sums = [from_slots(hidden_sums[:, :1]), from_slots(by_slot(self_sums)), from_slots(by_slot(cross_sums))]
    packed = jnp.concatenate([feature_sums.reshape(-1)] + [u.reshape(-1) for u in unit_sums]).reshape(-1, 1024)
    for bit in range(bits):
        packed = packed + flip(packed, bit, n_f)
    for step in (1, 2):
        packed = packed + lax.ppermute(packed, "tensor", [(i, i ^ step) for i in range(n_t)])
    packed = packed.reshape(-1)
    feature_share = lax.dynamic_slice(packed[: 9 * d].reshape(9, d), (0, f * per), (9, per))

    def unit_share(at, count, total):
        block = packed[at : at + count * n_t * total].reshape(count, n_t, total)
        return lax.dynamic_slice(block, (0, z, f * (total // n_f)), (count, 1, total // n_f))

    at = 9 * d
    hidden_bias_share = unit_share(at, 1, units)[0]
    at += n_t * units
    self_bias_share = unit_share(at, 2, heads_here * n_f)
    at += 2 * n_t * heads_here * n_f
    cross_bias_share = unit_share(at, 2, heads_here * n_f)

    def own_of(slots, c):
        stacked = jnp.stack(slots)
        return jnp.stack(
            [
                lax.dynamic_index_in_dim(stacked, (z - c * own_clips - i) % n_t, axis=0, keepdims=False)
                for i in range(own_clips)
            ]
        )

    def join(slots, axis):
        keep, came = own_of(slots, core), flip(own_of(slots, 1 - core), 0, n_f)
        return jnp.where(core == 0, jnp.concatenate([keep, came], axis), jnp.concatenate([came, keep], axis))

    def spread_clip(x):
        return join(around(x), 1)

    summed = memory_sum.reshape(n_t, part_pad, d // 2)
    slots = []
    for s in range(n_t):
        block = lax.dynamic_index_in_dim(summed, (z + s) % n_t, axis=0, keepdims=False)
        slots.append(turn(block, s, n_t) if s else block)
    memory_share = join(slots, 2)

    return (
        spread_clip(output_half),
        spread_clip(start_half),
        memory_share[:, :part_frames],
        jnp.stack([q_share, k_share, v_share]),
        self_bias_share,
        self_out_t.T,
        cq_share,
        jnp.stack([ck_share, cv_share]),
        cross_bias_share,
        cross_out_t.T,
        hidden_share,
        hidden_bias_share,
        reduce_t.T,
        feature_share[0:3],
        feature_share[3:6],
        feature_share[6:9],
    )


def solution(mesh):
    n_f, n_t = mesh.shape["fsdp"], mesh.shape["tensor"]
    clips = P("fsdp", None, None)
    stacked = P(None, "fsdp", "tensor")
    biases = P(None, "tensor", "fsdp")
    up, down, rows = P("fsdp", "tensor"), P("tensor", "fsdp"), P(None, "fsdp")
    return jax.shard_map(
        functools.partial(on_device, n_f, n_t),
        mesh=mesh,
        in_specs=(
            clips, clips, clips, stacked, biases, down, up, stacked, biases, down, up, down, down, rows, rows, rows,
        ),
        out_specs=(
            clips, clips, P("fsdp", "tensor", None), stacked, biases, down, up, stacked, biases, down, up, down,
            down, rows, rows, rows,
        ),
        check_vma=False,
    )
```

time: 661 us -> 586 us (0.89)
  the two profiles are of different devices: /device:TPU:0 before, /device:TPU:25 now
where the time goes in v3:
time: 586 us; the launch traced here: 576 us
  Pallas kernels  380 us (65%)
  waiting for transfers between devices  83.2 us (14%)
  local copies, waits for them, and re-layouts  50.5 us (9%)
  other arithmetic  31.1 us (5%)
  starting transfers between devices  29.8 us (5%)
    pallas_call x8, Pallas kernels, call(): pl.pallas_call(kernel, name=name, out_shape=out_shape, scratch_shapes=lis...  380 us
    ppermute x9, waiting for transfers between devices, turn(): lax.ppermute(x, 'tensor', [(i, (i + step) % size) for i in range(size)])  57.9 us
    ppermute x18, starting transfers between devices, flip(): return lax.ppermute(x, 'fsdp', [(i, i ^ 1 << bit) for i in range(size)])  16.2 us
    ppermute x2, waiting for transfers between devices, on_device(): lax.ppermute(packed, 'tensor', [(i, i ^ step) for i in range(n_t)])  14 us
    ppermute x9, starting transfers between devices, turn(): lax.ppermute(x, 'tensor', [(i, (i + step) % size) for i in range(size)])  13.5 us
  transfers between devices with their start and end apart: 29, of which 12 were waited for; matrix products, arithmetic and copies ran while one was open for 9% of the time, Pallas kernels for 48%

profile of v3, /device:TPU:25, one launch (start us, length us, event | category | flops | bytes accessed | tf_op | source)
XLA Modules:
  0.0 576.3 jit_solution(11941230306567076964)
XLA Ops:
  0.7 7.6 %constant_dynamic-slice_fusion.26 = bf16[1,1500,1024]{2,0,1:T(2,128)(2,1)S(1)} fusion(bf16[2,1500,1024]{2,0,1:T(2,128)(2,1)} %param.17, s32[]{:T(128)S(6)} %select_n.340), kind=kLoop, calls=%fused_computation.99 | loop fusion | bytes 6144004 | tf_op jit(solution)/shard_map/jit(dynamic_index_in_dim)/dynamic_slice | solution.py:968
  8.4 3.4 copy.69
  16.1 2.2 dynamic-slice_bitcast_fusion
  21.7 42.6 %gather.1.weights = bf16[4,1152,512]{2,1,0:T(8,128)(2,1)} custom-call(bf16[288,512]{1,0:T(8,128)(2,1)} %pad_maximum_fusion.11.own), custom_call_target="tpu_custom_call" | custom-call | bytes 5013504 | tf_op jit(solution)/shard_map/gather/pallas_call | solution.py:42
  64.3 1.2 slice_convert_fusion
  65.5 1.2 reshape.455
  72.4 2.0 maximum_select_fusion.2.own_weights
  75.4 47.1 %self_forward.1 = (bf16[4,1024,512]{2,1,0:T(8,128)(2,1)}, bf16[448,1024]{1,0:T(8,128)(2,1)}, bf16[448,1536]{1,0:T(8,128)(2,1)}, bf16[448,512]{1,0:T(8,128)(2,1)}...) custom-call(bf16[256,512]{1,0:T(8,128)(2,1)} %maximum_select_fusion.5.own, ...), custom_call_target="tpu_custom_call" | custom-call | flops 2701131776 | bytes 14809088 | tf_op jit(solution)/shard_map/self_forward/pallas_call | solution.py:42
  122.5 2.2 broadcast_select_fusion.1.upstream
  124.7 3.8 broadcast_select_fusion
  128.6 2.4 reshape.443
  131.0 4.1 pad.10
  135.1 84.0 %cross_forward.1 = (bf16[4,1024,1024]{2,1,0:T(8,128)(2,1)}, f32[448,1024]{1,0:T(8,128)}, bf16[448,1024]{1,0:T(8,128)(2,1)}, bf16[448,512]{1,0:T(8,128)(2,1)}, bf...) custom-call(bf16[256,1024]{1,0:T(8,128)(2,1)} %maximum_select_fusion, ...), custom_call_target="tpu_custom_call" | custom-call | flops 6979321856 | bytes 27789312 | tf_op jit(solution)/shard_map/cross_forward/pallas_call | solution.py:42
  219.1 20.6 %feed_forward_and_back.1 = (f32[448,1024]{1,0:T(8,128)}, bf16[448,1024]{1,0:T(8,128)(2,1)}, bf16[448,1024]{1,0:T(8,128)(2,1)}, f32[4,8,512]{2,1,0:T(8,128)}, bf16[4,1024,1024]{2,1,0:T(8,128)(2,1)}) custom-call(f32[448,1024]{1,0:T(8,128)} %get-tuple-element.59.middle, bf16[448,1024]{1,0:T(8,128)(2,1)} %get-tuple-element.60.own, ...), custom_call_target="tpu_custom_call" | custom-call | flops 11274289152 | bytes 25120768 | tf_op jit(solution)/shard_map/feed_forward_and_back/pallas_call | solution.py:42
  241.0 1.4 collective-permute-done.11.came
  242.5 91.5 %cross_back.1 = (f32[448,1024]{1,0:T(8,128)}, f32[8,1024]{1,0:T(8,128)}, f32[8,512]{1,0:T(8,128)}, bf16[448,1024]{1,0:T(8,128)(2,1)}, bf16[448,1024]{1,0:T(8,128...) custom-call(bf16[448,1024]{1,0:T(8,128)(2,1)} %get-tuple-element.65., ...), custom_call_target="tpu_custom_call" | custom-call | flops 15367929856 | bytes 37523456 | tf_op jit(solution)/shard_map/cross_back/pallas_call | solution.py:42
  334.0 49.8 %self_back.1 = (f32[448,1024]{1,0:T(8,128)}, f32[8,1024]{1,0:T(8,128)}, f32[8,512]{1,0:T(8,128)}, bf16[448,1024]{1,0:T(8,128)(2,1)}, bf16[448,1024]{1,0:T(8,128)...) custom-call(bf16[448,1024]{1,0:T(8,128)(2,1)} %get-tuple-element.72.own, ...), custom_call_target="tpu_custom_call" | custom-call | flops 5813305344 | bytes 25726976 | tf_op jit(solution)/shard_map/self_back/pallas_call | solution.py:42
  383.8 40.8 %start_back.1 = (bf16[448,1024]{1,0:T(8,128)(2,1)}, f32[8,1024]{1,0:T(8,128)}, f32[256,512]{1,0:T(8,128)}) custom-call(bf16[448,1024]{1,0:T(8,128)(2,1)} %get-tuple-element.80.own, bf16[448,1024]{1,0:T(8,128)(2,1)} %get-tuple-element.81.came, bf16[448,1024]{1,0:T(8,128)(2,1)} %broadcast_select_fusion.2.start, f32[1,1024]{1,0:T(1,128)} %bitcast.153, ...), custom_call_target="tpu_custom_call" | custom-call | bytes 10260480 | tf_op jit(solution)/shard_map/start_back/pallas_call | solution.py:42
  424.6 1.8 constant_dynamic-slice_fusion.19
  426.4 1.3 collective-permute-start.12
  427.7 3.7 collective-permute-start.13
  433.1 3.3 output.1
  436.4 1.9 constant_dynamic-slice_fusion.24
  441.0 4.5 collective-permute-start.27
  449.1 1.2 collective-permute-done.22
  451.2 3.4 collective-permute-done.23
  455.4 3.1 collective-permute-done.24
  458.5 1.8 collective-permute-start.21
  464.6 8.3 %collective-permute-done.25 = f32[17,1024]{1,0:T(8,128)S(1)} collective-permute-done((f32[17,1024]{1,0:T(8,128)S(1)}, f32[17,1024]{1,0:T(8,128)S(1)}, u32[]{:S(2)}, u32[]{:S(2)}) %collective-permute-start.25) | collective-permute-done | bytes 69664 | tf_op jit(solution)/shard_map/ppermute | solution.py:1047
  473.6 5.7 collective-permute-done.26
  482.0 1.8 collective-permute-start.9
  483.8 1.3 collective-permute-start.28
  485.1 1.5 pad_maximum_fusion.1
  487.8 4.5 collective-permute-done.7
  492.3 1.7 collective-permute-start.15
  494.0 23.8 %collective-permute-done.8 = bf16[224,1024]{1,0:T(8,128)(2,1)S(1)} collective-permute-done((bf16[224,1024]{1,0:T(8,128)(2,1)}, bf16[224,1024]{1,0:T(8,128)(2,1)S(1)}, u32[]{:S(2)}, u32[]{:S(2)}) %collective-permute-start.8) | collective-permute-done | bytes 458784 | tf_op jit(solution)/shard_map/ppermute | solution.py:869
  518.0 1.2 copy-done.3
  519.2 1.8 add_convert_fusion
  521.2 4.8 collective-permute-start.18
  526.0 1.4 collective-permute-start.19
  528.5 1.3 collective-permute-start.10
  530.6 2.1 collective-permute-done.17
  532.7 27.5 %collective-permute-done.18 = bf16[384,512]{1,0:T(8,128)(2,1)S(1)} collective-permute-done((bf16[384,512]{1,0:T(8,128)(2,1)S(1)}, bf16[384,512]{1,0:T(8,128)(2,1)S(1)}, u32[]{:S(2)}, u32[]{:S(2)}) %collective-permute-start.18) | collective-permute-done | bytes 393248 | tf_op jit(solution)/shard_map/ppermute | solution.py:869
  563.6 1.9 maximum_select_fusion.3
  565.5 2.9 maximum_select_fusion.1
  568.3 2.9 maximum_select_fusion
  571.2 1.9 fusion
  573.1 2.7 copy.53
  (198 shorter events, 39.4 us)
Async XLA Ops:
  8.3 3.6 copy-start
  8.3 4.2 copy-start.10
  8.3 4.2 copy-start.11
  8.3 4.3 copy-start.13
  8.4 4.3 copy-start.14
  8.4 4.4 copy-start.20
  8.4 4.5 copy-start.21
  8.4 4.6 copy-start.16
  8.4 4.6 copy-start.17
  8.4 4.6 copy-start.18
  8.4 4.6 copy-start.19
  11.9 112.9 %collective-permute-start.4 = (bf16[1500,1024]{1,0:T(8,128)(2,1)}, bf16[1500,1024]{1,0:T(8,128)(2,1)}, u32[]{:S(2)}, u32[]{:S(2)}) collective-permute-start(bf16[1500,1024]{1,0:T(8,128)(2,1)} %bitcast.127), channel_id=1, source_target_pairs={{0,4},{4,0},{8,12},{12,8},{16,20},{20,16},{24,28},{28,24},{1,5},{5... | collective-permute-start | bytes 9216008 | tf_op jit(solution)/shard_map/ppermute | solution.py:865
  12.6 2.6 copy-start.12
  12.6 2.7 copy-start.8
  13.2 2.3 copy-start.9
  13.2 7.6 %collective-permute-start.3 = (bf16[144,512]{1,0:T(8,128)(2,1)S(1)}, bf16[144,512]{1,0:T(8,128)(2,1)S(1)}, u32[]{:S(2)}, u32[]{:S(2)}) collective-permute-start(bf16[144,512]{1,0:T(8,128)(2,1)S(1)} %pad_maximum_fusion.14), channel_id=1, source_target_pairs={{0,4},{4,0},{8,12},{12,8},{16,20},{20,16},{24,28},{28,24},{1,5},{5... | collective-permute-start | bytes 442376 | tf_op jit(solution)/shard_map/ppermute | solution.py:865
  14.4 60.0 %collective-permute-start.1 = (bf16[448,1024]{1,0:T(8,128)(2,1)}, bf16[448,1024]{1,0:T(8,128)(2,1)}, u32[]{:S(2)}, u32[]{:S(2)}) collective-permute-start(bf16[448,1024]{1,0:T(8,128)(2,1)} %dynamic-slice_bitcast_fusion.1), channel_id=1, source_target_pairs={{0,4},{4,0},{8,12},{12,8},{16,20},{20,16},{24,28},{28,24},{1,5},{5... | collective-permute-start | bytes 2752520 | tf_op jit(solution)/shard_map/ppermute | solution.py:865
  15.2 4.5 collective-permute-start.2
  15.5 56.8 %collective-permute-start = (bf16[128,1024]{1,0:T(8,128)(2,1)S(1)}, bf16[128,1024]{1,0:T(8,128)(2,1)}, u32[]{:S(2)}, u32[]{:S(2)}) collective-permute-start(bf16[128,1024]{1,0:T(8,128)(2,1)S(1)} %pad_maximum_fusion.12), channel_id=1, source_target_pairs={{0,4},{4,0},{8,12},{12,8},{16,20},{20,16},{24,28},{28,24},{1,5},{5... | collective-permute-start | bytes 786440 | tf_op jit(solution)/shard_map/ppermute | solution.py:865
  19.7 102.8 %collective-permute-start.5 = (bf16[448,1024]{1,0:T(8,128)(2,1)}, bf16[448,1024]{1,0:T(8,128)(2,1)}, u32[]{:S(2)}, u32[]{:S(2)}) collective-permute-start(bf16[448,1024]{1,0:T(8,128)(2,1)} %dynamic-slice_bitcast_fusion), channel_id=1, source_target_pairs={{0,4},{4,0},{8,12},{12,8},{16,20},{20,16},{24,28},{28,24},{1,5},{5... | collective-permute-start | bytes 2752520 | tf_op jit(solution)/shard_map/ppermute | solution.py:865
  65.5 8.9 %copy-start.2 = (bf16[2,448,1024]{2,1,0:T(8,128)(2,1)S(1)}, bf16[2,448,1024]{2,1,0:T(8,128)(2,1)}, u32[]{:S(2)}) copy-start(bf16[2,448,1024]{2,1,0:T(8,128)(2,1)} %param.16) | copy-start | bytes 5505028
  239.6 2.8 collective-permute-start.11
  239.8 193.2 %collective-permute-start.6 = (bf16[448,1024]{1,0:T(8,128)(2,1)}, bf16[448,1024]{1,0:T(8,128)(2,1)}, u32[]{:S(2)}, u32[]{:S(2)}) collective-permute-start(bf16[448,1024]{1,0:T(8,128)(2,1)} %get-tuple-element.64.own), channel_id=1, source_target_pairs={{0,4},{4,0},{8,12},{12,8},{16,20},{20,16},{24,28},{28,24},{1,5},{5... | collective-permute-start | bytes 2752520 | tf_op jit(solution)/shard_map/ppermute | solution.py:865
  383.8 48.2 %copy-start.15 = (f32[8,1024]{1,0:T(8,128)S(1)}, f32[8,1024]{1,0:T(8,128)}, u32[]{:S(2)}) copy-start(f32[8,1024]{1,0:T(8,128)} %get-tuple-element.90) | copy-start | bytes 98308
  426.4 55.6 %collective-permute-start.12 = (bf16[224,1024]{1,0:T(8,128)(2,1)}, bf16[224,1024]{1,0:T(8,128)(2,1)}, u32[]{:S(2)}, u32[]{:S(2)}) collective-permute-start(bf16[224,1024]{1,0:T(8,128)(2,1)} %constant_dynamic-slice_fusion.19), channel_id=1, source_target_pairs={{0,1},{1,2},{2,3},{3,0},{4,5},{5,6},{6,7},{7,4},{8,9},{9,10},{10,1... | collective-permute-start | bytes 1376264 | tf_op jit(solution)/shard_map/ppermute | solution.py:869
  427.7 54.3 %collective-permute-start.13 = (bf16[224,1024]{1,0:T(8,128)(2,1)}, bf16[224,1024]{1,0:T(8,128)(2,1)}, u32[]{:S(2)}, u32[]{:S(2)}) collective-permute-start(bf16[224,1024]{1,0:T(8,128)(2,1)} %constant_dynamic-slice_fusion.19), channel_id=1, source_target_pairs={{0,2},{1,3},{2,0},{3,1},{4,6},{5,7},{6,4},{7,5},{8,10},{9,11},{10,... | collective-permute-start | bytes 1376264 | tf_op jit(solution)/shard_map/ppermute | solution.py:869
  431.4 52.4 %collective-permute-start.14 = (bf16[224,1024]{1,0:T(8,128)(2,1)}, bf16[224,1024]{1,0:T(8,128)(2,1)}, u32[]{:S(2)}, u32[]{:S(2)}) collective-permute-start(bf16[224,1024]{1,0:T(8,128)(2,1)} %constant_dynamic-slice_fusion.19), channel_id=1, source_target_pairs={{0,3},{1,0},{2,1},{3,2},{4,7},{5,4},{6,5},{7,6},{8,11},{9,8},{10,9... | collective-permute-start | bytes 1376264 | tf_op jit(solution)/shard_map/ppermute | solution.py:869
  436.3 3.0 copy-start.4
  436.3 4.6 copy-start.7
  439.3 9.7 %copy-start.6 = (f32[256,512]{1,0:T(8,128)S(1)}, f32[256,512]{1,0:T(8,128)}, u32[]{:S(2)}) copy-start(f32[256,512]{1,0:T(8,128)} %get-tuple-element.87) | copy-start | bytes 1572868
  441.0 19.4 %collective-permute-start.27 = (f32[128,512]{1,0:T(8,128)S(1)}, f32[128,512]{1,0:T(8,128)S(1)}, u32[]{:S(2)}, u32[]{:S(2)}) collective-permute-start(f32[128,512]{1,0:T(8,128)S(1)} %constant_dynamic-slice_fusion.6), channel_id=1, source_target_pairs={{0,4},{4,0},{8,12},{12,8},{16,20},{20,16},{24,28},{28,24},{1,5},{5... | collective-permute-start | bytes 786440 | tf_op jit(solution)/shard_map/ppermute | solution.py:865
  448.9 1.4 collective-permute-start.22
  450.3 4.3 collective-permute-start.23
  454.6 3.9 collective-permute-start.24
  458.5 2.9 collective-permute-start.21
  460.3 57.7 %collective-permute-start.16 = (bf16[1536,512]{1,0:T(8,128)(2,1)}, bf16[1536,512]{1,0:T(8,128)(2,1)}, u32[]{:S(2)}, u32[]{:S(2)}) collective-permute-start(bf16[1536,512]{1,0:T(8,128)(2,1)} %get-tuple-element.86), channel_id=1, source_target_pairs={{0,4},{4,0},{8,12},{12,8},{16,20},{20,16},{24,28},{28,24},{1,5},{5... | collective-permute-start | bytes 4718600 | tf_op jit(solution)/shard_map/ppermute | solution.py:865
  461.5 11.4 %collective-permute-start.25 = (f32[17,1024]{1,0:T(8,128)S(1)}, f32[17,1024]{1,0:T(8,128)S(1)}, u32[]{:S(2)}, u32[]{:S(2)}) collective-permute-start(f32[17,1024]{1,0:T(8,128)S(1)} %add.211), channel_id=1, source_target_pairs={{0,1},{1,0},{2,3},{3,2},{4,5},{5,4},{6,7},{7,6},{8,9},{9,8},{10,11... | collective-permute-start | bytes 208904 | tf_op jit(solution)/shard_map/ppermute | solution.py:1047
  472.9 6.5 %collective-permute-start.26 = (f32[17,1024]{1,0:T(8,128)S(1)}, f32[17,1024]{1,0:T(8,128)S(1)}, u32[]{:S(2)}, u32[]{:S(2)}) collective-permute-start(f32[17,1024]{1,0:T(8,128)S(1)} %add.212), channel_id=1, source_target_pairs={{0,2},{1,3},{2,0},{3,1},{4,6},{5,7},{6,4},{7,5},{8,10},{9,11},{10,... | collective-permute-start | bytes 208904 | tf_op jit(solution)/shard_map/ppermute | solution.py:1047
  479.4 13.0 %collective-permute-start.7 = (bf16[224,1024]{1,0:T(8,128)(2,1)}, bf16[224,1024]{1,0:T(8,128)(2,1)S(1)}, u32[]{:S(2)}, u32[]{:S(2)}) collective-permute-start(bf16[224,1024]{1,0:T(8,128)(2,1)} %constant_dynamic-slice_fusion.24), channel_id=1, source_target_pairs={{0,1},{1,2},{2,3},{3,0},{4,5},{5,6},{6,7},{7,4},{8,9},{9,10},{10,1... | collective-permute-start | bytes 1376264 | tf_op jit(solution)/shard_map/ppermute | solution.py:869
  482.0 35.8 %collective-permute-start.8 = (bf16[224,1024]{1,0:T(8,128)(2,1)}, bf16[224,1024]{1,0:T(8,128)(2,1)S(1)}, u32[]{:S(2)}, u32[]{:S(2)}) collective-permute-start(bf16[224,1024]{1,0:T(8,128)(2,1)} %constant_dynamic-slice_fusion.24), channel_id=1, source_target_pairs={{0,2},{1,3},{2,0},{3,1},{4,6},{5,7},{6,4},{7,5},{8,10},{9,11},{10,... | collective-permute-start | bytes 1376264 | tf_op jit(solution)/shard_map/ppermute | solution.py:869
  482.0 35.7 %collective-permute-start.9 = (bf16[224,1024]{1,0:T(8,128)(2,1)}, bf16[224,1024]{1,0:T(8,128)(2,1)S(1)}, u32[]{:S(2)}, u32[]{:S(2)}) collective-permute-start(bf16[224,1024]{1,0:T(8,128)(2,1)} %constant_dynamic-slice_fusion.24), channel_id=1, source_target_pairs={{0,3},{1,0},{2,1},{3,2},{4,7},{5,4},{6,5},{7,6},{8,11},{9,8},{10,9... | collective-permute-start | bytes 1376264 | tf_op jit(solution)/shard_map/ppermute | solution.py:869
  483.8 44.8 %collective-permute-start.28 = (f32[128,1024]{1,0:T(8,128)}, f32[128,1024]{1,0:T(8,128)S(1)}, u32[]{:S(2)}, u32[]{:S(2)}) collective-permute-start(f32[128,1024]{1,0:T(8,128)} %constant_dynamic-slice_fusion.4), channel_id=1, source_target_pairs={{0,4},{4,0},{8,12},{12,8},{16,20},{20,16},{24,28},{28,24},{1,5},{5... | collective-permute-start | bytes 1572872 | tf_op jit(solution)/shard_map/ppermute | solution.py:865
  492.3 73.1 %collective-permute-start.15 = (bf16[2,224,1024]{2,1,0:T(8,128)(2,1)}, bf16[2,224,1024]{2,1,0:T(8,128)(2,1)}, u32[]{:S(2)}, u32[]{:S(2)}) collective-permute-start(bf16[2,224,1024]{2,1,0:T(8,128)(2,1)} %pad_maximum_fusion.8), channel_id=1, source_target_pairs={{0,4},{4,0},{8,12},{12,8},{16,20},{20,16},{24,28},{28,24},{1,5},{5... | collective-permute-start | bytes 2752520 | tf_op jit(solution)/shard_map/ppermute | solution.py:865
  521.1 11.5 %collective-permute-start.17 = (bf16[384,512]{1,0:T(8,128)(2,1)S(1)}, bf16[384,512]{1,0:T(8,128)(2,1)S(1)}, u32[]{:S(2)}, u32[]{:S(2)}) collective-permute-start(bf16[384,512]{1,0:T(8,128)(2,1)S(1)} %get-tuple-element.143), channel_id=1, source_target_pairs={{0,1},{1,2},{2,3},{3,0},{4,5},{5,6},{6,7},{7,4},{8,9},{9,10},{10,1... | collective-permute-start | bytes 1179656 | tf_op jit(solution)/shard_map/ppermute | solution.py:869
  521.2 39.0 %collective-permute-start.18 = (bf16[384,512]{1,0:T(8,128)(2,1)S(1)}, bf16[384,512]{1,0:T(8,128)(2,1)S(1)}, u32[]{:S(2)}, u32[]{:S(2)}) collective-permute-start(bf16[384,512]{1,0:T(8,128)(2,1)S(1)} %get-tuple-element.142), channel_id=1, source_target_pairs={{0,2},{1,3},{2,0},{3,1},{4,6},{5,7},{6,4},{7,5},{8,10},{9,11},{10,... | collective-permute-start | bytes 1179656 | tf_op jit(solution)/shard_map/ppermute | solution.py:869
  526.0 34.2 %collective-permute-start.19 = (bf16[384,512]{1,0:T(8,128)(2,1)S(1)}, bf16[384,512]{1,0:T(8,128)(2,1)S(1)}, u32[]{:S(2)}, u32[]{:S(2)}) collective-permute-start(bf16[384,512]{1,0:T(8,128)(2,1)S(1)} %get-tuple-element.141), channel_id=1, source_target_pairs={{0,3},{1,0},{2,1},{3,2},{4,7},{5,4},{6,5},{7,6},{8,11},{9,8},{10,9... | collective-permute-start | bytes 1179656 | tf_op jit(solution)/shard_map/ppermute | solution.py:869
  528.5 39.8 %collective-permute-start.10 = (bf16[2,224,1024]{2,1,0:T(8,128)(2,1)}, bf16[2,224,1024]{2,1,0:T(8,128)(2,1)}, u32[]{:S(2)}, u32[]{:S(2)}) collective-permute-start(bf16[2,224,1024]{2,1,0:T(8,128)(2,1)} %pad_maximum_fusion.7), channel_id=1, source_target_pairs={{0,4},{4,0},{8,12},{12,8},{16,20},{20,16},{24,28},{28,24},{1,5},{5... | collective-permute-start | bytes 2752520 | tf_op jit(solution)/shard_map/ppermute | solution.py:865
  561.5 9.8 %collective-permute-start.20 = (bf16[2,384,512]{2,1,0:T(8,128)(2,1)}, bf16[2,384,512]{2,1,0:T(8,128)(2,1)}, u32[]{:S(2)}, u32[]{:S(2)}) collective-permute-start(bf16[2,384,512]{2,1,0:T(8,128)(2,1)} %pad_maximum_fusion.9), channel_id=1, source_target_pairs={{0,4},{4,0},{8,12},{12,8},{16,20},{20,16},{24,28},{28,24},{1,5},{5... | collective-permute-start | bytes 2359304 | tf_op jit(solution)/shard_map/ppermute | solution.py:865
  (3 other events, 5.1 us)

commit v4 on v3

--- a/solution.py
+++ b/solution.py
@@ -22,7 +22,7 @@
 TN = (((0,), (0,)), ((), ()))
 
 
-def call(kernel, name, outs, args, scratch=(), flops=0, grid=None, specs=None, out_specs=None, remote=None, anywhere=(0, 0)):
+def call(kernel, name, outs, args, scratch=(), flops=0, grid=None, specs=None, out_specs=None, remote=None, anywhere=((), ())):
     out_shape = [jax.ShapeDtypeStruct(shape, dtype) for shape, dtype in outs]
     moved = sum(a.size * a.dtype.itemsize for a in args) + sum(
         math.prod(o.shape) * jnp.dtype(o.dtype).itemsize for o in out_shape
@@ -30,8 +30,8 @@
     extra = {}
     if grid is None:
         here, there = pl.BlockSpec(memory_space=pltpu.VMEM), pl.BlockSpec(memory_space=pl.ANY)
-        extra["in_specs"] = [there if i < anywhere[0] else here for i in range(len(args))]
-        extra["out_specs"] = [there if i < anywhere[1] else here for i in range(len(outs))]
+        extra["in_specs"] = [there if i in anywhere[0] else here for i in range(len(args))]
+        extra["out_specs"] = [there if i in anywhere[1] else here for i in range(len(outs))]
     else:
         extra["grid"] = grid
         extra["in_specs"], extra["out_specs"] = specs(block_whole), out_specs(block_whole)
@@ -60,14 +60,20 @@
     return lax.dot_general(a, b, dims, preferred_element_type=F32)
 
 
-def fill(weights, buffer, columns):
+def fetch(weights, buffer, columns, sem):
     rows, held = buffer.shape[0] // GROUPS, weights.shape[1] // GROUPS
+    parts = [(0, 0, buffer.shape[0])] if rows == held else [(g * held, g * rows, rows) for g in range(GROUPS)]
     for s in range(weights.shape[0]):
-        for g in range(GROUPS):
+        for src, to, size in parts:
             for which, at in columns:
-                buffer[g * rows : (g + 1) * rows, at + s * PAIR : at + (s + 1) * PAIR] = weights[
-                    s, g * held : g * held + rows, which * PAIR : (which + 1) * PAIR
-                ]
+                pltpu.make_async_copy(
+                    weights.at[s, src : src + size, which * PAIR : (which + 1) * PAIR],
+                    buffer.at[to : to + size, at + s * PAIR : at + (s + 1) * PAIR], sem,
+                ).start()
+
+
+def fetched(buffer, sem):
+    pltpu.make_async_copy(buffer, buffer, sem).wait()
 
 
 def unfill(grads, which, value):
@@ -99,17 +105,30 @@
     def y(self):
         return self.device(self.to_y, self.z)
 
-    def barrier(self):
+    def box(self, at):
+        core, x, y, step = at % 2, at // 2 % 2, at // 4 % 2, at // 8
+        f, place = self.f, 2 * self.group + self.core
+        if core:
+            f, place = f + 1 - 2 * self.core, place + 1 - 2 * self.core
+        if x:
+            f, place = f + self.to_x - self.f, place + 2 * (self.group_x - self.group)
+        if y:
+            f, place = f + self.to_y - self.f, place + 2 * (self.group_y - self.group)
+        z = (self.z, self.z + 1 - 2 * lax.rem(self.z, 2), self.z + 2 - 4 * (self.z // 2), 3 - self.z)[step]
+        return f, z, place * self.n_t + z
+
+    def barrier(self, all_of_box=False):
         sem = pltpu.get_barrier_semaphore()
-        for f in (self.to_x, self.to_y, self.to_core):
-            pl.semaphore_signal(sem, inc=1, device_id=self.device(f, self.z), device_id_type=MESH)
-        for step in (-1, 1):
-
-            @pl.when(self.has(self.z + step))
-            def _():
-                pl.semaphore_signal(sem, inc=1, device_id=self.device(self.f, self.z + step), device_id_type=MESH)
-
-        pl.semaphore_wait(sem, 3 + jnp.where(self.z > 0, 1, 0) + jnp.where(self.z < self.n_t - 1, 1, 0))
+        if all_of_box:
+            peers = [self.box(at)[:2] for at in range(1, 8 * self.n_t)]
+        else:
+            peers = [(self.to_x, self.z), (self.to_y, self.z), (self.to_core, self.z)]
+            for step in range(1, self.n_t):
+                z = lax.rem(self.z + step, self.n_t)
+                peers += [(self.f, z), (self.to_core, z)]
+        for f, z in peers:
+            pl.semaphore_signal(sem, inc=1, device_id=self.device(f, z), device_id_type=MESH)
+        pl.semaphore_wait(sem, len(peers))
 
     def has(self, z):
         return jnp.logical_and(z >= 0, z < self.n_t)
@@ -213,6 +232,216 @@
             pltpu.make_async_copy(self.own, self.rows(p.z, p.group), self.local).wait()
 
 
+class Clips:
+    @staticmethod
+    def scratch(count):
+        return [*sem_pair(count), pltpu.SemaphoreType.DMA((count,))]
+
+    def __init__(self, place, stored, here, scratch):
+        self.place, self.pairs, self.sems, self.local = place, list(zip(stored, here)), scratch[:2], scratch[2]
+
+    def copies(self, i, local):
+        p, (stored, here) = self.place, self.pairs[i]
+        src = stored.at[lax.rem(p.z, stored.shape[0])]
+        if local:
+            return pltpu.make_async_copy(src, here, self.local.at[i])
+        return remote(src, here, self.sems, i, p.device(p.to_core, p.z))
+
+    def owner(self):
+        p = self.place
+        return p.z // self.pairs[0][0].shape[0] == p.core
+
+    def start(self):
+        @pl.when(self.owner())
+        def _():
+            for i in range(len(self.pairs)):
+                self.copies(i, True).start()
+                self.copies(i, False).start()
+
+    def finish(self):
+        @pl.when(self.owner())
+        def _():
+            for i in range(len(self.pairs)):
+                self.copies(i, True).wait()
+                self.copies(i, False).wait_send()
+
+        @pl.when(jnp.logical_not(self.owner()))
+        def _():
+            for i in range(len(self.pairs)):
+                self.copies(i, False).wait_recv()
+
+
+class Spread:
+    steps = 6
+
+    @staticmethod
+    def scratch(clips):
+        return [pltpu.SemaphoreType.DMA, *sem_pair(1), pltpu.SemaphoreType.DMA((2, clips)), pltpu.SemaphoreType.DMA((clips,))]
+
+    def __init__(self, place, half, whole, scratch):
+        self.place, self.half, self.whole = place, half, whole
+        self.local, a, b, self.z_send, self.z_recv = scratch
+        self.halves = (a, b)
+        self.clips = whole.shape[0]
+        self.mine = place.z // self.clips == place.core
+
+    def columns(self, core):
+        wide = self.half.shape[1]
+        return self.whole.at[lax.rem(self.place.z, self.clips), :, pl.ds(pl.multiple_of(core * wide, 128), wide)]
+
+    def to_owner(self, core):
+        p = self.place
+        return remote(self.half, self.columns(core), self.halves, 0, p.device(p.to_core, p.z))
+
+    def along_z(self, z, step):
+        p = self.place
+        clip = lax.rem(z, self.clips)
+        return pltpu.make_async_remote_copy(
+            src_ref=self.whole.at[clip], dst_ref=self.whole.at[clip], send_sem=self.z_send.at[(step + 1) // 2, clip],
+            recv_sem=self.z_recv.at[clip], device_id=p.device(p.f, p.z + step), device_id_type=MESH,
+        )
+
+    def run(self, k):
+        p = self.place
+        if k == 0:
+            keep = pltpu.make_async_copy(self.half, self.columns(p.core), self.local)
+            pl.when(self.mine)(keep.start)
+            pl.when(jnp.logical_not(self.mine))(lambda: self.to_owner(p.core).start())
+        elif k == 1:
+
+            @pl.when(self.mine)
+            def _():
+                pltpu.make_async_copy(self.half, self.columns(p.core), self.local).wait()
+                self.to_owner(1 - p.core).wait_recv()
+                for step in (-1, 1):
+                    pl.when(p.has(p.z + step))(lambda step=step: self.along_z(p.z, step).start())
+
+        elif k <= 4:
+            for step in (-1, 1):
+                z = p.z + step * (k - 1)
+
+                @pl.when(jnp.logical_and(p.has(z), z // self.clips == p.core))
+                def _():
+                    self.along_z(z, -step).wait_recv()
+                    pl.when(p.has(p.z - step))(lambda: self.along_z(z, -step).start())
+
+        else:
+            pl.when(jnp.logical_not(self.mine))(lambda: self.to_owner(p.core).wait_send())
+            for i in range(self.clips):
+                z = p.core * self.clips + i
+                for step in (-1, 1):
+                    sent = jnp.logical_and(p.has(p.z + step), (p.z - z) * step >= 0)
+                    pl.when(sent)(lambda: self.along_z(z, step).wait_send())
+
+
+class Frames:
+    @staticmethod
+    def scratch(n_t, clips):
+        return [pltpu.SemaphoreType.DMA, pltpu.SemaphoreType.DMA((n_t,)), pltpu.SemaphoreType.DMA((clips, 2))]
+
+    def __init__(self, place, half, whole, part, scratch):
+        self.place, self.half, self.whole, self.part = place, half, whole, part
+        self.local, self.send, self.recv = scratch
+        self.clips = whole.shape[0]
+        self.mine = place.z // self.clips == place.core
+
+    def to(self, clip, core):
+        wide = self.half.shape[1]
+        return self.whole.at[clip, :, pl.ds(pl.multiple_of(core * wide, 128), wide)]
+
+    def rows(self, z):
+        return self.half.at[pl.ds(pl.multiple_of(self.part * z // 16 * 16, 16), self.whole.shape[1])]
+
+    def keep(self):
+        p = self.place
+        return pltpu.make_async_copy(self.rows(p.z), self.to(lax.rem(p.z, self.clips), p.core), self.local)
+
+    def copy(self, step):
+        p = self.place
+        clip, z = lax.rem(p.z, self.clips), lax.rem(p.z + step, p.n_t)
+        f = p.to_core if step == 0 else p.f - p.core + p.z // self.clips
+        return pltpu.make_async_remote_copy(
+            src_ref=self.rows(z), dst_ref=self.to(clip, p.core), send_sem=self.send.at[step],
+            recv_sem=self.recv.at[clip, p.core], device_id=p.device(f, z), device_id_type=MESH,
+        )
+
+    def arriving(self, clip, core):
+        p = self.place
+        return pltpu.make_async_remote_copy(
+            src_ref=self.rows(p.z), dst_ref=self.to(clip, core), send_sem=self.send.at[0],
+            recv_sem=self.recv.at[clip, core], device_id=p.device(p.to_core, p.z), device_id_type=MESH,
+        )
+
+    def start(self, step):
+        if step:
+            self.copy(step).start()
+        else:
+            pl.when(self.mine)(lambda: self.keep().start())
+            pl.when(jnp.logical_not(self.mine))(lambda: self.copy(0).start())
+
+    def finish(self):
+        p = self.place
+        for step in range(1, p.n_t):
+            self.copy(step).wait_send()
+        pl.when(self.mine)(lambda: self.keep().wait())
+        pl.when(jnp.logical_not(self.mine))(lambda: self.copy(0).wait_send())
+        for clip in range(self.clips):
+            for core in range(2):
+                own = jnp.logical_and(p.core * self.clips + clip == p.z, p.core == core)
+                pl.when(jnp.logical_not(own))(lambda: self.arriving(clip, core).wait_recv())
+
+
+class Total:
+    @staticmethod
+    def scratch(shape):
+        return [pltpu.VMEM(shape, F32), *sem_pair(shape[0]), *sem_pair(shape[0])]
+
+    def __init__(self, place, packed, total, scratch):
+        self.place, self.packed, self.total, self.came = place, packed, total, scratch[0]
+        self.to_sum, self.to_all = scratch[1:3], scratch[3:5]
+        self.me = place.box(0)[2]
+        self.peers = [place.box(at) for at in range(1, packed.shape[0])]
+
+    def out(self, peer):
+        f, z, at = peer
+        return pltpu.make_async_remote_copy(
+            src_ref=self.packed.at[at], dst_ref=self.came.at[self.me], send_sem=self.to_sum[0].at[at],
+            recv_sem=self.to_sum[1].at[self.me], device_id=self.place.device(f, z), device_id_type=MESH,
+        )
+
+    def back(self, peer):
+        f, z, at = peer
+        return pltpu.make_async_remote_copy(
+            src_ref=self.total.at[self.me], dst_ref=self.total.at[self.me], send_sem=self.to_all[0].at[at],
+            recv_sem=self.to_all[1].at[self.me], device_id=self.place.device(f, z), device_id_type=MESH,
+        )
+
+    def arrived(self, sems, buffer, peer):
+        f, z, at = peer
+        pltpu.make_async_remote_copy(
+            src_ref=buffer.at[at], dst_ref=buffer.at[at], send_sem=sems[0].at[at], recv_sem=sems[1].at[at],
+            device_id=self.place.device(f, z), device_id_type=MESH,
+        ).wait_recv()
+
+    def run(self, k):
+        if k == 0:
+            for peer in self.peers:
+                self.out(peer).start()
+            self.came[self.me] = self.packed[self.me]
+        elif k == 1:
+            for peer in self.peers:
+                self.arrived(self.to_sum, self.came, peer)
+            self.total[self.me] = jnp.sum(self.came[...], axis=0)
+        elif k == 2:
+            for peer in self.peers:
+                self.back(peer).start()
+        else:
+            for peer in self.peers:
+                self.arrived(self.to_all, self.total, peer)
+                self.out(peer).wait_send()
+                self.back(peer).wait_send()
+
+
 class Scatter:
     steps = 7
 
@@ -223,12 +452,13 @@
             pltpu.VMEM((n_t, 2, half, wide), BF16), pltpu.VMEM((n_t, 2, half, wide), BF16),
             pltpu.VMEM((n_t, half, wide), BF16), pltpu.VMEM((n_t, half, wide), BF16),
             pltpu.VMEM((n_t, size, wide), BF16), pltpu.VMEM((2, n_t, size, wide), BF16),
+            pltpu.VMEM((n_t, 4, half, wide), BF16), pltpu.SemaphoreType.DMA((n_t, 4)),
             *sem_pair(n_t, 6), *sem_pair(2, n_t),
         ]
 
     def __init__(self, place, grads, own, scratch):
         self.place, self.grads, self.own = place, grads, own
-        self.came_y, self.came_x, self.last_x, self.last_y, self.sums, self.came_z, a, b, c, d = scratch
+        self.came_y, self.came_x, self.last_x, self.last_y, self.sums, self.came_z, self.held, self.load, a, b, c, d = scratch
         self.xy, self.zs = (a, b), (c, d)
         self.half = own.shape[0] // 2
 
@@ -278,20 +508,26 @@
 
         lax.fori_loop(0, rows // step, one, 0)
 
+    def hold(self, slot, at):
+        p = self.place
+        rows = self.at((p.group_x, p.group_y, p.group, p.group)[at], (0, 1, 0, 1)[at])
+        return pltpu.make_async_copy(self.grads.at[slot, rows], self.held.at[slot, at], self.load.at[slot, at])
+
     def first(self, slot):
         for at in range(4):
             self.copy(slot, at).start()
+        for at in range(4):
+            self.hold(slot, at).start()
 
     def second(self, slot):
-        p = self.place
-        self.copy(slot, 0).wait_recv()
-        self.copy(slot, 1).wait_recv()
+        for at in range(2):
+            self.hold(slot, at).wait()
+            self.copy(slot, at).wait_recv()
 
         def body(at, step):
             to = pl.ds(at, step)
-            for came, group, half in ((self.came_y, p.group_x, 0), (self.came_x, p.group_y, 1)):
-                own = self.grads[slot, pl.ds(pl.multiple_of((2 * group + half) * self.half + at, step), step)]
-                came[slot, 1, to] = add(came[slot, 1, to], own)
+            for i, came in enumerate((self.came_y, self.came_x)):
+                came[slot, 1, to] = add(came[slot, 1, to], self.held[slot, i, to])
 
         self.over(self.half, body)
         self.copy(slot, 4).start()
@@ -301,12 +537,13 @@
         p = self.place
         for at in (2, 3, 4, 5):
             self.copy(slot, at).wait_recv()
+        for at in (2, 3):
+            self.hold(slot, at).wait()
 
         def body(at, step):
             to = pl.ds(at, step)
             for came, last, half in ((self.came_y, self.last_x, 0), (self.came_x, self.last_y, 1)):
-                own = self.grads[slot, pl.ds(pl.multiple_of((2 * p.group + half) * self.half + at, step), step)]
-                total = own.astype(F32) + came[slot, 0, to].astype(F32) + last[slot, to].astype(F32)
+                total = self.held[slot, 2 + half, to].astype(F32) + came[slot, 0, to].astype(F32) + last[slot, to].astype(F32)
                 self.sums[slot, pl.ds(pl.multiple_of(half * self.half + at, step), step)] = total.astype(BF16)
 
         self.over(self.half, body)
@@ -368,12 +605,20 @@
                     pl.when((slot - z) * (2 * way - 1) > 0)(self.along_z(slot, way).wait_send)
 
 
-def hook_of(job, first):
+def hook_of(steps):
     def hook(p, pairs):
-        for k in range(pairs):
-            pl.when(p == k)(functools.partial(job.run, first + k))
+        for k, functions in steps.items():
+
+            @pl.when(p == k)
+            def _():
+                for function in functions:
+                    function()
 
     return hook
+
+
+def step(job, k):
+    return functools.partial(job.run, k)
 
 
 def swap(place, part, came, sems):
@@ -471,7 +716,7 @@
             top = None
             for i in range(blocks):
                 rows = slice(i * size, (i + 1) * size)
-                scores = mask_scores(dot(k_ref[rows, at], queries, NT), causal, valid)
+                scores = mask_scores(dot(k_ref[rows, at], queries, NT), causal, valid - i * size)
                 score_buf[rows, :] = scores
                 now = jnp.max(scores, axis=0, keepdims=True)
                 top = now if top is None else jnp.maximum(top, now)
@@ -523,7 +768,7 @@
             keys, values = k_ref[rows, at], v_ref[rows, at]
             key_grad, value_grad = None, None
             for h in range(2):
-                chance = jnp.exp(mask_scores(dot(keys, queries[h], NT), causal, valid) - logs[h])
+                chance = jnp.exp(mask_scores(dot(keys, queries[h], NT), causal, valid - i * size) - logs[h])
                 now = dot(chance.astype(BF16), upstream[h])
                 value_grad = now if value_grad is None else value_grad + now
                 grad = dot(values, upstream[h], NT)
@@ -548,41 +793,52 @@
     lax.fori_loop(0, pairs, one_pair, 0)
 
 
-def gather_kernel(sizes, own, whole, *scratch):
+def gather_kernel(sizes, own, *refs):
+    stored, whole, here, scratch = refs[:3], refs[3], refs[4:7], refs[7:]
     place = Place(sizes)
-    job = Gather(place, own, whole, scratch)
+    clips = Clips(place, stored, here, scratch[:3])
+    job = Gather(place, own, whole, scratch[3:])
     place.barrier()
-    for k in range(Gather.steps):
+    job.run(0)
+    clips.start()
+    for k in range(1, Gather.steps):
         job.run(k)
-
-
-def gather(sizes, own):
+    clips.finish()
+
+
+def gather(sizes, own, stored):
     n_t = sizes[1]
     return call(
-        functools.partial(gather_kernel, sizes), "gather", [((n_t, GROUPS * own.shape[0], own.shape[1]), BF16)], [own],
-        scratch=Gather.scratch(n_t), remote=0, anywhere=(1, 1),
-    )[0]
+        functools.partial(gather_kernel, sizes), "gather",
+        [((n_t, GROUPS * own.shape[0], own.shape[1]), BF16)] + [(v.shape[1:], v.dtype) for v in stored], [own, *stored],
+        scratch=Clips.scratch(len(stored)) + Gather.scratch(n_t), remote=0, anywhere=((0, 1, 2, 3), (0,)),
+    )
 
 
 def self_forward_kernel(
     sizes, own, start, gain, shift, bias, weights, whole, normed, qkv, mixed, logs, part, came, w_in, w_out, score_buf,
-    sems, *scratch,
+    sems, loads, *scratch,
 ):
     place = Place(sizes)
     job = Gather(place, own, whole, scratch)
+    wide = mixed.shape[1]
+    fetch(weights, w_in, [(0, 0), (1, wide), (2, 2 * wide)], loads.at[0])
+    fetch(weights, w_out, [(3, 0)], loads.at[1])
     place.barrier()
     job.run(0)
-    wide = mixed.shape[1]
     norm_rows(lambda at: start[at, :].astype(F32), gain, shift, normed)
-    fill(weights, w_in, [(0, 0), (1, wide), (2, 2 * wide)])
-    fill(weights, w_out, [(3, 0)])
+    fetched(w_in, loads.at[0])
+    fetched(w_out, loads.at[1])
     qkv[...] = (dot(normed[...], w_in[...]) + bias[...]).astype(BF16)
+    job.run(1)
     q, k, v = (qkv.at[:, i * wide : (i + 1) * wide] for i in range(3))
-    attend(q, k, v, mixed, logs, score_buf, True, 1, start.shape[0], hook_of(job, 1))
+    attend(q, k, v, mixed, logs, score_buf, True, 1, start.shape[0], hook_of({2: [step(job, 2)]}))
     part[...] = dot(mixed[...], w_out[...], NT).astype(BF16)
-    job.run(5)
+    job.run(3)
     exchange = swap(place, part, came, sems)
     exchange.start()
+    job.run(4)
+    job.run(5)
     exchange.wait()
 
 
@@ -598,22 +854,25 @@
         [own, start, gain, shift, bias, weights],
         scratch=[
             pltpu.VMEM((d, 3 * wide), BF16), pltpu.VMEM((d, wide), BF16), pltpu.VMEM((m, m), F32),
-            pltpu.SemaphoreType.DMA((2,)), *Gather.scratch(n_t),
+            pltpu.SemaphoreType.DMA((2,)), pltpu.SemaphoreType.DMA((2,)), *Gather.scratch(n_t),
         ],
-        flops=2 * m * d * 4 * wide + 4 * m * m * wide * 2, remote=1, anywhere=(1, 1),
+        flops=2 * m * d * 4 * wide + 4 * m * m * wide * 2, remote=1, anywhere=((0, 5), (0,)),
     )
 
 
 def cross_forward_kernel(
     sizes, blocks, valid, own_weights, start, own, came, branch, gain, shift, bias, bias_kv, memory, weights,
-    whole, middle, normed, q, kv, mixed, logs, part, part_came, w_in, w_kv, w_out, score_buf, sems, *scratch,
+    whole, middle, normed, q, kv, mixed, logs, part, part_came, w_in, w_kv, w_out, score_buf, sems, loads, *scratch,
 ):
     place = Place(sizes)
     job = Gather(place, own_weights, whole, scratch)
+    wide = mixed.shape[1]
+    fetch(weights, w_kv, [(1, 0), (2, wide)], loads.at[0])
+    fetch(weights, w_in, [(0, 0)], loads.at[1])
+    fetch(weights, w_out, [(3, 0)], loads.at[2])
     place.barrier()
     job.run(0)
-    wide = mixed.shape[1]
-    fill(weights, w_kv, [(1, 0), (2, wide)])
+    fetched(w_kv, loads.at[0])
     size = memory.shape[0] // blocks
 
     def one_block(i, carry):
@@ -628,19 +887,19 @@
         lambda at: start[at, :].astype(F32) + (own[at, :].astype(F32) + came[at, :].astype(F32)) + branch_row,
         gain, shift, normed, middle,
     )
-    fill(weights, w_in, [(0, 0)])
-    fill(weights, w_out, [(3, 0)])
+    fetched(w_in, loads.at[1])
+    fetched(w_out, loads.at[2])
     q[...] = (dot(normed[...], w_in[...]) + bias[...]).astype(BF16)
 
-    def hook(p, pairs):
-        for k in range(3):
-            pl.when(p == k)(functools.partial(job.run, 2 + k))
-
-    attend(q, kv.at[:, :wide], kv.at[:, wide:], mixed, logs, score_buf, False, blocks, valid, hook)
+    attend(
+        q, kv.at[:, :wide], kv.at[:, wide:], mixed, logs, score_buf, False, blocks, valid, hook_of({1: [step(job, 2)]})
+    )
     part[...] = dot(mixed[...], w_out[...], NT).astype(BF16)
-    job.run(5)
+    job.run(3)
     exchange = swap(place, part, part_came, sems)
     exchange.start()
+    job.run(4)
+    job.run(5)
     exchange.wait()
 
 
@@ -657,9 +916,9 @@
         [own_weights, start, own, came, branch, gain, shift, bias, bias_kv, memory, weights],
         scratch=[
             pltpu.VMEM((d, wide), BF16), pltpu.VMEM((d, 2 * wide), BF16), pltpu.VMEM((d, wide), BF16),
-            pltpu.VMEM((n, m), F32), pltpu.SemaphoreType.DMA((2,)), *Gather.scratch(n_t),
+            pltpu.VMEM((n, m), F32), pltpu.SemaphoreType.DMA((2,)), pltpu.SemaphoreType.DMA((3,)), *Gather.scratch(n_t),
         ],
-        flops=2 * m * d * 2 * wide + 4 * n * d * wide + 4 * m * n * wide * 2, remote=2, anywhere=(1, 1),
+        flops=2 * m * d * 2 * wide + 4 * n * d * wide + 4 * m * n * wide * 2, remote=2, anywhere=((0, 10), (0,)),
     )
 
 
@@ -726,42 +985,48 @@
     )
 
 
-def output_kernel(later, own, came, branch, out):
-    branch_row = branch[...]
-
-    def body(at, carry):
-        out[at, :] = (later[at, :] + (own[at, :].astype(F32) + came[at, :].astype(F32)) + branch_row).astype(BF16)
-        return carry
-
-    over_rows(out.shape[0], body)(0)
-
-
 def cross_back_kernel(
     sizes, blocks, valid, own, came, later, gain, upstream, q, kv, mixed, logs, weights, normed, memory, feed_grads,
-    later_grad, sums, head_sums, part, part_came, grads, keep, send, feed_own,
-    later_low, dq, dkv, w_one, w_two, w_kv, mixed_grad, piece, sems, *scratch,
+    out_part, out_came, branch,
+    output, memory_came, later_grad, sums, head_sums, part, part_came, grads, keep, feed_own,
+    later_low, dq, dkv, w_one, w_two, w_kv, mixed_grad, piece, out_half, send, sems, memory_sems, loads, *scratch,
 ):
     place = Place(sizes)
-    job = Scatter(place, feed_grads, feed_own, scratch)
+    spread = Spread(place, out_half, output, scratch[:5])
+    job = Scatter(place, feed_grads, feed_own, scratch[5:])
+    wide = q.shape[1]
+    n, d = memory.shape
+    fetch(weights, w_one, [(3, 0)], loads.at[0])
+    fetch(weights, w_two, [(0, 0)], loads.at[1])
+    fetch(weights, w_kv, [(1, 0), (2, wide)], loads.at[2])
     place.barrier()
     job.run(0)
-    wide = q.shape[1]
-    n, d = memory.shape
-    fill(weights, w_one, [(3, 0)])
-    fill(weights, w_two, [(0, 0)])
+    out_wide = out_half.shape[1]
+    out_at = pl.ds(pl.multiple_of(place.core * out_wide, out_wide), out_wide)
+    branch_half = branch[:, out_at]
+
+    def one_row(at, carry):
+        total = later[at, out_at] + (out_part[at, out_at].astype(F32) + out_came[at, out_at].astype(F32)) + branch_half
+        out_half[at, :] = total.astype(BF16)
+        return carry
+
+    over_rows(out_half.shape[0], one_row)(0)
     norm_back_rows(own, came, later, gain, upstream, later_grad, later_low, sums)
+    spread.run(0)
+    for at, buffer in enumerate((w_one, w_two, w_kv)):
+        fetched(buffer, loads.at[at])
     mixed_grad[...] = dot(later_low[...], w_one[...]).astype(BF16)
     attend_back(
         q, kv.at[:, :wide], kv.at[:, wide:], mixed_grad, mixed, logs, dq, dkv.at[:, :wide], dkv.at[:, wide:],
-        head_sums, False, blocks, valid, hook_of(job, 1),
+        head_sums, False, blocks, valid, hook_of({0: [step(job, 1), step(spread, 1)], 2: [step(job, 2), step(spread, 2)]}),
     )
     part[...] = dot(dq[...], w_two[...], NT).astype(BF16)
-    fill(weights, w_kv, [(1, 0), (2, wide)])
     unfill(grads, 3, dot(later_low[...], mixed[...], TN).astype(BF16))
     exchange = swap(place, part, part_came, sems)
     exchange.start()
     unfill(grads, 0, dot(normed[...], dq[...], TN).astype(BF16))
-    job.run(5)
+    job.run(3)
+    spread.run(3)
     size = n // blocks
     own_half = pl.ds(pl.multiple_of(place.core * (d // 2), d // 2), d // 2)
     other_half = pl.ds(pl.multiple_of((1 - place.core) * (d // 2), d // 2), d // 2)
@@ -774,14 +1039,21 @@
         return carry
 
     lax.fori_loop(0, blocks, one_block, 0)
+    spread.run(4)
+    memory_exchange = swap(place, send, memory_came, memory_sems)
+    memory_exchange.start()
     unfill(grads, 1, dot(memory[...], dkv[:, :wide], TN).astype(BF16))
     unfill(grads, 2, dot(memory[...], dkv[:, wide:], TN).astype(BF16))
-    job.run(6)
+    for k in (4, 5, 6):
+        job.run(k)
+    spread.run(5)
     exchange.wait()
+    memory_exchange.wait()
 
 
 def cross_back(
-    sizes, own, came, later, gain, upstream, q, kv, mixed, logs, weights, normed, memory, feed_grads, blocks, valid
+    sizes, own, came, later, gain, upstream, q, kv, mixed, logs, weights, normed, memory, feed_grads, out_part, out_came,
+    branch, clips, blocks, valid,
 ):
     m, d = later.shape
     n_t = sizes[1]
@@ -789,97 +1061,138 @@
     size, feed_wide = d // GROUPS, feed_grads.shape[2]
     return call(
         functools.partial(cross_back_kernel, sizes, blocks, valid), "cross_back",
-        [((m, d), F32), ((8, d), F32), ((8, wide), F32), ((m, d), BF16), ((m, d), BF16), ((n_t, d, 4 * PAIR), BF16),
-         ((n, d // 2), BF16), ((n, d // 2), BF16), ((size, feed_wide), F32)],
-        [own, came, later, gain, upstream, q, kv, mixed, logs, weights, normed, memory, feed_grads],
+        [((clips, m, d), BF16), ((n, d // 2), BF16), ((m, d), F32), ((8, d), F32), ((8, wide), F32), ((m, d), BF16),
+         ((m, d), BF16), ((n_t, d, 4 * PAIR), BF16), ((n, d // 2), BF16), ((size, feed_wide), F32)],
+        [own, came, later, gain, upstream, q, kv, mixed, logs, weights, normed, memory, feed_grads, out_part, out_came,
+         branch],
         scratch=[
             pltpu.VMEM((m, d), BF16), pltpu.VMEM((m, wide), BF16), pltpu.VMEM((n, 2 * wide), BF16),
             pltpu.VMEM((d, wide), BF16), pltpu.VMEM((d, wide), BF16), pltpu.VMEM((d, 2 * wide), BF16),
-            pltpu.VMEM((m, wide), BF16), pltpu.VMEM((n // blocks, d), BF16), pltpu.SemaphoreType.DMA((2,)),
-            *Scatter.scratch(n_t, size, feed_wide),
+            pltpu.VMEM((m, wide), BF16), pltpu.VMEM((n // blocks, d), BF16), pltpu.VMEM((m, d // 2), BF16),
+            pltpu.VMEM((n, d // 2), BF16), pltpu.SemaphoreType.DMA((2,)), pltpu.SemaphoreType.DMA((2,)),
+            pltpu.SemaphoreType.DMA((3,)), *Spread.scratch(clips), *Scatter.scratch(n_t, size, feed_wide),
         ],
-        flops=8 * m * d * wide + 10 * m * n * wide * 2 + 8 * n * d * wide, remote=3,
+        flops=8 * m * d * wide + 10 * m * n * wide * 2 + 8 * n * d * wide, remote=3, anywhere=((9, 12), (0, 1)),
     )
 
 
 def self_back_kernel(
-    sizes, own, came, middle, gain, upstream, qkv, mixed, logs, weights, normed, cross_grads,
-    middle_grad, sums, head_sums, part, part_came, grads, cross_own,
-    middle_low, dqkv, w_in, w_out, mixed_grad, sems, *scratch,
+    sizes, frames, own, came, middle, gain, upstream, qkv, mixed, logs, weights, normed, cross_grads, keep, keep_came,
+    start, start_gain,
+    whole, half_grad, start_sums, sums, head_sums, grads, cross_own,
+    middle_grad, grad, part, part_came, middle_low, dqkv, w_in, w_out, mixed_grad, memory_sum, sems, loads, *scratch,
 ):
     place = Place(sizes)
-    job = Scatter(place, cross_grads, cross_own, scratch)
+    memory_job = Frames(place, memory_sum, whole, frames, scratch[:3])
+    job = Scatter(place, cross_grads, cross_own, scratch[3:])
+    wide = mixed.shape[1]
+    fetch(weights, w_in, [(0, 0), (1, wide), (2, 2 * wide)], loads.at[0])
+    fetch(weights, w_out, [(3, 0)], loads.at[1])
     place.barrier()
     job.run(0)
-    wide = mixed.shape[1]
-    fill(weights, w_in, [(0, 0), (1, wide), (2, 2 * wide)])
-    fill(weights, w_out, [(3, 0)])
+
+    def one_row(at, carry):
+        memory_sum[at, :] = add(keep[at, :], keep_came[at, :])
+        return carry
+
+    over_rows(memory_sum.shape[0], one_row)(0)
+    fetched(w_in, loads.at[0])
+    fetched(w_out, loads.at[1])
+    for at in (1, 3, 0):
+        memory_job.start(at)
     norm_back_rows(own, came, middle, gain, upstream, middle_grad, middle_low, sums)
+    job.run(1)
     mixed_grad[...] = dot(middle_low[...], w_out[...]).astype(BF16)
     cut = [slice(i * wide, (i + 1) * wide) for i in range(3)]
     attend_back(
         *(qkv.at[:, c] for c in cut), mixed_grad, mixed, logs, *(dqkv.at[:, c] for c in cut), head_sums, True, 1,
-        middle.shape[0], hook_of(job, 1),
+        middle.shape[0], hook_of({0: [step(job, 2)], 2: [step(job, 3)]}),
     )
     part[...] = dot(dqkv[...], w_in[...], NT).astype(BF16)
-    unfill(grads, 3, dot(middle_low[...], mixed[...], TN).astype(BF16))
+    job.run(4)
     exchange = swap(place, part, part_came, sems)
     exchange.start()
-    for which in range(3):
+    unfill(grads, 3, dot(middle_low[...], mixed[...], TN).astype(BF16))
+    unfill(grads, 0, dot(normed[...], dqkv[:, cut[0]], TN).astype(BF16))
+    job.run(5)
+    memory_job.start(2)
+    exchange.wait()
+    norm_back_rows(part, part_came, start, start_gain, middle_grad, grad, None, start_sums)
+    half = half_grad.shape[1]
+    half_grad[...] = grad[:, pl.ds(pl.multiple_of(place.core * half, half), half)]
+    for which in (1, 2):
         unfill(grads, which, dot(normed[...], dqkv[:, cut[which]], TN).astype(BF16))
-    job.run(5)
     job.run(6)
-    exchange.wait()
-
-
-def self_back(sizes, own, came, middle, gain, upstream, qkv, mixed, logs, weights, normed, cross_grads):
+    memory_job.finish()
+
+
+def self_back(
+    sizes, own, came, middle, gain, upstream, qkv, mixed, logs, weights, normed, cross_grads, keep, keep_came, start, start_gain,
+    clips, frames,
+):
     m, d = middle.shape
     n_t = sizes[1]
     wide = mixed.shape[1]
     size, cross_wide = d // GROUPS, cross_grads.shape[2]
     return call(
-        functools.partial(self_back_kernel, sizes), "self_back",
-        [((m, d), F32), ((8, d), F32), ((8, wide), F32), ((m, d), BF16), ((m, d), BF16), ((n_t, d, 4 * PAIR), BF16),
-         ((size, cross_wide), F32)],
-        [own, came, middle, gain, upstream, qkv, mixed, logs, weights, normed, cross_grads],
+        functools.partial(self_back_kernel, sizes, frames), "self_back",
+        [((clips, (frames + 30) // 16 * 16, d), BF16), ((m, d // 2), BF16), ((8, d), F32), ((8, d), F32), ((8, wide), F32),
+         ((n_t, d, 4 * PAIR), BF16), ((size, cross_wide), F32)],
+        [own, came, middle, gain, upstream, qkv, mixed, logs, weights, normed, cross_grads, keep, keep_came,
+         start, start_gain],
         scratch=[
-            pltpu.VMEM((m, d), BF16), pltpu.VMEM((m, 3 * wide), BF16), pltpu.VMEM((d, 3 * wide), BF16),
-            pltpu.VMEM((d, wide), BF16), pltpu.VMEM((m, wide), BF16), pltpu.SemaphoreType.DMA((2,)),
-            *Scatter.scratch(n_t, size, cross_wide),
+            pltpu.VMEM((m, d), F32), *[pltpu.VMEM((m, d), BF16)] * 4,
+            pltpu.VMEM((m, 3 * wide), BF16), pltpu.VMEM((d, 3 * wide), BF16),
+            pltpu.VMEM((d, wide), BF16), pltpu.VMEM((m, wide), BF16), pltpu.VMEM(keep.shape, BF16),
+            pltpu.SemaphoreType.DMA((2,)), pltpu.SemaphoreType.DMA((2,)), *Frames.scratch(n_t, clips), *Scatter.scratch(n_t, size, cross_wide),
         ],
-        flops=16 * m * d * wide + 10 * m * m * wide * 2, remote=4,
-    )
-
-
-def start_back_kernel(sizes, own, came, start, gain, upstream, self_grads, grad, sums, self_own, *scratch):
+        flops=16 * m * d * wide + 10 * m * m * wide * 2, remote=4, anywhere=((8, 10), (0,)),
+    )
+
+
+def finish_kernel(sizes, self_grads, half_grad, packed, whole, total, self_own, *scratch):
     place = Place(sizes)
-    job = Scatter(place, self_grads, self_own, scratch)
-    place.barrier()
+    spread = Spread(place, half_grad, whole, scratch[:5])
+    all_sum = Total(place, packed, total, scratch[5:10])
+    job = Scatter(place, self_grads, self_own, scratch[10:])
+    place.barrier(True)
+    all_sum.run(0)
+    spread.run(0)
     job.run(0)
-    norm_back_rows(own, came, start, gain, upstream, grad, None, sums)
-    for k in range(1, Scatter.steps):
+    spread.run(1)
+    job.run(1)
+    all_sum.run(1)
+    spread.run(2)
+    job.run(2)
+    all_sum.run(2)
+    spread.run(3)
+    job.run(3)
+    spread.run(4)
+    for k in (4, 5, 6):
         job.run(k)
+    spread.run(5)
+    all_sum.run(3)
+
+
+def finish(sizes, half_grad, self_grads, packed, clips):
+    m, half = half_grad.shape
+    n_t, d, wide = self_grads.shape
+    size = d // GROUPS
+    return call(
+        functools.partial(finish_kernel, sizes), "finish",
+        [((clips, m, 2 * half), BF16), (packed.shape, F32), ((size, wide), F32)], [self_grads, half_grad, packed],
+        scratch=[*Spread.scratch(clips), *Total.scratch(packed.shape), *Scatter.scratch(n_t, size, wide)],
+        remote=5, anywhere=((0,), (0,)),
+    )
 
 
 def flip(x, bit, size):
     return lax.ppermute(x, "fsdp", [(i, i ^ (1 << bit)) for i in range(size)])
-
-
-def turn(x, step, size):
-    return lax.ppermute(x, "tensor", [(i, (i + step) % size) for i in range(size)])
 
 
 def half(x, index, axis):
     size = x.shape[axis] // 2
     return lax.dynamic_slice_in_dim(x, index * size, size, axis=axis)
-
-
-def after(x, *waits):
-    return lax.optimization_barrier((x, *waits))[0]
-
-
-def after_all(xs, waits):
-    return lax.optimization_barrier((*xs, *waits))[: len(xs)]
 
 
 def add(a, b):
@@ -928,9 +1241,6 @@
                 more = jnp.where(low, jnp.concatenate([more, b]), jnp.concatenate([b, more]))
         return now if more is None else jnp.concatenate([now, more])
 
-    def around(now):
-        return [now] + [turn(now, s, n_t) for s in range(1, n_t)]
-
     small = jnp.concatenate(
         [v.reshape(-1) for v in (norm_gains, norm_shifts, branch_biases, hidden_bias, self_biases, cross_biases)]
     )
@@ -942,7 +1252,10 @@
     second = begin([cross_query, cross_memory[0], cross_memory[1], cross_output.T])
     third = begin([hidden_weight, reduce_weight.T])
     wide_half = units // 2
-    w_self = gather(sizes, first)
+    pad = -(-frames // 512) * 512 - frames
+    w_self, start, upstream, memory = gather(
+        sizes, first, [tokens, cotangent, jnp.pad(encoder, ((0, 0), (0, pad), (0, 0)))]
+    )
 
     rows = d // GROUPS
     table = w_self.reshape(n_t, GROUPS, -1, lanes)[:, :, rows:].reshape(n_t, n_f, -1).astype(F32)
@@ -962,19 +1275,7 @@
     kv_bias = jnp.concatenate([zero, cross_bias[1]], axis=1)
     gain, shift, branch = ([features[3 * i + j : 3 * i + j + 1] for j in range(3)] for i in range(3))
 
-    mine = core == z // own_clips
-
-    def take_clip(x):
-        x = lax.dynamic_index_in_dim(x, z % own_clips, axis=0, keepdims=False)
-        return jnp.where(mine, x, flip(x, 0, n_f))
-
     part_frames = frames // n_t
-    part_pad = -(-part_frames // 128) * 128
-    start = take_clip(tokens)
-    upstream = take_clip(cotangent)
-    memory = jnp.pad(
-        take_clip(encoder).reshape(n_t, part_frames, d), ((0, 0), (0, part_pad - part_frames), (0, 0))
-    ).reshape(n_t * part_pad, d)
 
     def scatter_end(now):
         for bit in range(bits - 3, 0, -1):
@@ -996,34 +1297,21 @@
     )
     w_feed, middle, normed_two, cross_q, kv, mixed_two, log_two, part, came = cross_forward(
         sizes, third, start, part, came, branch[0], gain[1], shift[1], cross_bias[0], kv_bias, memory, w_cross, n_t,
-        part_frames,
+        frames,
     )
     later, out_part, part, hidden_sums, g_feed = feed(
         middle, part, came, branch[1], gain[2], shift[2], upstream, hidden_slots, w_feed
     )
 
-    came = flip(part, 0, n_f)
-    (output,) = call(output_kernel, "output", [((length, d), BF16)], [later, out_part, flip(out_part, 0, n_f), branch[2]])
-    output_half = half(output, core, 0)
-    later_grad, sums_three, cross_sums, part, part_came, g_cross, memory_keep, memory_send, feed_own = cross_back(
+    came, out_came = flip(part, 0, n_f), flip(out_part, 0, n_f)
+    output, memory_came, later_grad, sums_three, cross_sums, part, part_came, g_cross, memory_keep, feed_own = cross_back(
         sizes, part, came, later, gain[2], upstream, cross_q, kv, mixed_two, log_two, w_cross, normed_two, memory,
-        g_feed, n_t, part_frames,
-    )
-    memory_sum = add(memory_keep, flip(memory_send, 0, n_f))
-    middle_grad, sums_two, self_sums, part, part_came, g_self, cross_own = self_back(
-        sizes, part, part_came, middle, gain[1], later_grad, qkv, mixed_one, log_one, w_self, normed_one, g_cross
-    )
-    size = d // GROUPS
-    start_grad, sums_one, self_own = call(
-        functools.partial(start_back_kernel, sizes), "start_back",
-        [((length, d), BF16), ((8, d), F32), ((size, 4 * PAIR), F32)],
-        [part, part_came, start, gain[0], middle_grad, g_self], scratch=Scatter.scratch(n_t, size, 4 * PAIR), remote=5,
-    )
-    start_half = half(start_grad, core, 0)
-
-    hidden_share, reduce_t = unpack(scatter_end(feed_own), [wide_half, wide_half])
-    cq_share, ck_share, cv_share, cross_out_t = unpack(scatter_end(cross_own), [PAIR] * 4)
-    q_share, k_share, v_share, self_out_t = unpack(scatter_end(self_own), [PAIR] * 4)
+        g_feed, out_part, out_came, branch[2], own_clips, n_t, frames,
+    )
+    memory_share, half_grad, sums_one, sums_two, self_sums, g_self, cross_own = self_back(
+        sizes, part, part_came, middle, gain[1], later_grad, qkv, mixed_one, log_one, w_self, normed_one, g_cross,
+        memory_keep, memory_came, start, gain[0], own_clips, part_frames,
+    )
 
     lead = jnp.where(core == 0, 1.0, 0.0).astype(F32)
     feature_sums = jnp.stack(
@@ -1040,11 +1328,12 @@
         return v[:2].reshape(2, n_t, -1).transpose(1, 0, 2)
 
     unit_sums = [from_slots(hidden_sums[:, :1]), from_slots(by_slot(self_sums)), from_slots(by_slot(cross_sums))]
-    packed = jnp.concatenate([feature_sums.reshape(-1)] + [u.reshape(-1) for u in unit_sums]).reshape(-1, 1024)
-    for bit in range(bits):
+    packed = jnp.concatenate([feature_sums.reshape(-1)] + [u.reshape(-1) for u in unit_sums])
+    boxes = -(-packed.size // (32 * 1024))
+    packed = jnp.pad(packed.reshape(-1), (0, boxes * 32 * 1024 - packed.size)).reshape(32, 8 * boxes, 128)
+    tokens_grad, packed, self_own = finish(sizes, half_grad, g_self, packed, own_clips)
+    for bit in range(1, bits - 2):
         packed = packed + flip(packed, bit, n_f)
-    for step in (1, 2):
-        packed = packed + lax.ppermute(packed, "tensor", [(i, i ^ step) for i in range(n_t)])
     packed = packed.reshape(-1)
     feature_share = lax.dynamic_slice(packed[: 9 * d].reshape(9, d), (0, f * per), (9, per))
 
@@ -1059,33 +1348,16 @@
     at += 2 * n_t * heads_here * n_f
     cross_bias_share = unit_share(at, 2, heads_here * n_f)
 
-    def own_of(slots, c):
-        stacked = jnp.stack(slots)
-        return jnp.stack(
-            [
-                lax.dynamic_index_in_dim(stacked, (z - c * own_clips - i) % n_t, axis=0, keepdims=False)
-                for i in range(own_clips)
-            ]
-        )
-
-    def join(slots, axis):
-        keep, came = own_of(slots, core), flip(own_of(slots, 1 - core), 0, n_f)
-        return jnp.where(core == 0, jnp.concatenate([keep, came], axis), jnp.concatenate([came, keep], axis))
-
-    def spread_clip(x):
-        return join(around(x), 1)
-
-    summed = memory_sum.reshape(n_t, part_pad, d // 2)
-    slots = []
-    for s in range(n_t):
-        block = lax.dynamic_index_in_dim(summed, (z + s) % n_t, axis=0, keepdims=False)
-        slots.append(turn(block, s, n_t) if s else block)
-    memory_share = join(slots, 2)
+    hidden_share, reduce_t = unpack(scatter_end(feed_own), [wide_half, wide_half])
+    cq_share, ck_share, cv_share, cross_out_t = unpack(scatter_end(cross_own), [PAIR] * 4)
+    q_share, k_share, v_share, self_out_t = unpack(scatter_end(self_own), [PAIR] * 4)
+
+    memory_share = lax.dynamic_slice_in_dim(memory_share, part_frames * z % 16, part_frames, axis=1)
 
     return (
-        spread_clip(output_half),
-        spread_clip(start_half),
-        memory_share[:, :part_frames],
+        output,
+        tokens_grad,
+        memory_share,
         jnp.stack([q_share, k_share, v_share]),
         self_bias_share,
         self_out_t.T,

time: 586 us -> 487 us (0.83)
  the two profiles are of different devices: /device:TPU:25 before, /device:TPU:0 now
where the time goes in v4:
time: 487 us; the launch traced here: 478 us
  Pallas kernels  415 us (85%)
  local copies, waits for them, and re-layouts  43.7 us (9%)
  other arithmetic  8.17 us (2%)
  starting transfers between devices  6.54 us (1%)
    pallas_call x7, Pallas kernels, call(): pl.pallas_call(kernel, name=name, out_shape=out_shape, scratch_shapes=lis...  415 us
    unnamed x35, local copies, waits for them, and re-layouts  14 us
  transfers between devices with their start and end apart: 8, of which 2 were waited for; matrix products, arithmetic and copies ran while one was open for 7% of the time, Pallas kernels for 19%

profile of v4, /device:TPU:0, one launch (start us, length us, event | category | flops | bytes accessed | tf_op | source)
XLA Modules:
  0.0 477.6 jit_solution(4192812096915683333)
XLA Ops:
  0.7 0.9 constant_dynamic-slice_fusion.17
  1.7 0.9 fusion.15
  3.2 0.7 reshape.426
  3.9 0.7 reshape.427
  4.7 2.8 concatenate.216
  7.5 0.8 constant_dynamic-slice_fusion.20
  8.4 0.9 fusion.13
  10.7 4.7 copy.36
  15.4 3.3 pad.14.refs_2_
  18.7 0.8 maximum_select_fusion.4.own
  19.6 0.7 pad_maximum_fusion.1.own
  20.3 49.5 %gather.1 = (bf16[4,1152,512]{2,1,0:T(8,128)(2,1)}, bf16[448,1024]{1,0:T(8,128)(2,1)}, bf16[448,1024]{1,0:T(8,128)(2,1)}, bf16[1536,1024]{1,0:T(8,128)(2,1)}) custom-call(bf16[288,512]{1,0:T(8,128)(2,1)} %pad_maximum_fusion.1.own, bf16[2,448,1024]{2,1,0:T(8,128)(2,1)} %refs_0_.1, bf16[2,448,1024]{2,1,0:T(8,128)(2,1)} %refs_1_.1, ...), custom_call_target="tpu_custom_call" | custom-call | bytes 19955712 | tf_op jit(solution)/shard_map/gather/pallas_call | solution.py:42
  69.9 1.2 slice_convert_fusion
  74.7 43.5 %self_forward.1 = (bf16[4,1024,512]{2,1,0:T(8,128)(2,1)}, bf16[448,1024]{1,0:T(8,128)(2,1)}, bf16[448,1536]{1,0:T(8,128)(2,1)}, bf16[448,512]{1,0:T(8,128)(2,1)}...) custom-call(bf16[256,512]{1,0:T(8,128)(2,1)} %maximum_select_fusion.4.own, ...), custom_call_target="tpu_custom_call" | custom-call | flops 2701131776 | bytes 14809088 | tf_op jit(solution)/shard_map/self_forward/pallas_call | solution.py:42
  118.2 0.9 maximum_select_fusion.own_weights
  119.1 79.4 %cross_forward.1 = (bf16[4,1024,1024]{2,1,0:T(8,128)(2,1)}, f32[448,1024]{1,0:T(8,128)}, bf16[448,1024]{1,0:T(8,128)(2,1)}, bf16[448,512]{1,0:T(8,128)(2,1)}, bf...) custom-call(bf16[256,1024]{1,0:T(8,128)(2,1)} %maximum_select_fusion, ...), custom_call_target="tpu_custom_call" | custom-call | flops 6979321856 | bytes 27789312 | tf_op jit(solution)/shard_map/cross_forward/pallas_call | solution.py:42
  198.5 20.7 %feed_forward_and_back.1 = (f32[448,1024]{1,0:T(8,128)}, bf16[448,1024]{1,0:T(8,128)(2,1)}, bf16[448,1024]{1,0:T(8,128)(2,1)}, f32[4,8,512]{2,1,0:T(8,128)}, bf16[4,1024,1024]{2,1,0:T(8,128)(2,1)}) custom-call(f32[448,1024]{1,0:T(8,128)} %get-tuple-element.67.middle, bf16[448,1024]{1,0:T(8,128)(2,1)} %get-tuple-element.68.own, ...), custom_call_target="tpu_custom_call" | custom-call | flops 11274289152 | bytes 25120768 | tf_op jit(solution)/shard_map/feed_forward_and_back/pallas_call | solution.py:42
  219.8 0.9 constant_dynamic-update-slice_fusion.2
  220.7 1.3 collective-permute-done.3.came
  222.0 1.4 collective-permute-done.4.out_came
  223.4 92.2 %cross_back.1 = (bf16[2,448,1024]{2,1,0:T(8,128)(2,1)}, bf16[1536,512]{1,0:T(8,128)(2,1)}, f32[448,1024]{1,0:T(8,128)}, f32[8,1024]{1,0:T(8,128)}, f32[8,512]{1,...) custom-call(bf16[448,1024]{1,0:T(8,128)(2,1)} %get-tuple-element.72., ...), custom_call_target="tpu_custom_call" | custom-call | flops 15367929856 | bytes 41197568 | tf_op jit(solution)/shard_map/cross_back/pallas_call | solution.py:42
  315.6 0.8 slice.267
  316.3 0.8 fusion.19
  317.2 66.8 %self_back.1 = (bf16[2,400,1024]{2,1,0:T(8,128)(2,1)}, bf16[448,512]{1,0:T(8,128)(2,1)}, f32[8,1024]{1,0:T(8,128)}, f32[8,1024]{1,0:T(8,128)}, f32[8,512]{1,0:T(...) custom-call(bf16[448,1024]{1,0:T(8,128)(2,1)} %get-tuple-element.82.own, ...), custom_call_target="tpu_custom_call" | custom-call | flops 5813305344 | bytes 28254208 | tf_op jit(solution)/shard_map/self_back/pallas_call | solution.py:42
  384.0 0.7 slice.269
  384.8 0.7 slice.270
  385.5 0.8 fusion.20
  386.4 0.9 fusion.18
  388.1 63.0 %finish.1 = (bf16[2,448,1024]{2,1,0:T(8,128)(2,1)}, f32[32,8,128]{2,1,0:T(8,128)}, f32[256,512]{1,0:T(8,128)}) custom-call(bf16[4,1024,512]{2,1,0:T(8,128)(2,1)} %get-tuple-element.92.self_grads, bf16[448,512]{1,0:T(8,128)(2,1)} %get-tuple-element.93.half_grad, f32[32,8,128]{2,1,0:T(8,128)} %fusion.1.packed), custom_call_target="tpu_custom_call" | custom-call | bytes 7274496 | tf_op jit(solution)/shard_map/finish/pallas_call | solution.py:42
  451.2 0.8 slice.291
  452.0 0.7 fusion.14
  452.8 0.8 slice.294
  454.9 1.0 constant_dynamic-slice_fusion.10
  455.9 4.3 collective-permute-start.6
  460.3 1.9 constant_dynamic-slice_fusion.5
  463.7 0.7 fusion.16
  464.4 2.7 copy.41
  467.3 0.7 maximum_select_fusion.9
  468.0 0.8 copy.43
  468.8 0.8 copy.42
  469.6 0.7 pad_maximum_fusion.3
  470.3 0.8 pad_maximum_fusion
  471.1 1.1 fusion.8
  472.2 1.0 copy.44
  473.2 0.8 maximum_select_fusion.1
  474.1 1.2 copy.62
  475.3 0.9 copy-done.1
  476.2 1.2 copy.63
  (104 shorter events, 10.5 us)
Async XLA Ops:
  0.6 8.9 %copy-start.6 = (bf16[128,1024]{1,0:T(8,128)(2,1)S(1)}, bf16[128,1024]{1,0:T(8,128)(2,1)}, u32[]{:S(2)}) copy-start(bf16[128,1024]{1,0:T(8,128)(2,1)} %param.26) | copy-start | bytes 786436
  0.7 8.9 %copy-start.7 = (bf16[1024,128]{1,0:T(8,128)(2,1)S(1)}, bf16[1024,128]{1,0:T(8,128)(2,1)}, u32[]{:S(2)}) copy-start(bf16[1024,128]{1,0:T(8,128)(2,1)} %param.28) | copy-start | bytes 786436
  2.6 16.1 %collective-permute-start.2 = (bf16[128,512]{1,0:T(8,128)(2,1)S(1)}, bf16[128,512]{1,0:T(8,128)(2,1)S(1)}, u32[]{:S(2)}, u32[]{:S(2)}) collective-permute-start(bf16[128,512]{1,0:T(8,128)(2,1)S(1)} %pad_maximum_fusion.5), channel_id=1, source_target_pairs={{0,4},{4,0},{8,12},{12,8},{16,20},{20,16},{24,28},{28,24},{1,5},{5... | collective-permute-start | bytes 393224 | tf_op jit(solution)/shard_map/ppermute | solution.py:1190
  9.5 10.0 %collective-permute-start.1 = (bf16[144,512]{1,0:T(8,128)(2,1)S(1)}, bf16[144,512]{1,0:T(8,128)(2,1)S(1)}, u32[]{:S(2)}, u32[]{:S(2)}) collective-permute-start(bf16[144,512]{1,0:T(8,128)(2,1)S(1)} %pad_maximum_fusion.4), channel_id=1, source_target_pairs={{0,4},{4,0},{8,12},{12,8},{16,20},{20,16},{24,28},{28,24},{1,5},{5... | collective-permute-start | bytes 442376 | tf_op jit(solution)/shard_map/ppermute | solution.py:1190
  9.8 108.4 %collective-permute-start = (bf16[128,1024]{1,0:T(8,128)(2,1)S(1)}, bf16[128,1024]{1,0:T(8,128)(2,1)S(1)}, u32[]{:S(2)}, u32[]{:S(2)}) collective-permute-start(bf16[128,1024]{1,0:T(8,128)(2,1)S(1)} %pad_maximum_fusion.2), channel_id=1, source_target_pairs={{0,4},{4,0},{8,12},{12,8},{16,20},{20,16},{24,28},{28,24},{1,5},{5... | collective-permute-start | bytes 786440 | tf_op jit(solution)/shard_map/ppermute | solution.py:1190
  219.2 2.7 collective-permute-start.3
  219.3 4.1 collective-permute-start.4
  222.0 1.4 copy-start.8
  388.1 67.7 %copy-start.4 = (f32[256,512]{1,0:T(8,128)S(1)}, f32[256,512]{1,0:T(8,128)}, u32[]{:S(2)}) copy-start(f32[256,512]{1,0:T(8,128)} %get-tuple-element.104) | copy-start | bytes 1572868
  451.2 12.0 %copy-start.2 = (bf16[2,400,1024]{2,1,0:T(8,128)(2,1)S(1)}, bf16[2,400,1024]{2,1,0:T(8,128)(2,1)}, u32[]{:S(2)}) copy-start(bf16[2,400,1024]{2,1,0:T(8,128)(2,1)} %get-tuple-element.101) | copy-start | bytes 4915204
  455.9 11.3 %collective-permute-start.6 = (f32[128,512]{1,0:T(8,128)S(1)}, f32[128,512]{1,0:T(8,128)S(1)}, u32[]{:S(2)}, u32[]{:S(2)}) collective-permute-start(f32[128,512]{1,0:T(8,128)S(1)} %constant_dynamic-slice_fusion.7), channel_id=1, source_target_pairs={{0,4},{4,0},{8,12},{12,8},{16,20},{20,16},{24,28},{28,24},{1,5},{5... | collective-permute-start | bytes 786440 | tf_op jit(solution)/shard_map/ppermute | solution.py:1190
  460.2 7.8 %collective-permute-start.5 = (f32[128,512]{1,0:T(8,128)S(1)}, f32[128,512]{1,0:T(8,128)S(1)}, u32[]{:S(2)}, u32[]{:S(2)}) collective-permute-start(f32[128,512]{1,0:T(8,128)S(1)} %constant_dynamic-slice_fusion.10), channel_id=1, source_target_pairs={{0,4},{4,0},{8,12},{12,8},{16,20},{20,16},{24,28},{28,24},{1,5},{5... | collective-permute-start | bytes 786440 | tf_op jit(solution)/shard_map/ppermute | solution.py:1190
  460.3 3.4 copy-start.5
  462.2 8.9 %collective-permute-start.7 = (f32[128,1024]{1,0:T(8,128)}, f32[128,1024]{1,0:T(8,128)}, u32[]{:S(2)}, u32[]{:S(2)}) collective-permute-start(f32[128,1024]{1,0:T(8,128)} %constant_dynamic-slice_fusion.5), channel_id=1, source_target_pairs={{0,4},{4,0},{8,12},{12,8},{16,20},{20,16},{24,28},{28,24},{1,5},{5... | collective-permute-start | bytes 1572872 | tf_op jit(solution)/shard_map/ppermute | solution.py:1190
  463.7 3.4 copy-start.3
  472.2 1.9 copy-start
  474.1 2.2 copy-start.1

commit v5 on v4

--- a/solution.py
+++ b/solution.py
@@ -130,6 +130,19 @@
             pl.semaphore_signal(sem, inc=1, device_id=self.device(f, z), device_id_type=MESH)
         pl.semaphore_wait(sem, len(peers))
 
+    def slot(self, k):
+        z, last = self.z, self.n_t - 1
+        low = z * 2 <= last
+        far, near = jnp.where(low, last, 0), jnp.where(low, 0, last)
+        inward = jnp.where(low, 1, -1)
+        if k == 0:
+            return far
+        if k == last:
+            return z
+        if k == last - 1:
+            return z + inward
+        return jnp.where(jnp.logical_or(z == 0, z == last), z + 2 * inward, near)
+
     def has(self, z):
         return jnp.logical_and(z >= 0, z < self.n_t)
 
@@ -199,7 +212,11 @@
             slot = p.z + step * r
             pl.when(p.has(slot))(functools.partial(act, slot, step))
 
-    def run(self, k):
+    def complete(self, slot):
+        for at in (1, 3, 4, 5):
+            self.copy(slot, at).wait_recv()
+
+    def run(self, k, arrivals=True):
         p = self.place
         if k == 0:
             for step in (-1, 1):
@@ -218,18 +235,18 @@
             self.arrived(k, passed)
         if k == 1:
             self.forward_xy(p.z)
+            pltpu.make_async_copy(self.own, self.rows(p.z, p.group), self.local).wait()
         elif k <= 4:
             self.arrived(k - 1, lambda slot, step: self.forward_xy(slot))
         else:
             for slot in range(p.n_t):
-                for at in (1, 3, 4, 5):
-                    self.copy(slot, at).wait_recv()
+                if arrivals:
+                    self.complete(slot)
                 for at in range(6):
                     self.copy(slot, at).wait_send()
                 for step in (-1, 1):
                     sent = jnp.logical_and(p.has(p.z + step), (p.z - slot) * step >= 0)
                     pl.when(sent)(self.along_z(slot, step).wait_send)
-            pltpu.make_async_copy(self.own, self.rows(p.z, p.group), self.local).wait()
 
 
 class Clips:
@@ -462,21 +479,6 @@
         self.xy, self.zs = (a, b), (c, d)
         self.half = own.shape[0] // 2
 
-    def slot(self, k):
-        z = self.place.z
-        last = self.place.n_t - 1
-        low = z * 2 <= last
-        far, near = jnp.where(low, last, 0), jnp.where(low, 0, last)
-        edge = jnp.logical_or(z == 0, z == last)
-        inward = jnp.where(low, 1, -1)
-        if k == 0:
-            return far
-        if k == last:
-            return z
-        if k == last - 1:
-            return z + inward
-        return jnp.where(edge, z + 2 * inward, near)
-
     def at(self, group, half):
         return pl.ds(pl.multiple_of((2 * group + half) * self.half, 16), self.half)
 
@@ -568,15 +570,15 @@
         p = self.place
         n = p.n_t
         if k == 0:
-            self.first(self.slot(0))
-            self.first(self.slot(1))
+            self.first(self.place.slot(0))
+            self.first(self.place.slot(1))
             return
         if k <= n:
-            self.second(self.slot(k - 1))
+            self.second(self.place.slot(k - 1))
         if k + 1 < n:
-            self.first(self.slot(k + 1))
+            self.first(self.place.slot(k + 1))
         if 2 <= k <= n + 1:
-            self.third(self.slot(k - 2))
+            self.third(self.place.slot(k - 2))
         if k == n + 2:
             z = p.z
 
@@ -862,7 +864,10 @@
 
 def cross_forward_kernel(
     sizes, blocks, valid, own_weights, start, own, came, branch, gain, shift, bias, bias_kv, memory, weights,
-    whole, middle, normed, q, kv, mixed, logs, part, part_came, w_in, w_kv, w_out, score_buf, sems, loads, *scratch,
+    branch_two, gain_two, shift_two, upstream, hidden_bias,
+    grads, middle, normed, q, kv, mixed, logs, later, out_part, out_came, grad_part, grad_came, sums,
+    whole, normed_three, out_acc, grad_acc, stage, part, part_came, w_in, w_kv, w_out, score_buf, sems, loads, stores,
+    out_sems, grad_sems, *scratch,
 ):
     place = Place(sizes)
     job = Gather(place, own_weights, whole, scratch)
@@ -895,93 +900,85 @@
         q, kv.at[:, :wide], kv.at[:, wide:], mixed, logs, score_buf, False, blocks, valid, hook_of({1: [step(job, 2)]})
     )
     part[...] = dot(mixed[...], w_out[...], NT).astype(BF16)
+    exchange = swap(place, part, part_came, sems)
     job.run(3)
-    exchange = swap(place, part, part_came, sems)
     exchange.start()
-    job.run(4)
-    job.run(5)
+    out_acc[...] = jnp.zeros(out_acc.shape, F32)
+    grad_acc[...] = jnp.zeros(grad_acc.shape, F32)
     exchange.wait()
-
-
-def cross_forward(sizes, own_weights, start, own, came, branch, gain, shift, bias, bias_kv, memory, weights, blocks, valid):
+    branch_two_row = branch_two[...]
+    norm_rows(
+        lambda at: middle[at, :] + (part[at, :].astype(F32) + part_came[at, :].astype(F32)) + branch_two_row,
+        gain_two, shift_two, normed_three, later,
+    )
+    slots, width = place.n_t, hidden_bias.shape[2]
+    order = [place.slot(slots - 1 - i) for i in range(slots)]
+
+    def store(i, slot):
+        return pltpu.make_async_copy(stage.at[lax.rem(i, 2)], grads.at[slot], stores.at[lax.rem(i, 2)])
+
+    def one_slot(i, carry):
+        slot = order[-1]
+        for at in range(slots - 1):
+            slot = jnp.where(i == at, order[at], slot)
+        pl.when(i == slots - 1)(step(job, 4))
+        job.complete(slot)
+        pl.when(i >= 2)(lambda: store(i, slot).wait())
+        expanded = dot(normed_three[...], whole[slot, :, :width]) + hidden_bias[slot]
+        phi = 0.5 * (1.0 + lax.erf(expanded * (0.5**0.5)))
+        activated = (expanded * phi).astype(BF16)
+        density = jnp.exp(expanded * expanded * -0.5) * ((2.0 * math.pi) ** -0.5)
+        slope = phi + expanded * density
+        expanded_grad = dot(upstream[...], whole[slot, :, width:]) * slope
+        expanded_low = expanded_grad.astype(BF16)
+        sums[slot] = jnp.broadcast_to(jnp.sum(expanded_grad, axis=0, keepdims=True), sums.shape[1:])
+        out_acc[...] += dot(activated, whole[slot, :, width:], NT)
+        grad_acc[...] += dot(expanded_low, whole[slot, :, :width], NT)
+        held = stage.at[lax.rem(i, 2)]
+        held[:, :width] = dot(normed_three[...], expanded_low, TN).astype(BF16)
+        held[:, width:] = dot(upstream[...], activated, TN).astype(BF16)
+        store(i, slot).start()
+        return carry
+
+    lax.fori_loop(0, slots, one_slot, 0)
+    grad_part[...] = grad_acc[...].astype(BF16)
+    out_part[...] = out_acc[...].astype(BF16)
+    job.run(5, False)
+    grad_exchange = swap(place, grad_part, grad_came, grad_sems)
+    out_exchange = swap(place, out_part, out_came, out_sems)
+    grad_exchange.start()
+    out_exchange.start()
+    store(0, 0).wait()
+    store(1, 0).wait()
+    grad_exchange.wait()
+    out_exchange.wait()
+
+
+def cross_forward(
+    sizes, own_weights, start, own, came, branch, gain, shift, bias, bias_kv, memory, weights, branch_two, gain_two,
+    shift_two, upstream, hidden_bias, blocks, valid,
+):
     m, d = start.shape
     n_t = sizes[1]
     n, wide = memory.shape[0], bias.shape[1]
+    feed_wide = own_weights.shape[1]
     heads = wide // HEAD_DIM
     return call(
-        functools.partial(cross_forward_kernel, sizes, blocks, valid), "cross_forward",
-        [((n_t, GROUPS * own_weights.shape[0], own_weights.shape[1]), BF16), ((m, d), F32), ((m, d), BF16),
-         ((m, wide), BF16), ((n, 2 * wide), BF16), ((m, wide), BF16), ((heads, 8, m), F32), ((m, d), BF16),
-         ((m, d), BF16)],
-        [own_weights, start, own, came, branch, gain, shift, bias, bias_kv, memory, weights],
+        functools.partial(cross_forward_kernel, sizes, blocks, valid), "cross_and_feed",
+        [((n_t, d, feed_wide), BF16), ((m, d), F32), ((m, d), BF16),
+         ((m, wide), BF16), ((n, 2 * wide), BF16), ((m, wide), BF16), ((heads, 8, m), F32), ((m, d), F32)]
+        + [((m, d), BF16)] * 4 + [((n_t, 8, feed_wide // 2), F32)],
+        [own_weights, start, own, came, branch, gain, shift, bias, bias_kv, memory, weights, branch_two, gain_two,
+         shift_two, upstream, hidden_bias],
         scratch=[
+            pltpu.VMEM((n_t, GROUPS * own_weights.shape[0], feed_wide), BF16), pltpu.VMEM((m, d), BF16),
+            pltpu.VMEM((m, d), F32), pltpu.VMEM((m, d), F32), pltpu.VMEM((2, d, feed_wide), BF16),
+            pltpu.VMEM((m, d), BF16), pltpu.VMEM((m, d), BF16),
             pltpu.VMEM((d, wide), BF16), pltpu.VMEM((d, 2 * wide), BF16), pltpu.VMEM((d, wide), BF16),
-            pltpu.VMEM((n, m), F32), pltpu.SemaphoreType.DMA((2,)), pltpu.SemaphoreType.DMA((3,)), *Gather.scratch(n_t),
+            pltpu.VMEM((n, m), F32), pltpu.SemaphoreType.DMA((2,)), pltpu.SemaphoreType.DMA((3,)),
+            *[pltpu.SemaphoreType.DMA((2,))] * 3, *Gather.scratch(n_t),
         ],
-        flops=2 * m * d * 2 * wide + 4 * n * d * wide + 4 * m * n * wide * 2, remote=2, anywhere=((0, 10), (0,)),
-    )
-
-
-def feed_kernel(
-    slots, middle, own, came, branch, gain, shift, upstream, bias, weights,
-    later, out_part, grad_part, sums, grads, normed, out_acc, grad_acc,
-):
-    s = pl.program_id(0)
-    width = bias.shape[1]
-    w_hidden, w_reduce = weights.at[:, :width], weights.at[:, width:]
-
-    @pl.when(s == 0)
-    def _():
-        branch_row = branch[...]
-        norm_rows(
-            lambda at: middle[at, :] + (own[at, :].astype(F32) + came[at, :].astype(F32)) + branch_row,
-            gain, shift, normed, later,
-        )
-
-    expanded = dot(normed[...], w_hidden[...]) + bias[...]
-    phi = 0.5 * (1.0 + lax.erf(expanded * (0.5**0.5)))
-    activated = (expanded * phi).astype(BF16)
-    density = jnp.exp(expanded * expanded * -0.5) * ((2.0 * math.pi) ** -0.5)
-    slope = phi + expanded * density
-    expanded_grad = dot(upstream[...], w_reduce[...]) * slope
-    expanded_low = expanded_grad.astype(BF16)
-    sums[...] = jnp.broadcast_to(jnp.sum(expanded_grad, axis=0, keepdims=True), sums.shape)
-    out_now = dot(activated, w_reduce[...], NT)
-    grad_now = dot(expanded_low, w_hidden[...], NT)
-
-    @pl.when(s == 0)
-    def _():
-        out_acc[...] = out_now
-        grad_acc[...] = grad_now
-
-    @pl.when(jnp.logical_and(s > 0, s < slots - 1))
-    def _():
-        out_acc[...] += out_now
-        grad_acc[...] += grad_now
-
-    @pl.when(s == slots - 1)
-    def _():
-        out_part[...] = (out_acc[...] + out_now).astype(BF16)
-        grad_part[...] = (grad_acc[...] + grad_now).astype(BF16)
-
-    grads[:, :width] = dot(normed[...], expanded_low, TN).astype(BF16)
-    grads[:, width:] = dot(upstream[...], activated, TN).astype(BF16)
-
-
-def feed(middle, own, came, branch, gain, shift, upstream, bias, weights):
-    m, d = middle.shape
-    slots, _, width = bias.shape
-    piece = pl.BlockSpec((None, d, 2 * width), lambda s: (s, 0, 0))
-    args = [middle, own, came, branch, gain, shift, upstream]
-    return call(
-        functools.partial(feed_kernel, slots), "feed_forward_and_back",
-        [((m, d), F32), ((m, d), BF16), ((m, d), BF16), ((slots, 8, width), F32), ((slots, d, 2 * width), BF16)],
-        [*args, bias, weights],
-        scratch=[pltpu.VMEM((m, d), BF16), pltpu.VMEM((m, d), F32), pltpu.VMEM((m, d), F32)],
-        flops=12 * m * d * slots * width, grid=(slots,),
-        specs=lambda whole: [whole(a.shape) for a in args]
-        + [pl.BlockSpec((None, 1, width), lambda s: (s, 0, 0)), piece],
-        out_specs=lambda whole: [whole((m, d))] * 3 + [pl.BlockSpec((None, 8, width), lambda s: (s, 0, 0)), piece],
+        flops=6 * m * d * feed_wide * n_t + 2 * m * d * 2 * wide + 4 * n * d * wide + 4 * m * n * wide * 2, remote=2, anywhere=((0, 10), (0,)),
     )
 
 
@@ -1295,15 +1292,13 @@
     w_cross, normed_one, qkv, mixed_one, log_one, part, came = self_forward(
         sizes, second, start, gain[0], shift[0], qkv_bias, w_self
     )
-    w_feed, middle, normed_two, cross_q, kv, mixed_two, log_two, part, came = cross_forward(
-        sizes, third, start, part, came, branch[0], gain[1], shift[1], cross_bias[0], kv_bias, memory, w_cross, n_t,
-        frames,
-    )
-    later, out_part, part, hidden_sums, g_feed = feed(
-        middle, part, came, branch[1], gain[2], shift[2], upstream, hidden_slots, w_feed
-    )
-
-    came, out_came = flip(part, 0, n_f), flip(out_part, 0, n_f)
+    (
+        g_feed, middle, normed_two, cross_q, kv, mixed_two, log_two, later, out_part, out_came, part, came, hidden_sums,
+    ) = cross_forward(
+        sizes, third, start, part, came, branch[0], gain[1], shift[1], cross_bias[0], kv_bias, memory, w_cross, branch[1],
+        gain[2], shift[2], upstream, hidden_slots, n_t, frames,
+    )
+
     output, memory_came, later_grad, sums_three, cross_sums, part, part_came, g_cross, memory_keep, feed_own = cross_back(
         sizes, part, came, later, gain[2], upstream, cross_q, kv, mixed_two, log_two, w_cross, normed_two, memory,
         g_feed, out_part, out_came, branch[2], own_clips, n_t, frames,

time: 487 us -> 475 us (0.975)
  Pallas kernels: 415 us -> 406 us
    pallas_call x7 -> x6, Pallas kernels: 415 us -> 406 us  [call(): pl.pallas_call(kernel, name=name, out_shape=out_shape, scratch_shapes=lis...]
    unnamed x35 -> x33, local copies, waits for them, and re-layouts: 14 us -> 14 us
  transfers between devices with their start and end apart: 8 -> 6, of which waited for: 2 -> 0; matrix products, arithmetic and copies ran while one was open for 7% -> 7% of each run, Pallas kernels for 19% -> 20%
where the time goes in v5:
time: 475 us; the launch traced here: 466 us
  Pallas kernels  406 us (85%)
  local copies, waits for them, and re-layouts  43.7 us (9%)
  other arithmetic  8.16 us (2%)
  starting transfers between devices  6.45 us (1%)
    pallas_call x6, Pallas kernels, call(): pl.pallas_call(kernel, name=name, out_shape=out_shape, scratch_shapes=lis...  406 us
    unnamed x33, local copies, waits for them, and re-layouts  14 us
  transfers between devices with their start and end apart: 6, of which 0 were waited for; matrix products, arithmetic and copies ran while one was open for 7% of the time, Pallas kernels for 20%

profile of v5, /device:TPU:0, one launch (start us, length us, event | category | flops | bytes accessed | tf_op | source)
XLA Modules:
  0.0 465.9 jit_solution(5344141270365655016)
XLA Ops:
  0.7 0.9 constant_dynamic-slice_fusion.17
  1.7 0.9 fusion.15
  3.2 0.7 reshape.426
  3.9 0.7 reshape.427
  4.7 2.8 concatenate.216
  7.5 0.8 constant_dynamic-slice_fusion.20
  8.4 0.9 fusion.13
  10.7 4.7 %copy.36 = bf16[2,1500,1024]{2,1,0:T(8,128)(2,1)S(1)} copy(bf16[2,1500,1024]{2,0,1:T(2,128)(2,1)} %param.17) | data formatting | bytes 12288000 | tf_op args[1]
  15.4 3.4 pad.14.refs_2_
  18.8 0.8 maximum_select_fusion.4.own
  19.6 0.7 pad_maximum_fusion.1.own
  20.4 49.5 %gather.1 = (bf16[4,1152,512]{2,1,0:T(8,128)(2,1)}, bf16[448,1024]{1,0:T(8,128)(2,1)}, bf16[448,1024]{1,0:T(8,128)(2,1)}, bf16[1536,1024]{1,0:T(8,128)(2,1)}) custom-call(bf16[288,512]{1,0:T(8,128)(2,1)} %pad_maximum_fusion.1.own, bf16[2,448,1024]{2,1,0:T(8,128)(2,1)} %refs_0_.1, bf16[2,448,1024]{2,1,0:T(8,128)(2,1)} %refs_1_.1, ...), custom_call_target="tpu_custom_call" | custom-call | bytes 19955712 | tf_op jit(solution)/shard_map/gather/pallas_call | solution.py:42
  69.9 1.2 slice_convert_fusion
  74.8 43.4 %self_forward.1 = (bf16[4,1024,512]{2,1,0:T(8,128)(2,1)}, bf16[448,1024]{1,0:T(8,128)(2,1)}, bf16[448,1536]{1,0:T(8,128)(2,1)}, bf16[448,512]{1,0:T(8,128)(2,1)}...) custom-call(bf16[256,512]{1,0:T(8,128)(2,1)} %maximum_select_fusion.4.own, ...), custom_call_target="tpu_custom_call" | custom-call | flops 2701131776 | bytes 14809088 | tf_op jit(solution)/shard_map/self_forward/pallas_call | solution.py:42
  118.2 0.9 maximum_select_fusion.own_weights
  119.1 92.2 %cross_and_feed.1 = (bf16[4,1024,1024]{2,1,0:T(8,128)(2,1)}, f32[448,1024]{1,0:T(8,128)}, bf16[448,1024]{1,0:T(8,128)(2,1)}, bf16[448,512]{1,0:T(8,128)(2,1)}, b...) custom-call(bf16[256,1024]{1,0:T(8,128)(2,1)} %maximum_select_fusion, ...), custom_call_target="tpu_custom_call" | custom-call | flops 18253611008 | bytes 32462848 | tf_op jit(solution)/shard_map/cross_and_feed/pallas_call | solution.py:42
  211.3 90.6 %cross_back.1 = (bf16[2,448,1024]{2,1,0:T(8,128)(2,1)}, bf16[1536,512]{1,0:T(8,128)(2,1)}, f32[448,1024]{1,0:T(8,128)}, f32[8,1024]{1,0:T(8,128)}, f32[8,512]{1,...) custom-call(bf16[448,1024]{1,0:T(8,128)(2,1)} %get-tuple-element.67., ...), custom_call_target="tpu_custom_call" | custom-call | flops 15367929856 | bytes 41197568 | tf_op jit(solution)/shard_map/cross_back/pallas_call | solution.py:42
  301.9 0.8 slice.267
  302.7 0.8 fusion.19
  303.5 68.4 %self_back.1 = (bf16[2,400,1024]{2,1,0:T(8,128)(2,1)}, bf16[448,512]{1,0:T(8,128)(2,1)}, f32[8,1024]{1,0:T(8,128)}, f32[8,1024]{1,0:T(8,128)}, f32[8,512]{1,0:T(...) custom-call(bf16[448,1024]{1,0:T(8,128)(2,1)} %get-tuple-element.79.own, ...), custom_call_target="tpu_custom_call" | custom-call | flops 5813305344 | bytes 28254208 | tf_op jit(solution)/shard_map/self_back/pallas_call | solution.py:42
  371.9 0.7 slice.269
  372.7 0.7 slice.270
  373.4 0.8 fusion.20
  374.3 0.9 fusion.18
  375.4 0.9 constant_dynamic-update-slice_fusion.2
  376.2 0.7 fusion.1.packed
  376.9 62.1 %finish.1 = (bf16[2,448,1024]{2,1,0:T(8,128)(2,1)}, f32[32,8,128]{2,1,0:T(8,128)}, f32[256,512]{1,0:T(8,128)}) custom-call(bf16[4,1024,512]{2,1,0:T(8,128)(2,1)} %get-tuple-element.90.self_grads, bf16[448,512]{1,0:T(8,128)(2,1)} %get-tuple-element.91.half_grad, f32[32,8,128]{2,1,0:T(8,128)} %fusion.1.packed), custom_call_target="tpu_custom_call" | custom-call | bytes 7274496 | tf_op jit(solution)/shard_map/finish/pallas_call | solution.py:42
  439.0 0.8 slice.291
  439.8 0.7 fusion.14
  440.5 0.8 slice.294
  441.3 0.6 constant_dynamic-slice_fusion.6
  442.0 0.6 constant_dynamic-slice_fusion.9
  442.7 1.0 constant_dynamic-slice_fusion.10
  443.7 4.8 %collective-permute-start.4 = (f32[128,512]{1,0:T(8,128)S(1)}, f32[128,512]{1,0:T(8,128)S(1)}, u32[]{:S(2)}, u32[]{:S(2)}) collective-permute-start(f32[128,512]{1,0:T(8,128)S(1)} %constant_dynamic-slice_fusion.7), channel_id=1, source_target_pairs={{0,4},{4,0},{8,12},{12,8},{16,20},{20,16},{24,28},{28,24},{1,5},{5... | collective-permute-start | bytes 786440 | tf_op jit(solution)/shard_map/ppermute | solution.py:1187
  448.5 1.9 constant_dynamic-slice_fusion.5
  452.0 0.7 fusion.16
  452.7 2.7 copy.41
  455.6 0.7 maximum_select_fusion.9
  456.3 0.8 copy.43
  457.1 0.8 copy.42
  457.9 0.7 pad_maximum_fusion.3
  458.6 0.8 pad_maximum_fusion
  459.4 1.1 fusion.8
  460.5 1.0 copy.44
  461.5 0.8 maximum_select_fusion.1
  462.3 1.2 copy.62
  463.6 0.9 copy-done.1
  464.5 1.2 copy.63
  (97 shorter events, 8.0 us)
Async XLA Ops:
  0.6 8.9 %copy-start.6 = (bf16[128,1024]{1,0:T(8,128)(2,1)S(1)}, bf16[128,1024]{1,0:T(8,128)(2,1)}, u32[]{:S(2)}) copy-start(bf16[128,1024]{1,0:T(8,128)(2,1)} %param.26) | copy-start | bytes 786436
  0.7 8.9 %copy-start.7 = (bf16[1024,128]{1,0:T(8,128)(2,1)S(1)}, bf16[1024,128]{1,0:T(8,128)(2,1)}, u32[]{:S(2)}) copy-start(bf16[1024,128]{1,0:T(8,128)(2,1)} %param.28) | copy-start | bytes 786436
  2.6 16.1 %collective-permute-start.2 = (bf16[128,512]{1,0:T(8,128)(2,1)S(1)}, bf16[128,512]{1,0:T(8,128)(2,1)S(1)}, u32[]{:S(2)}, u32[]{:S(2)}) collective-permute-start(bf16[128,512]{1,0:T(8,128)(2,1)S(1)} %pad_maximum_fusion.5), channel_id=1, source_target_pairs={{0,4},{4,0},{8,12},{12,8},{16,20},{20,16},{24,28},{28,24},{1,5},{5... | collective-permute-start | bytes 393224 | tf_op jit(solution)/shard_map/ppermute | solution.py:1187
  9.5 10.1 %collective-permute-start.1 = (bf16[144,512]{1,0:T(8,128)(2,1)S(1)}, bf16[144,512]{1,0:T(8,128)(2,1)S(1)}, u32[]{:S(2)}, u32[]{:S(2)}) collective-permute-start(bf16[144,512]{1,0:T(8,128)(2,1)S(1)} %pad_maximum_fusion.4), channel_id=1, source_target_pairs={{0,4},{4,0},{8,12},{12,8},{16,20},{20,16},{24,28},{28,24},{1,5},{5... | collective-permute-start | bytes 442376 | tf_op jit(solution)/shard_map/ppermute | solution.py:1187
  9.8 108.3 %collective-permute-start = (bf16[128,1024]{1,0:T(8,128)(2,1)S(1)}, bf16[128,1024]{1,0:T(8,128)(2,1)S(1)}, u32[]{:S(2)}, u32[]{:S(2)}) collective-permute-start(bf16[128,1024]{1,0:T(8,128)(2,1)S(1)} %pad_maximum_fusion.2), channel_id=1, source_target_pairs={{0,4},{4,0},{8,12},{12,8},{16,20},{20,16},{24,28},{28,24},{1,5},{5... | collective-permute-start | bytes 786440 | tf_op jit(solution)/shard_map/ppermute | solution.py:1187
  376.9 66.7 %copy-start.4 = (f32[256,512]{1,0:T(8,128)S(1)}, f32[256,512]{1,0:T(8,128)}, u32[]{:S(2)}) copy-start(f32[256,512]{1,0:T(8,128)} %get-tuple-element.102) | copy-start | bytes 1572868
  439.0 12.5 %copy-start.2 = (bf16[2,400,1024]{2,1,0:T(8,128)(2,1)S(1)}, bf16[2,400,1024]{2,1,0:T(8,128)(2,1)}, u32[]{:S(2)}) copy-start(bf16[2,400,1024]{2,1,0:T(8,128)(2,1)} %get-tuple-element.99) | copy-start | bytes 4915204
  443.7 11.8 %collective-permute-start.4 = (f32[128,512]{1,0:T(8,128)S(1)}, f32[128,512]{1,0:T(8,128)S(1)}, u32[]{:S(2)}, u32[]{:S(2)}) collective-permute-start(f32[128,512]{1,0:T(8,128)S(1)} %constant_dynamic-slice_fusion.7), channel_id=1, source_target_pairs={{0,4},{4,0},{8,12},{12,8},{16,20},{20,16},{24,28},{28,24},{1,5},{5... | collective-permute-start | bytes 786440 | tf_op jit(solution)/shard_map/ppermute | solution.py:1187
  448.5 7.8 %collective-permute-start.3 = (f32[128,512]{1,0:T(8,128)S(1)}, f32[128,512]{1,0:T(8,128)S(1)}, u32[]{:S(2)}, u32[]{:S(2)}) collective-permute-start(f32[128,512]{1,0:T(8,128)S(1)} %constant_dynamic-slice_fusion.10), channel_id=1, source_target_pairs={{0,4},{4,0},{8,12},{12,8},{16,20},{20,16},{24,28},{28,24},{1,5},{5... | collective-permute-start | bytes 786440 | tf_op jit(solution)/shard_map/ppermute | solution.py:1187
  448.5 3.4 copy-start.5
  450.5 8.9 %collective-permute-start.5 = (f32[128,1024]{1,0:T(8,128)}, f32[128,1024]{1,0:T(8,128)}, u32[]{:S(2)}, u32[]{:S(2)}) collective-permute-start(f32[128,1024]{1,0:T(8,128)} %constant_dynamic-slice_fusion.5), channel_id=1, source_target_pairs={{0,4},{4,0},{8,12},{12,8},{16,20},{20,16},{24,28},{28,24},{1,5},{5... | collective-permute-start | bytes 1572872 | tf_op jit(solution)/shard_map/ppermute | solution.py:1187
  452.0 3.4 copy-start.3
  460.4 1.9 copy-start
  462.3 2.2 copy-start.1

commit v6 on v5

--- a/solution.py
+++ b/solution.py
@@ -631,7 +631,7 @@
 
 
 def row_step(m):
-    return m // 4 if m % 64 == 0 else m
+    return 32 if m % 32 == 0 else m
 
 
 def over_rows(m, body):

time: 475 us -> 475 us (level)
  no operation moved by 1% of the time
where the time goes in v6:
time: 475 us; the launch traced here: 466 us
  Pallas kernels  406 us (85%)
  local copies, waits for them, and re-layouts  43.7 us (9%)
  other arithmetic  8.16 us (2%)
  starting transfers between devices  6.18 us (1%)
    pallas_call x6, Pallas kernels, call(): pl.pallas_call(kernel, name=name, out_shape=out_shape, scratch_shapes=lis...  406 us
    unnamed x33, local copies, waits for them, and re-layouts  14 us
  transfers between devices with their start and end apart: 6, of which 0 were waited for; matrix products, arithmetic and copies ran while one was open for 7% of the time, Pallas kernels for 20%

profile of v6, /device:TPU:0, one launch (start us, length us, event | category | flops | bytes accessed | tf_op | source)
XLA Modules:
  0.0 465.9 jit_solution(16202825759097681821)
XLA Ops:
  0.7 0.9 constant_dynamic-slice_fusion.17
  1.7 0.9 fusion.15
  3.2 0.7 reshape.426
  3.9 0.7 reshape.427
  4.7 2.8 concatenate.216
  7.5 0.8 constant_dynamic-slice_fusion.20
  8.4 0.9 fusion.13
  10.7 4.7 %copy.36 = bf16[2,1500,1024]{2,1,0:T(8,128)(2,1)S(1)} copy(bf16[2,1500,1024]{2,0,1:T(2,128)(2,1)} %param.17) | data formatting | bytes 12288000 | tf_op args[1]
  15.4 3.4 pad.14.refs_2_
  18.8 0.8 maximum_select_fusion.4.own
  19.6 0.7 pad_maximum_fusion.1.own
  20.4 49.5 %gather.1 = (bf16[4,1152,512]{2,1,0:T(8,128)(2,1)}, bf16[448,1024]{1,0:T(8,128)(2,1)}, bf16[448,1024]{1,0:T(8,128)(2,1)}, bf16[1536,1024]{1,0:T(8,128)(2,1)}) custom-call(bf16[288,512]{1,0:T(8,128)(2,1)} %pad_maximum_fusion.1.own, bf16[2,448,1024]{2,1,0:T(8,128)(2,1)} %refs_0_.1, bf16[2,448,1024]{2,1,0:T(8,128)(2,1)} %refs_1_.1, ...), custom_call_target="tpu_custom_call" | custom-call | bytes 19955712 | tf_op jit(solution)/shard_map/gather/pallas_call | solution.py:42
  69.9 1.2 slice_convert_fusion
  74.8 43.4 %self_forward.1 = (bf16[4,1024,512]{2,1,0:T(8,128)(2,1)}, bf16[448,1024]{1,0:T(8,128)(2,1)}, bf16[448,1536]{1,0:T(8,128)(2,1)}, bf16[448,512]{1,0:T(8,128)(2,1)}...) custom-call(bf16[256,512]{1,0:T(8,128)(2,1)} %maximum_select_fusion.4.own, ...), custom_call_target="tpu_custom_call" | custom-call | flops 2701131776 | bytes 14809088 | tf_op jit(solution)/shard_map/self_forward/pallas_call | solution.py:42
  118.2 0.9 maximum_select_fusion.own_weights
  119.1 92.2 %cross_and_feed.1 = (bf16[4,1024,1024]{2,1,0:T(8,128)(2,1)}, f32[448,1024]{1,0:T(8,128)}, bf16[448,1024]{1,0:T(8,128)(2,1)}, bf16[448,512]{1,0:T(8,128)(2,1)}, b...) custom-call(bf16[256,1024]{1,0:T(8,128)(2,1)} %maximum_select_fusion, ...), custom_call_target="tpu_custom_call" | custom-call | flops 18253611008 | bytes 32462848 | tf_op jit(solution)/shard_map/cross_and_feed/pallas_call | solution.py:42
  211.3 90.6 %cross_back.1 = (bf16[2,448,1024]{2,1,0:T(8,128)(2,1)}, bf16[1536,512]{1,0:T(8,128)(2,1)}, f32[448,1024]{1,0:T(8,128)}, f32[8,1024]{1,0:T(8,128)}, f32[8,512]{1,...) custom-call(bf16[448,1024]{1,0:T(8,128)(2,1)} %get-tuple-element.67., ...), custom_call_target="tpu_custom_call" | custom-call | flops 15367929856 | bytes 41197568 | tf_op jit(solution)/shard_map/cross_back/pallas_call | solution.py:42
  301.9 0.8 slice.267
  302.7 0.8 fusion.19
  303.5 68.0 %self_back.1 = (bf16[2,400,1024]{2,1,0:T(8,128)(2,1)}, bf16[448,512]{1,0:T(8,128)(2,1)}, f32[8,1024]{1,0:T(8,128)}, f32[8,1024]{1,0:T(8,128)}, f32[8,512]{1,0:T(...) custom-call(bf16[448,1024]{1,0:T(8,128)(2,1)} %get-tuple-element.79.own, ...), custom_call_target="tpu_custom_call" | custom-call | flops 5813305344 | bytes 28254208 | tf_op jit(solution)/shard_map/self_back/pallas_call | solution.py:42
  371.5 0.7 slice.269
  372.3 0.7 slice.270
  373.0 0.8 fusion.20
  373.9 0.9 fusion.18
  375.0 0.9 constant_dynamic-update-slice_fusion.2
  375.8 0.7 fusion.1.packed
  376.5 62.4 %finish.1 = (bf16[2,448,1024]{2,1,0:T(8,128)(2,1)}, f32[32,8,128]{2,1,0:T(8,128)}, f32[256,512]{1,0:T(8,128)}) custom-call(bf16[4,1024,512]{2,1,0:T(8,128)(2,1)} %get-tuple-element.90.self_grads, bf16[448,512]{1,0:T(8,128)(2,1)} %get-tuple-element.91.half_grad, f32[32,8,128]{2,1,0:T(8,128)} %fusion.1.packed), custom_call_target="tpu_custom_call" | custom-call | bytes 7274496 | tf_op jit(solution)/shard_map/finish/pallas_call | solution.py:42
  439.0 0.8 slice.291
  439.8 0.7 fusion.14
  440.5 0.8 slice.294
  441.3 0.6 constant_dynamic-slice_fusion.6
  442.0 0.6 constant_dynamic-slice_fusion.9
  442.6 1.0 constant_dynamic-slice_fusion.10
  443.7 4.5 collective-permute-start.4
  448.2 1.9 constant_dynamic-slice_fusion.5
  451.7 0.7 fusion.16
  452.4 2.7 copy.41
  455.3 0.7 maximum_select_fusion.9
  456.0 0.8 copy.43
  456.8 0.8 copy.42
  457.6 0.7 pad_maximum_fusion.3
  458.3 0.8 pad_maximum_fusion
  459.1 1.1 fusion.8
  460.2 1.0 copy.44
  461.2 0.8 maximum_select_fusion.1
  462.0 1.2 copy.62
  463.3 0.9 copy-done.1
  464.2 1.2 copy.63
  (97 shorter events, 8.0 us)
Async XLA Ops:
  0.6 8.9 %copy-start.6 = (bf16[128,1024]{1,0:T(8,128)(2,1)S(1)}, bf16[128,1024]{1,0:T(8,128)(2,1)}, u32[]{:S(2)}) copy-start(bf16[128,1024]{1,0:T(8,128)(2,1)} %param.26) | copy-start | bytes 786436
  0.7 8.9 %copy-start.7 = (bf16[1024,128]{1,0:T(8,128)(2,1)S(1)}, bf16[1024,128]{1,0:T(8,128)(2,1)}, u32[]{:S(2)}) copy-start(bf16[1024,128]{1,0:T(8,128)(2,1)} %param.28) | copy-start | bytes 786436
  2.6 16.1 %collective-permute-start.2 = (bf16[128,512]{1,0:T(8,128)(2,1)S(1)}, bf16[128,512]{1,0:T(8,128)(2,1)S(1)}, u32[]{:S(2)}, u32[]{:S(2)}) collective-permute-start(bf16[128,512]{1,0:T(8,128)(2,1)S(1)} %pad_maximum_fusion.5), channel_id=1, source_target_pairs={{0,4},{4,0},{8,12},{12,8},{16,20},{20,16},{24,28},{28,24},{1,5},{5... | collective-permute-start | bytes 393224 | tf_op jit(solution)/shard_map/ppermute | solution.py:1187
  9.5 10.1 %collective-permute-start.1 = (bf16[144,512]{1,0:T(8,128)(2,1)S(1)}, bf16[144,512]{1,0:T(8,128)(2,1)S(1)}, u32[]{:S(2)}, u32[]{:S(2)}) collective-permute-start(bf16[144,512]{1,0:T(8,128)(2,1)S(1)} %pad_maximum_fusion.4), channel_id=1, source_target_pairs={{0,4},{4,0},{8,12},{12,8},{16,20},{20,16},{24,28},{28,24},{1,5},{5... | collective-permute-start | bytes 442376 | tf_op jit(solution)/shard_map/ppermute | solution.py:1187
  9.8 108.3 %collective-permute-start = (bf16[128,1024]{1,0:T(8,128)(2,1)S(1)}, bf16[128,1024]{1,0:T(8,128)(2,1)S(1)}, u32[]{:S(2)}, u32[]{:S(2)}) collective-permute-start(bf16[128,1024]{1,0:T(8,128)(2,1)S(1)} %pad_maximum_fusion.2), channel_id=1, source_target_pairs={{0,4},{4,0},{8,12},{12,8},{16,20},{20,16},{24,28},{28,24},{1,5},{5... | collective-permute-start | bytes 786440 | tf_op jit(solution)/shard_map/ppermute | solution.py:1187
  376.5 67.1 %copy-start.4 = (f32[256,512]{1,0:T(8,128)S(1)}, f32[256,512]{1,0:T(8,128)}, u32[]{:S(2)}) copy-start(f32[256,512]{1,0:T(8,128)} %get-tuple-element.102) | copy-start | bytes 1572868
  439.0 12.3 %copy-start.2 = (bf16[2,400,1024]{2,1,0:T(8,128)(2,1)S(1)}, bf16[2,400,1024]{2,1,0:T(8,128)(2,1)}, u32[]{:S(2)}) copy-start(bf16[2,400,1024]{2,1,0:T(8,128)(2,1)} %get-tuple-element.99) | copy-start | bytes 4915204
  443.7 11.5 %collective-permute-start.4 = (f32[128,512]{1,0:T(8,128)S(1)}, f32[128,512]{1,0:T(8,128)S(1)}, u32[]{:S(2)}, u32[]{:S(2)}) collective-permute-start(f32[128,512]{1,0:T(8,128)S(1)} %constant_dynamic-slice_fusion.7), channel_id=1, source_target_pairs={{0,4},{4,0},{8,12},{12,8},{16,20},{20,16},{24,28},{28,24},{1,5},{5... | collective-permute-start | bytes 786440 | tf_op jit(solution)/shard_map/ppermute | solution.py:1187
  448.2 7.8 %collective-permute-start.3 = (f32[128,512]{1,0:T(8,128)S(1)}, f32[128,512]{1,0:T(8,128)S(1)}, u32[]{:S(2)}, u32[]{:S(2)}) collective-permute-start(f32[128,512]{1,0:T(8,128)S(1)} %constant_dynamic-slice_fusion.10), channel_id=1, source_target_pairs={{0,4},{4,0},{8,12},{12,8},{16,20},{20,16},{24,28},{28,24},{1,5},{5... | collective-permute-start | bytes 786440 | tf_op jit(solution)/shard_map/ppermute | solution.py:1187
  448.2 3.4 copy-start.5
  450.2 8.9 %collective-permute-start.5 = (f32[128,1024]{1,0:T(8,128)}, f32[128,1024]{1,0:T(8,128)}, u32[]{:S(2)}, u32[]{:S(2)}) collective-permute-start(f32[128,1024]{1,0:T(8,128)} %constant_dynamic-slice_fusion.5), channel_id=1, source_target_pairs={{0,4},{4,0},{8,12},{12,8},{16,20},{20,16},{24,28},{28,24},{1,5},{5... | collective-permute-start | bytes 1572872 | tf_op jit(solution)/shard_map/ppermute | solution.py:1187
  451.7 3.4 copy-start.3
  460.1 1.9 copy-start
  462.0 2.2 copy-start.1
